TPU v7x, 32 devices: a whole 2x2x4 slice. The times are simulated.
32 devices in a mesh: dp: 4 (over z), fsdp: 8 (over y, x, core).
Axes of the slice: x: 2, y: 2, z: 4, core: 2. Of those that a mesh axis runs over, the one named last changes fastest.
Arguments:
- frames: bfloat16 [256, 256, 512], P(('dp', 'fsdp')), may hold values from -6 to 6
- group: int32 [256], P(('dp', 'fsdp')), may hold values from 0 to 1
- lengths: int32 [256], P(('dp', 'fsdp')), may hold values from 128 to 256, as said below
- conv_weight: bfloat16 [2, 7, 512], P(None, None, ('dp', 'fsdp')), may hold values from -2 to 2
- conv_bias: bfloat16 [2, 512], P(None, ('dp', 'fsdp')), may hold values from -3 to 3
- ada_scale: bfloat16 [2, 2, 512], P(None, None, ('dp', 'fsdp')), may hold values from 0.5 to 1.5
- ada_shift: bfloat16 [2, 2, 512], P(None, None, ('dp', 'fsdp')), may hold values from -3 to 3
- up_weight: bfloat16 [2, 512, 1536], P(None, ('dp', 'fsdp')), may hold values from -0.25 to 0.25
- up_bias: bfloat16 [2, 1536], P(None, ('dp', 'fsdp')), may hold values from -3 to 3
- down_weight: bfloat16 [2, 1536, 512], P(None, ('dp', 'fsdp')), may hold values from -0.15625 to 0.15625
- down_bias: bfloat16 [2, 512], P(None, ('dp', 'fsdp')), may hold values from -3 to 3
- layer_scale: bfloat16 [2, 512], P(None, ('dp', 'fsdp')), may hold values from 0.5 to 1.5
- out_grad: bfloat16 [256, 256, 512], P(('dp', 'fsdp')), may hold values from -6 to 6
Outputs:
- output: bfloat16 [256, 256, 512], P(('dp', 'fsdp'))
- input_grad: float32 [256, 256, 512], P(('dp', 'fsdp'))
- conv_weight_grad: float32 [2, 7, 512], P(None, None, ('dp', 'fsdp'))
- conv_bias_grad: float32 [2, 512], P(None, ('dp', 'fsdp'))
- ada_scale_grad: float32 [2, 2, 512], P(None, None, ('dp', 'fsdp'))
- ada_shift_grad: float32 [2, 2, 512], P(None, None, ('dp', 'fsdp'))
- up_weight_grad: float32 [2, 512, 1536], P(None, ('dp', 'fsdp'))
- up_bias_grad: float32 [2, 1536], P(None, ('dp', 'fsdp'))
- down_weight_grad: float32 [2, 1536, 512], P(None, ('dp', 'fsdp'))
- down_bias_grad: float32 [2, 512], P(None, ('dp', 'fsdp'))
- layer_scale_grad: float32 [2, 512], P(None, ('dp', 'fsdp'))
Inputs may be any that keep to these rules, and one draw needn't show every extreme that they name: `lengths`: A clip of group 0 has at most 256 valid frames, one of group 1 at most 236; clip 0 has 256 and clip 1 has 236.
All inputs are finite; a program needn't handle non-finite values.
Results may differ from a plain program's by a relative error of at most 0.0066.
Values may be sent and summed in bfloat16 or wider, within the bound.
A program may use at most 192 MiB of HBM per device.

v0:
```python
from functools import partial

import jax
import jax.numpy as jnp
from jax import lax
from jax.sharding import PartitionSpec as P

EPSILON = 1e-06


def forward_block(fetched, stream, valid_rows, select):
    kernel_taps = fetched[0].astype(jnp.float32)
    conv_shift = fetched[1].astype(jnp.float32)
    scale_table = fetched[2].astype(jnp.float32)
    shift_table = fetched[3].astype(jnp.float32)
    up_matrix = fetched[4]
    up_offset = fetched[5].astype(jnp.float32)
    down_matrix = fetched[6]
    down_offset = fetched[7].astype(jnp.float32)
    layer_gain = fetched[8].astype(jnp.float32)
    clip_count, frame_count, model_width = stream.shape
    half_kernel = kernel_taps.shape[0] // 2
    masked = stream * valid_rows
    padded = jnp.pad(masked, ((0, 0), (half_kernel, half_kernel), (0, 0)))
    mixed = conv_shift
    for offset in range(kernel_taps.shape[0]):
        mixed = mixed + kernel_taps[offset] * padded[:, offset : offset + frame_count, :]
    center = mixed - jnp.mean(mixed, axis=-1, keepdims=True)
    spread = jnp.mean(center * center, axis=-1, keepdims=True)
    inv_std = lax.rsqrt(spread + EPSILON)
    normed = center * inv_std
    gain_rows = jnp.einsum("cg,gd->cd", select, scale_table, precision=lax.Precision.HIGHEST)
    shift_rows = jnp.einsum("cg,gd->cd", select, shift_table, precision=lax.Precision.HIGHEST)
    shaped = normed * gain_rows[:, None, :] + shift_rows[:, None, :]
    shaped_low = shaped.astype(jnp.bfloat16).reshape(clip_count * frame_count, model_width)
    before = jnp.dot(shaped_low, up_matrix, preferred_element_type=jnp.float32) + up_offset
    activated_low = jax.nn.gelu(before, approximate=False).astype(jnp.bfloat16)
    branch = jnp.dot(activated_low, down_matrix, preferred_element_type=jnp.float32) + down_offset
    branch = branch.reshape(clip_count, frame_count, model_width)
    output = stream + valid_rows * layer_gain * branch
    return (output, (padded, normed, inv_std, gain_rows, shaped_low, before, activated_low, branch))


def backward_block(fetched, saved_state, grad_stream, valid_rows, select):
    kernel_taps = fetched[0].astype(jnp.float32)
    up_matrix = fetched[4]
    down_matrix = fetched[6]
    layer_gain = fetched[8].astype(jnp.float32)
    padded, normed, inv_std, gain_rows, shaped_low, before, activated_low, branch = saved_state
    clip_count, frame_count, model_width = grad_stream.shape
    kernel_len = kernel_taps.shape[0]
    half_kernel = kernel_len // 2
    gain_term = jnp.sum(valid_rows * branch * grad_stream, axis=(0, 1))
    grad_branch = (valid_rows * layer_gain * grad_stream).astype(jnp.bfloat16)
    down_offset_term = jnp.sum(grad_branch.astype(jnp.float32), axis=(0, 1))
    branch_rows = grad_branch.reshape(clip_count * frame_count, model_width)
    down_term = jnp.einsum(
        "rh,rd->hd", activated_low, branch_rows, preferred_element_type=jnp.float32
    )
    grad_activated = jnp.einsum(
        "rd,hd->rh", branch_rows, down_matrix, preferred_element_type=jnp.float32
    )
    unused_value, gelu_pull = jax.vjp(partial(jax.nn.gelu, approximate=False), before)
    grad_before = gelu_pull(grad_activated)[0].astype(jnp.bfloat16)
    up_offset_term = jnp.sum(grad_before.astype(jnp.float32), axis=0)
    up_term = jnp.einsum("rd,rh->dh", shaped_low, grad_before, preferred_element_type=jnp.float32)
    grad_shaped = jnp.einsum(
        "rh,dh->rd", grad_before, up_matrix, preferred_element_type=jnp.float32
    )
    grad_shaped = grad_shaped.reshape(clip_count, frame_count, model_width)
    clip_scale = jnp.sum(grad_shaped * normed, axis=1)
    clip_shift = jnp.sum(grad_shaped, axis=1)
    scale_term = jnp.einsum("cg,cd->gd", select, clip_scale, precision=lax.Precision.HIGHEST)
    shift_term = jnp.einsum("cg,cd->gd", select, clip_shift, precision=lax.Precision.HIGHEST)
    grad_normed = grad_shaped * gain_rows[:, None, :]
    grad_mixed = inv_std * (
        grad_normed
        - jnp.mean(grad_normed, axis=-1, keepdims=True)
        - normed * jnp.mean(grad_normed * normed, axis=-1, keepdims=True)
    )
    conv_shift_term = jnp.sum(grad_mixed, axis=(0, 1))
    kernel_term = jnp.stack(
        [
            jnp.sum(grad_mixed * padded[:, offset : offset + frame_count, :], axis=(0, 1))
            for offset in range(kernel_len)
        ]
    )
    grad_padded = jnp.pad(grad_mixed, ((0, 0), (half_kernel, half_kernel), (0, 0)))
    grad_masked = jnp.zeros_like(grad_mixed)
    for offset in range(kernel_len):
        start_row = 2 * half_kernel - offset
        grad_masked = (
            grad_masked
            + kernel_taps[offset] * grad_padded[:, start_row : start_row + frame_count, :]
        )
    grad_input = grad_stream + valid_rows * grad_masked
    terms = (
        kernel_term,
        conv_shift_term,
        scale_term,
        shift_term,
        up_term,
        up_offset_term,
        down_term,
        down_offset_term,
        gain_term,
    )
    return (grad_input, terms)


def body(
    frames,
    group,
    lengths,
    conv_weight,
    conv_bias,
    ada_scale,
    ada_shift,
    up_weight,
    up_bias,
    down_weight,
    down_bias,
    layer_scale,
    out_grad,
):
    stream = frames.astype(jnp.float32)
    frame_count = stream.shape[1]
    block_count = conv_weight.shape[0]
    valid_rows = (jnp.arange(frame_count, dtype=jnp.int32)[None, :] < lengths[:, None]).astype(
        jnp.float32
    )[:, :, None]
    select = (group[:, None] == jnp.arange(ada_scale.shape[1], dtype=jnp.int32)[None, :]).astype(
        jnp.float32
    )
    saved_states = []
    for block_index in range(block_count):
        fetched = (
            lax.all_gather(conv_weight[block_index], ("dp", "fsdp"), axis=1, tiled=True),
            lax.all_gather(conv_bias[block_index], ("dp", "fsdp"), axis=0, tiled=True),
            lax.all_gather(ada_scale[block_index], ("dp", "fsdp"), axis=1, tiled=True),
            lax.all_gather(ada_shift[block_index], ("dp", "fsdp"), axis=1, tiled=True),
            lax.all_gather(up_weight[block_index], ("dp", "fsdp"), axis=0, tiled=True),
            lax.all_gather(up_bias[block_index], ("dp", "fsdp"), axis=0, tiled=True),
            lax.all_gather(down_weight[block_index], ("dp", "fsdp"), axis=0, tiled=True),
            lax.all_gather(down_bias[block_index], ("dp", "fsdp"), axis=0, tiled=True),
            lax.all_gather(layer_scale[block_index], ("dp", "fsdp"), axis=0, tiled=True),
        )
        stream, block_state = forward_block(fetched, stream, valid_rows, select)
        saved_states.append(block_state)
    output = stream.astype(jnp.bfloat16)
    grad_stream = out_grad.astype(jnp.float32)
    shard_lists = [None] * block_count
    for block_index in reversed(range(block_count)):
        fetched = (
            lax.all_gather(conv_weight[block_index], ("dp", "fsdp"), axis=1, tiled=True),
            lax.all_gather(conv_bias[block_index], ("dp", "fsdp"), axis=0, tiled=True),
            lax.all_gather(ada_scale[block_index], ("dp", "fsdp"), axis=1, tiled=True),
            lax.all_gather(ada_shift[block_index], ("dp", "fsdp"), axis=1, tiled=True),
            lax.all_gather(up_weight[block_index], ("dp", "fsdp"), axis=0, tiled=True),
            lax.all_gather(up_bias[block_index], ("dp", "fsdp"), axis=0, tiled=True),
            lax.all_gather(down_weight[block_index], ("dp", "fsdp"), axis=0, tiled=True),
            lax.all_gather(down_bias[block_index], ("dp", "fsdp"), axis=0, tiled=True),
            lax.all_gather(layer_scale[block_index], ("dp", "fsdp"), axis=0, tiled=True),
        )
        grad_stream, terms = backward_block(
            fetched, saved_states[block_index], grad_stream, valid_rows, select
        )
        shards = (
            lax.psum_scatter(terms[0], ("dp", "fsdp"), scatter_dimension=1, tiled=True),
            lax.psum_scatter(terms[1], ("dp", "fsdp"), scatter_dimension=0, tiled=True),
            lax.psum_scatter(terms[2], ("dp", "fsdp"), scatter_dimension=1, tiled=True),
            lax.psum_scatter(terms[3], ("dp", "fsdp"), scatter_dimension=1, tiled=True),
            lax.psum_scatter(terms[4], ("dp", "fsdp"), scatter_dimension=0, tiled=True),
            lax.psum_scatter(terms[5], ("dp", "fsdp"), scatter_dimension=0, tiled=True),
            lax.psum_scatter(terms[6], ("dp", "fsdp"), scatter_dimension=0, tiled=True),
            lax.psum_scatter(terms[7], ("dp", "fsdp"), scatter_dimension=0, tiled=True),
            lax.psum_scatter(terms[8], ("dp", "fsdp"), scatter_dimension=0, tiled=True),
        )
        shard_lists[block_index] = shards
    stacked = tuple(
        (
            jnp.stack([shard_lists[block_index][entry] for block_index in range(block_count)])
            for entry in range(9)
        )
    )
    return (
        output,
        grad_stream,
        stacked[0],
        stacked[1],
        stacked[2],
        stacked[3],
        stacked[4],
        stacked[5],
        stacked[6],
        stacked[7],
        stacked[8],
    )


def solution(mesh):
    in_specs = (
        P(("dp", "fsdp"), None, None),
        P(("dp", "fsdp")),
        P(("dp", "fsdp")),
        P(None, None, ("dp", "fsdp")),
        P(None, ("dp", "fsdp")),
        P(None, None, ("dp", "fsdp")),
        P(None, None, ("dp", "fsdp")),
        P(None, ("dp", "fsdp"), None),
        P(None, ("dp", "fsdp")),
        P(None, ("dp", "fsdp"), None),
        P(None, ("dp", "fsdp")),
        P(None, ("dp", "fsdp")),
        P(("dp", "fsdp"), None, None),
    )
    out_specs = (
        P(("dp", "fsdp"), None, None),
        P(("dp", "fsdp"), None, None),
        P(None, None, ("dp", "fsdp")),
        P(None, ("dp", "fsdp")),
        P(None, None, ("dp", "fsdp")),
        P(None, None, ("dp", "fsdp")),
        P(None, ("dp", "fsdp"), None),
        P(None, ("dp", "fsdp")),
        P(None, ("dp", "fsdp"), None),
        P(None, ("dp", "fsdp")),
        P(None, ("dp", "fsdp")),
    )
    return jax.shard_map(body, mesh=mesh, in_specs=in_specs, out_specs=out_specs, check_vma=False)
```

profile of v0, /device:TPU:0, one launch (start us, length us, event | category | flops | bytes accessed | tf_op | source)
XLA Modules:
  0.0 1740.9 jit_solution(17593879401863547179)
XLA Ops:
  16.5 42.2 %all-reduce.21 = (bf16[512]{0:T(512)(128)(2,1)S(1)}, bf16[1536]{0:T(1024)(128)(2,1)S(1)}, bf16[512]{0:T(512)(128)(2,1)S(1)}, bf16[512]{0:T(512)(128)(2,1)S(1)}, ...) all-reduce(bf16[512]{0:T(512)(128)(2,1)S(1)} %dynamic-update-slice., ...), channel_id=3, replica_groups=mesh['dp'=4,'fsdp'=8] {'dp','fsdp'}, use_global_device_ids=true, to_apply=%add.5 | all-reduce | flops 6144 | bytes 24576
  59.6 41.4 %all-gather.2 = bf16[1,7,512]{1,0,2:T(2,128)(2,1)S(1)} all-gather(bf16[1,7,16]{1,0,2:T(2,128)(2,1)S(1)} %copy.55), channel_id=4, replica_groups=mesh['dp'=4,'fsdp'=8] {'dp','fsdp'}, dimensions={2}, use_global_device_ids=true | all-gather | bytes 7392 | tf_op jit(solution)/shard_map/all_gather | solution.py:138
  101.2 14.1 slice_reduce_fusion.13
  123.8 37.3 %all-gather.3 = bf16[1,2,512]{1,0,2:T(2,128)(2,1)S(1)} all-gather(bf16[1,2,16]{1,0,2:T(2,128)(2,1)S(1)} %copy.56), channel_id=5, replica_groups=mesh['dp'=4,'fsdp'=8] {'dp','fsdp'}, dimensions={2}, use_global_device_ids=true | all-gather | bytes 2112 | tf_op jit(solution)/shard_map/all_gather | solution.py:140
  161.4 38.8 %all-gather.4 = bf16[1,2,512]{1,0,2:T(2,128)(2,1)S(1)} all-gather(bf16[1,2,16]{1,0,2:T(2,128)(2,1)S(1)} %copy.57), channel_id=6, replica_groups=mesh['dp'=4,'fsdp'=8] {'dp','fsdp'}, dimensions={2}, use_global_device_ids=true | all-gather | bytes 2112 | tf_op jit(solution)/shard_map/all_gather | solution.py:141
  200.9 37.7 %all-gather.11 = bf16[1,7,512]{1,0,2:T(2,128)(2,1)S(1)} all-gather(bf16[1,7,16]{1,0,2:T(2,128)(2,1)S(1)} %copy.58), channel_id=13, replica_groups=mesh['dp'=4,'fsdp'=8] {'dp','fsdp'}, dimensions={2}, use_global_device_ids=true | all-gather | bytes 7392 | tf_op jit(solution)/shard_map/all_gather | solution.py:138
  238.8 14.1 slice_reduce_fusion.6
  253.0 38.5 %all-gather.12 = bf16[1,2,512]{1,0,2:T(2,128)(2,1)S(1)} all-gather(bf16[1,2,16]{1,0,2:T(2,128)(2,1)S(1)} %copy.59), channel_id=14, replica_groups=mesh['dp'=4,'fsdp'=8] {'dp','fsdp'}, dimensions={2}, use_global_device_ids=true | all-gather | bytes 2112 | tf_op jit(solution)/shard_map/all_gather | solution.py:140
  292.0 37.6 %all-gather.13 = bf16[1,2,512]{1,0,2:T(2,128)(2,1)S(1)} all-gather(bf16[1,2,16]{1,0,2:T(2,128)(2,1)S(1)} %copy.60), channel_id=15, replica_groups=mesh['dp'=4,'fsdp'=8] {'dp','fsdp'}, dimensions={2}, use_global_device_ids=true | all-gather | bytes 2112 | tf_op jit(solution)/shard_map/all_gather | solution.py:141
  334.2 33.1 %multiply_convert_fusion.1 = (bf16[2048,1536]{1,0:T(8,128)(2,1)}, f32[2048,1536]{1,0:T(8,128)}, f32[2048,1536]{1,0:T(8,128)}) fusion(f32[1536]{0:T(1024)S(1)} %convert_element_type.134, bf16[2048,512]{1,0:T(8,128)(2,1)} %bitcast.165, bf16[1,512,1536]{2,1,0:T(8,128)(2,1)} %all-gather.23.cloned.1.call-done), kind=kOutput, calls=%fused_computation.21 | convolution fusion | flops 3428843520 | bytes 35133440 | tf_op jit(solution)/shard_map/dot_general | solution.py:36
  383.3 34.2 %multiply_convert_fusion = (bf16[2048,1536]{1,0:T(8,128)(2,1)}, f32[2048,1536]{1,0:T(8,128)}, f32[2048,1536]{1,0:T(8,128)}) fusion(f32[1536]{0:T(1024)S(1)} %convert_element_type.138, bf16[2048,512]{1,0:T(8,128)(2,1)S(1)} %bitcast.167, bf16[1,512,1536]{2,1,0:T(8,128)(2,1)} %all-gather.27.cloned.1.call-done), kind=kOutput, calls=%fused_computation.8 | convolution fusion | flops 3428843520 | bytes 35133440 | tf_op jit(solution)/shard_map/dot_general | solution.py:36
  417.5 14.7 convert_reduce_fusion
  438.3 20.4 %multiply_reduce_fusion.3 = (f32[512]{0:T(512)S(1)}, f32[512]{0:T(512)S(1)}, f32[512]{0:T(512)S(1)}, f32[512]{0:T(512)S(1)}, f32[512]{0:T(512)S(1)}, /*index=5*/...) fusion(f32[8,256,512]{2,1,0:T(8,128)} %copy-done.9, ...), kind=kLoop, calls=%fused_computation.60 | loop fusion | flops 23064576 | bytes 16842752 | tf_op jit(solution)/shard_map/reduce_sum | solution.py:84
  458.8 8.0 convolution_add_fusion
  466.8 20.3 %convert_reduce_fusion.3 = (f32[512]{0:T(512)S(1)}, bf16[8,256,512]{2,1,0:T(8,128)(2,1)}, f32[8,256,512]{2,1,0:T(8,128)}, bf16[8,256,512]{2,1,0:T(8,128)(2,1)}) fusion(f32[512]{0:T(512)S(1)} %convert_element_type.132, f32[8,256]{1,0:T(8,128)S(1)} %fusion.38, f32[512]{0:T(512)S(1)} %get-tuple-element.72, f32[512]{0:T(512)S(1)} %get-tuple-element.67, ...), kind=kLoop, calls=%fused_computation.57 | loop fusion | flops 29359616 | bytes 25194496 | tf_op jit(solution)/shard_map/reduce_sum | solution.py:55
  487.1 14.9 convert_reduce_fusion.1
  514.3 23.7 %multiply_reduce_fusion.10 = (f32[512]{0:T(512)S(1)}, f32[512]{0:T(512)S(1)}, f32[512]{0:T(512)S(1)}, f32[512]{0:T(512)S(1)}, f32[512]{0:T(512)S(1)}, /*index=5*...) fusion(f32[8,256,512]{2,1,0:T(8,128)} %copy-done.6, ...), kind=kLoop, calls=%fused_computation.67 | loop fusion | flops 32500736 | bytes 33632256 | tf_op jit(solution)/shard_map/reduce_sum | solution.py:84
  540.0 8.7 fusion.68
  556.9 8.7 fusion.67
  565.7 7.9 fusion.66
  573.7 37.3 %all-reduce.20 = (f32[512]{0:T(512)S(1)}, f32[512]{0:T(512)S(1)}, f32[1536]{0:T(1024)S(1)}, f32[1536]{0:T(1024)S(1)}, f32[512]{0:T(512)S(1)}, /*index=5*/f32[512]{0:T(512)S(1)}, f32[512]{0:T(512)S(1)}, f32[512]{0:T(512)S(1)}) all-reduce(f32[512]{0:T(512)S(1)} %get-tuple-element.64, ...), channel_id=23, replica_groups=mesh['dp'=4,'fsdp'=8] {'dp','fsdp'}, use_global_device_ids=true, to_apply=%region_27.28.clone | all-reduce | flops 6144 | bytes 49152
  613.7 18.2 %multiply_add_fusion = f32[8,256,512]{2,1,0:T(8,128)} fusion(f32[8,256,512]{2,1,0:T(8,128)} %get-tuple-element.100, f32[8,256,512]{2,1,0:T(8,128)} %get-tuple-element.103, f32[512]{0:T(512)S(1)} %copy-done.39, f32[512]{0:T(512)S(1)} %copy-done.29, f32[512]{0:T(512)S(1)} %copy-done.31, f32[512]{0:T(512)S(1)} %copy-done.33, f32[512]{0:T(512)S(1)} %copy-done.35, ...), kind=kLoop, calls=%fused_computation.74 | loop fusion | flops 15728640 | bytes 12605440 | tf_op jit(solution)/shard_map/add | solution.py:96
  631.8 10.5 reduce-scatter.35.cloned.1.call-done
  643.1 132.8 %reduce-scatter.39.cloned.1.call-done = f32[16,2]{1,0:T(8,128)} async-done(((f32[512,2]{1,0:T(8,128)}), f32[16,2]{1,0:T(8,128)}) %reduce-scatter.39.cloned.1.call-update) | async-done | bytes 144
  776.7 133.0 %reduce-scatter.37.cloned.1.call-done = f32[16,2]{1,0:T(8,128)} async-done(((f32[512,2]{1,0:T(8,128)}), f32[16,2]{1,0:T(8,128)}) %reduce-scatter.37.cloned.1.call-update) | async-done | bytes 144
  910.4 132.6 %reduce-scatter.41.cloned.1.call-done = f32[16,2]{1,0:T(8,128)} async-done(((f32[512,2]{1,0:T(8,128)}), f32[16,2]{1,0:T(8,128)}) %reduce-scatter.41.cloned.1.call-update) | async-done | bytes 144
  1044.4 132.0 %reduce-scatter.31.cloned.1.call-done = f32[16,7]{1,0:T(8,128)} async-done(((f32[512,7]{1,0:T(8,128)}), f32[16,7]{1,0:T(8,128)}) %reduce-scatter.31.cloned.1.call-update) | async-done | bytes 464
  1177.1 132.4 %reduce-scatter.33.cloned.1.call-done = f32[16,7]{1,0:T(8,128)} async-done(((f32[512,7]{1,0:T(8,128)}), f32[16,7]{1,0:T(8,128)}) %reduce-scatter.33.cloned.1.call-update) | async-done | bytes 464
  1310.9 102.1 %reduce-scatter.27.cloned.1.call-done = f32[48,512]{1,0:T(8,128)} async-done(((f32[1536,512]{1,0:T(8,128)}), f32[48,512]{1,0:T(8,128)}) %reduce-scatter.27.cloned.1.call-update) | async-done | bytes 98320 | tf_op jit(solution)/shard_map/reduce_scatter | solution.py:175
  1413.0 106.4 %reduce-scatter.29.cloned.1.call-done = f32[48,512]{1,0:T(8,128)} async-done(((f32[1536,512]{1,0:T(8,128)}), f32[48,512]{1,0:T(8,128)}) %reduce-scatter.29.cloned.1.call-update) | async-done | bytes 98320 | tf_op jit(solution)/shard_map/reduce_scatter | solution.py:175
  1521.0 105.0 %reduce-scatter.25.cloned.1.call-done = f32[16,1536]{1,0:T(8,128)} async-done(((f32[512,1536]{1,0:T(8,128)}), f32[16,1536]{1,0:T(8,128)}) %reduce-scatter.25.cloned.1.call-update) | async-done | bytes 98320 | tf_op jit(solution)/shard_map/reduce_scatter | solution.py:173
  1626.0 106.5 %reduce-scatter.23.cloned.1.call-done = f32[16,1536]{1,0:T(8,128)} async-done(((f32[512,1536]{1,0:T(8,128)}), f32[16,1536]{1,0:T(8,128)}) %reduce-scatter.23.cloned.1.call-update) | async-done | bytes 98320 | tf_op jit(solution)/shard_map/reduce_scatter | solution.py:173
  (227 shorter events, 80.8 us)
Async XLA Ops:
  7.2 109.0 %copy-start.10 = (bf16[8,256,512]{2,1,0:T(8,128)(2,1)S(1)}, bf16[8,256,512]{2,1,0:T(8,128)(2,1)}, u32[]{:S(2)}) copy-start(bf16[8,256,512]{2,1,0:T(8,128)(2,1)} %param.13) | copy-start | bytes 6291460
  7.2 327.0 %all-gather.23.cloned.1.call-start = ((), (), s32[]{:S(2)}) async-start(), calls=%async_computation.14 | async-start | bytes 1622016 | tf_op jit(solution)/shard_map/all_gather | solution.py:142
  8.9 358.5 %all-gather.25.cloned.1.call-start = ((), (), s32[]{:S(2)}) async-start(), calls=%async_computation.15 | async-start | bytes 1622016 | tf_op jit(solution)/shard_map/all_gather | solution.py:144
  10.4 372.9 %all-gather.27.cloned.1.call-start = ((), (), s32[]{:S(2)}) async-start(), calls=%async_computation.16 | async-start | bytes 1622016 | tf_op jit(solution)/shard_map/all_gather | solution.py:142
  11.1 406.4 %all-gather.29.cloned.1.call-start = ((), (), s32[]{:S(2)}) async-start(), calls=%async_computation.17 | async-start | bytes 1622016 | tf_op jit(solution)/shard_map/all_gather | solution.py:144
  11.7 630.6 %reduce-scatter.35.cloned.1.call-start = ((), (), s32[]{:S(2)}) async-start(), calls=%async_computation.20 | async-start | bytes 270336
  120.9 40.4 %copy-start.45 = (bf16[2,2,16]{2,1,0:T(2,128)(2,1)S(1)}, bf16[2,2,16]{2,1,0:T(2,128)(2,1)}, u32[]{:S(2)}) copy-start(bf16[2,2,16]{2,1,0:T(2,128)(2,1)} %param.19) | copy-start | bytes 388
  120.9 79.4 %copy-start.40 = (s32[8]{0:T(128)S(1)}, s32[8]{0:T(128)}, u32[]{:S(2)}) copy-start(s32[8]{0:T(128)} %param.14) | copy-start | bytes 100
  120.9 209.6 %copy-start.22 = (f32[8,256]{1,0:T(8,128)}, f32[8,256]{1,0:T(8,128)S(1)}, u32[]{:S(2)}) copy-start(f32[8,256]{1,0:T(8,128)S(1)} %broadcast_multiply_fusion.5) | copy-start | bytes 24580
  123.7 210.4 %copy-start.24 = (f32[8,256]{1,0:T(8,128)}, f32[8,256]{1,0:T(8,128)S(1)}, u32[]{:S(2)}) copy-start(f32[8,256]{1,0:T(8,128)S(1)} %add_rsqrt_fusion.1) | copy-start | bytes 24580
  200.5 133.6 %copy-start.20 = (f32[8,512]{1,0:T(8,128)}, f32[8,512]{1,0:T(8,128)S(1)}, u32[]{:S(2)}) copy-start(f32[8,512]{1,0:T(8,128)S(1)} %fusion.42) | copy-start | bytes 49156
  383.3 34.2 %copy-start.16 = (bf16[8,256,512]{2,1,0:T(8,128)(2,1)}, bf16[8,256,512]{2,1,0:T(8,128)(2,1)S(1)}, u32[]{:S(2)}) copy-start(bf16[8,256,512]{2,1,0:T(8,128)(2,1)S(1)} %add_convert_fusion.2) | copy-start | bytes 6291460
  438.3 20.5 %copy-start.43 = (f32[512]{0:T(512)S(1)}, f32[512]{0:T(512)}, u32[]{:S(2)}) copy-start(f32[512]{0:T(512)} %convert_element_type.139) | copy-start | bytes 6148
  438.3 20.5 %copy-start.46 = (bf16[1,1536,512]{2,1,0:T(8,128)(2,1)S(1)}, bf16[1,1536,512]{2,1,0:T(8,128)(2,1)}, u32[]{:S(2)}) copy-start(bf16[1,1536,512]{2,1,0:T(8,128)(2,1)} %all-gather.29.cloned.1.call-done) | copy-start | bytes 4718596
  487.1 14.9 copy-start.18
  487.1 14.9 copy-start.21
  509.2 266.7 %reduce-scatter.39.cloned.1.call-start = ((), (), s32[]{:S(2)}) async-start(), calls=%async_computation.22 | async-start | bytes 270336
  512.7 397.0 %reduce-scatter.37.cloned.1.call-start = ((), (), s32[]{:S(2)}) async-start(), calls=%async_computation.21 | async-start | bytes 270336
  513.5 529.6 %reduce-scatter.41.cloned.1.call-start = ((), (), s32[]{:S(2)}) async-start(), calls=%async_computation.23 | async-start | bytes 270336
  514.2 662.1 %reduce-scatter.31.cloned.1.call-start = ((), (), s32[]{:S(2)}) async-start(), calls=%async_computation.18 | async-start | bytes 270336
  538.9 770.6 %reduce-scatter.33.cloned.1.call-start = ((), (), s32[]{:S(2)}) async-start(), calls=%async_computation.19 | async-start | bytes 270336
  539.9 873.1 %reduce-scatter.27.cloned.1.call-start = ((), (), s32[]{:S(2)}) async-start(), calls=%async_computation.12 | async-start | bytes 3244032 | tf_op jit(solution)/shard_map/reduce_scatter | solution.py:175
  548.7 970.7 %reduce-scatter.29.cloned.1.call-start = ((), (), s32[]{:S(2)}) async-start(), calls=%async_computation.13 | async-start | bytes 3244032 | tf_op jit(solution)/shard_map/reduce_scatter | solution.py:175
  556.8 1069.2 %reduce-scatter.25.cloned.1.call-start = ((), (), s32[]{:S(2)}) async-start(), calls=%async_computation.11 | async-start | bytes 3244032 | tf_op jit(solution)/shard_map/reduce_scatter | solution.py:173
  565.6 48.0 %copy-start.27 = (f32[512]{0:T(512)S(1)}, f32[512]{0:T(512)}, u32[]{:S(2)}) copy-start(f32[512]{0:T(512)} %copy-done.26) | copy-start | bytes 6148
  565.6 48.0 %copy-start.29 = (f32[512]{0:T(512)S(1)}, f32[512]{0:T(512)}, u32[]{:S(2)}) copy-start(f32[512]{0:T(512)} %copy-done.28) | copy-start | bytes 6148
  565.6 48.0 %copy-start.31 = (f32[512]{0:T(512)S(1)}, f32[512]{0:T(512)}, u32[]{:S(2)}) copy-start(f32[512]{0:T(512)} %copy-done.30) | copy-start | bytes 6148
  565.6 48.0 %copy-start.33 = (f32[512]{0:T(512)S(1)}, f32[512]{0:T(512)}, u32[]{:S(2)}) copy-start(f32[512]{0:T(512)} %copy-done.32) | copy-start | bytes 6148
  565.7 48.0 %copy-start.35 = (f32[512]{0:T(512)S(1)}, f32[512]{0:T(512)}, u32[]{:S(2)}) copy-start(f32[512]{0:T(512)} %copy-done.34) | copy-start | bytes 6148
  565.7 48.0 %copy-start.37 = (f32[512]{0:T(512)S(1)}, f32[512]{0:T(512)}, u32[]{:S(2)}) copy-start(f32[512]{0:T(512)} %copy-done.36) | copy-start | bytes 6148
  565.7 48.0 %copy-start.39 = (f32[512]{0:T(512)S(1)}, f32[512]{0:T(512)}, u32[]{:S(2)}) copy-start(f32[512]{0:T(512)} %copy-done.38) | copy-start | bytes 6148
  565.7 1166.8 %reduce-scatter.23.cloned.1.call-start = ((), (), s32[]{:S(2)}) async-start(), calls=%async_computation.10 | async-start | bytes 3244032 | tf_op jit(solution)/shard_map/reduce_scatter | solution.py:173
  (29 other events, 150.4 us)
Sparse Core Ops, SparseCore 0:
  11.4 57.6 all-gather.22
  72.0 54.0 all-gather.24
  129.5 54.0 all-gather.26
  186.9 54.2 all-gather.28
  509.3 132.9 reduce-scatter.34
  644.4 131.4 reduce-scatter.38
  778.1 131.4 reduce-scatter.36
  911.9 131.0 reduce-scatter.40
  1045.3 131.0 reduce-scatter.30
  1178.4 131.0 reduce-scatter.32
  1315.0 98.0 reduce-scatter.26
  1418.3 101.0 reduce-scatter.28
  1524.8 101.1 reduce-scatter.24
  1631.3 101.1 reduce-scatter.22
where the time goes:
time: 1740 us
  waiting for transfers between devices  1100 us (63%)
  blocking collectives  311 us (18%)
  matrix products  157 us (9%)
  other arithmetic  111 us (6%)
  local copies, waits for them, and re-layouts  50.3 us (3%)
    unnamed x20, waiting for transfers between devices  676 us
    reduce_scatter x2, waiting for transfers between devices, body(): lax.psum_scatter(terms[4], ('dp', 'fsdp'), scatter_dimension=0, tiled=True)  211 us
    reduce_scatter x2, waiting for transfers between devices, body(): lax.psum_scatter(terms[6], ('dp', 'fsdp'), scatter_dimension=0, tiled=True)  208 us
    unnamed x2, blocking collectives  79.5 us
    all_gather x2, blocking collectives, body(): lax.all_gather(conv_weight[block_index], ('dp', 'fsdp'), axis=1, tiled=True)  79 us
    all_gather x2, blocking collectives, body(): lax.all_gather(ada_shift[block_index], ('dp', 'fsdp'), axis=1, tiled=True)  76.5 us
    all_gather x2, blocking collectives, body(): lax.all_gather(ada_scale[block_index], ('dp', 'fsdp'), axis=1, tiled=True)  75.8 us
    dot_general x2, matrix products, forward_block(): jnp.dot(shaped_low, up_matrix, preferred_element_type=jnp.float32)  67.3 us
  transfers between devices with their start and end apart: 14, of which 10 were waited for; matrix products, arithmetic and copies ran while one was open for 13% of the time, Pallas kernels for 0%

commit v1 on v0

v1 whole, which is shorter than its diff:
```python
import functools
import math
import jax
import jax.numpy as jnp
from jax import lax
from jax.experimental import pallas as pl
from jax.experimental.pallas import tpu as pltpu
from jax.sharding import PartitionSpec as P

F32 = jnp.float32
BF16 = jnp.bfloat16
EPSILON = 1e-06
TAPS, CONV_BIAS, SCALE, SHIFT, DOWN_BIAS, GAIN, ROWS = 0, 7, 8, 10, 12, 13, 16
A_TAPS, A_BIAS, A_SCALE, A_SHIFT, A_DOWN, A_GAIN = 0, 7, 8, 9, 10, 11
HALO = 3
LANES = 128
VMEM_LIMIT = 64 * 1024 * 1024 - 128 * 1024
NN = (((1,), (0,)), ((), ()))
NT = (((1,), (1,)), ((), ()))
TN = (((0,), (0,)), ((), ()))
DMA = pltpu.SemaphoreType.DMA


def mm(a, b, dims):
    return lax.dot_general(a, b, dims, preferred_element_type=F32)


def gelu_pair(before):
    u = before * math.sqrt(0.5)
    phi = 0.5 + 0.5 * lax.erf(u)
    bell = jnp.exp2(u * u * (-math.log2(math.e))) * (1.0 / math.sqrt(math.pi))
    return before * phi, phi + u * bell


def per_clip(values, clips, width):
    rows = lax.broadcasted_iota(jnp.int32, (clips, width), 0)
    out = jnp.zeros((clips, width), jnp.int32)
    for c in range(clips):
        out = jnp.where(rows == c, values[c], out)
    return out


def prepare(small, lens, groups, s8, len8, group_count):
    clips, width = len8.shape
    for r in range(14):
        s8[r] = jnp.broadcast_to(small[r : r + 1, :], (clips, width))
    member = per_clip(groups, clips, width)
    len8[...] = per_clip(lens, clips, width)
    gain = jnp.zeros((clips, width), F32)
    shift = jnp.zeros((clips, width), F32)
    for g in range(group_count):
        chosen = jnp.where(member == g, 1.0, 0.0)
        gain = gain + chosen * s8[SCALE + g]
        shift = shift + chosen * s8[SHIFT + g]
    s8[SCALE] = gain
    s8[SHIFT] = shift


def keep_frames(v, t0, len8, other=0.0):
    t = lax.broadcasted_iota(jnp.int32, v.shape, 0) + t0
    return jnp.where(t < len8[...][None], v, other)


def spread_clips(block, t0, dst, d0, frames):
    clips = block.shape[0]
    for c in range(clips):
        for t in range(0, frames, 16):
            v = block[c, pl.ds(t0 + t, 16), :].astype(F32)
            for l in range(dst.shape[0]):
                dst[l, pl.ds((d0 + t) * clips + c, 16, stride=clips), :] = v[:, l * LANES : (l + 1) * LANES]


def collect_clips(src, block, frames):
    clips = block.shape[0]
    for c in range(clips):
        for t in range(0, frames, 16):
            for l in range(src.shape[0]):
                v = src[l, pl.ds(t * clips + c, 16, stride=clips), :]
                block[c, t : t + 16, l * LANES : (l + 1) * LANES] = v.astype(block.dtype)


def rows_of(src, start, n):
    return jnp.concatenate([src[l, pl.ds(start, n), :] for l in range(src.shape[0])], axis=-1)


def put_rows(dst, start, v):
    for l in range(dst.shape[0]):
        dst[l, pl.ds(start, v.shape[0]), :] = v[:, l * LANES : (l + 1) * LANES]


def fold(v):
    return jnp.sum(v, axis=0)


def smem():
    return pl.BlockSpec(memory_space=pltpu.SMEM)


def vmem():
    return pl.BlockSpec(memory_space=pltpu.VMEM)


def hbm():
    return pl.BlockSpec(memory_space=pl.ANY)


def whole(*dims):
    return pl.BlockSpec(dims, lambda i: (0,) * len(dims), pipeline_mode=pl.Buffered(1))


def shape(dims, dtype=F32):
    return jax.ShapeDtypeStruct(dims, dtype)


MESH = pl.DeviceIdType.MESH
PACK = 20


class Place:
    def __init__(self, deep, side):
        self.deep, self.side = deep, side
        self.z = lax.axis_index("dp")
        f = lax.axis_index("fsdp")
        self.f = f
        self.core = lax.rem(f, 2)
        chip = f // 2
        self.low = lax.rem(chip, side)
        self.high = chip // side
        self.first = jnp.where(self.core == 0, self.high, self.low)
        self.second = jnp.where(self.core == 0, self.low, self.high)

    def chip_of(self, first, second):
        high = jnp.where(self.core == 0, first, second)
        low = jnp.where(self.core == 0, second, first)
        return high, low

    def fsdp_of(self, first, second):
        high, low = self.chip_of(first, second)
        return (high * self.side + low) * 2 + self.core

    def z_peer(self, p):
        return {"dp": lax.rem(self.z + p, self.deep)}

    def first_peer(self, p):
        return {"fsdp": self.fsdp_of(lax.rem(self.first + p, self.side), self.second)}

    def second_peer(self, p):
        return {"fsdp": self.fsdp_of(self.first, lax.rem(self.second + p, self.side))}

    def core_peer(self):
        return {"fsdp": self.f + 1 - 2 * self.core}

    def greet(self):
        barrier = pltpu.get_barrier_semaphore()
        peers = [self.z_peer(p) for p in range(1, self.deep)]
        peers += [self.first_peer(p) for p in range(1, self.side)]
        peers += [self.second_peer(p) for p in range(1, self.side)]
        peers.append(self.core_peer())
        for peer in peers:
            pl.semaphore_signal(barrier, inc=1, device_id=peer, device_id_type=MESH)
        pl.semaphore_wait(barrier, len(peers))


def send(src, dst, send_sem, recv_sem, peer):
    return pltpu.make_async_remote_copy(
        src_ref=src, dst_ref=dst, send_sem=send_sem, recv_sem=recv_sem, device_id=peer, device_id_type=MESH
    )


def run(copies):
    for c in copies:
        c.start()


def done(copies):
    for c in copies:
        c.wait()


def weight_route(place, own, full, sems):
    zs, zr, fs, fr, ss, sr, cs, cr = sems
    deep, side, core = place.deep, place.side, place.core

    def held(p, q):
        high, low = place.chip_of(lax.rem(place.first + p, side), lax.rem(place.second + q, side))
        return full.at[:, high, low, core]

    mine = full.at[place.z, place.high, place.low, core]
    along_z = [send(own, mine, zs.at[p - 1], zr.at[p - 1], place.z_peer(p)) for p in range(1, deep)]
    along_first = [
        send(held(0, 0), held(0, 0), fs.at[p - 1], fr.at[p - 1], place.first_peer(p)) for p in range(1, side)
    ]
    along_second = []
    for j in range(side):
        high, low = place.chip_of(j, place.second)
        line = full.at[:, high, low, core]
        for p in range(1, side):
            n = j * (side - 1) + p - 1
            along_second.append(send(line, line, ss.at[n], sr.at[n], place.second_peer(p)))
    across = lambda p, q: send(held(p, q), held(p, q), cs.at[p * side + q], cr.at[p * side + q], place.core_peer())
    over = [[across(0, 0)], [across(p, 0) for p in range(1, side)],
            [across(p, q) for q in range(1, side) for p in range(side)]]
    return [along_z, along_first, along_second], over


def gather_sems(count, deep, side):
    one = [deep - 1, deep - 1, side - 1, side - 1, side * (side - 1), side * (side - 1), side * side, side * side]
    return [DMA((count, n)) for n in one]


def place_small(place, shards, pack, group_count, taps):
    conv_w, conv_b, scale, shift, up_b, down_b, gain = shards
    width = conv_b.shape[1]
    lane = lax.broadcasted_iota(jnp.int32, (width, LANES), 1)
    row = lax.broadcasted_iota(jnp.int32, (width, LANES), 0)
    spot = jnp.where(lane == row + place.f * width, 1.0, 0.0).astype(BF16)
    wide = up_b.shape[1]
    span = wide * LANES // width
    lane = lax.broadcasted_iota(jnp.int32, (wide, span), 1)
    row = lax.broadcasted_iota(jnp.int32, (wide, span), 0)
    spread = jnp.where(lane == row + place.f * wide, 1.0, 0.0).astype(BF16)
    pack[...] = jnp.zeros(pack.shape, F32)
    for b in range(2):
        o = b * PACK
        for k in range(taps):
            pack[o + k : o + k + 1, :] = mm(conv_w[k, b : b + 1, :], spot, NN)
        pack[o + SCALE : o + SCALE + group_count, :] = mm(scale[b], spot, NN)
        pack[o + SHIFT : o + SHIFT + group_count, :] = mm(shift[b], spot, NN)
        for src, at in ((conv_b, CONV_BIAS), (down_b, DOWN_BIAS), (gain, GAIN)):
            pack[o + at : o + at + 1, :] = mm(src[b : b + 1, :], spot, NN)
        bias = mm(up_b[b : b + 1, :], spread, NN)
        for q in range(span // LANES):
            pack[o + 14 + q : o + 15 + q, :] = bias[:, q * LANES : (q + 1) * LANES]


class Gather:
    def __init__(self, shards, up_full, down_full, small_full, upb_full, refs, deep, side, group_count, taps):
        (self.pack, self.zbuf, self.first_in, self.first_sum, self.second_in, self.second_sum, self.core_in,
         self.local_sems, self.out_sems, self.small_s, self.small_r) = refs[:11]
        sems = refs[11:]
        self.place = place = Place(deep, side)
        self.small_full, self.upb_full, self.shards = small_full, upb_full, shards
        self.group_count, self.taps = group_count, taps
        up_w, down_w = shards[4], shards[6]
        self.full = (up_full, down_full)
        self.routes, self.local = [], []
        for n, (own, full) in enumerate(
            ((up_w.at[0], up_full.at[0]), (down_w.at[0], down_full.at[0]), (up_w.at[1], up_full.at[1]), (down_w.at[1], down_full.at[1]))
        ):
            self.routes.append(weight_route(place, own, full, [s.at[n] for s in sems]))
            spot = full.at[place.z, place.high, place.low, place.core]
            self.local.append(pltpu.make_async_copy(own, spot, self.local_sems.at[n]))
        stages = [
            [(self.zbuf.at[place.z], self.zbuf.at[place.z], place.z_peer(p)) for p in range(1, deep)],
            [(self.zbuf, self.first_in.at[p - 1], place.first_peer(p)) for p in range(1, side)],
            [(self.first_sum, self.second_in.at[p - 1], place.second_peer(p)) for p in range(1, side)],
            [(self.second_sum, self.core_in, place.core_peer())],
        ]
        n = 0
        self.small = []
        for stage in stages:
            copies = []
            for src, dst, peer in stage:
                copies.append(send(src, dst, self.small_s.at[n], self.small_r.at[n], peer))
                n += 1
            self.small.append(copies)

    def begin(self, n):
        run(self.routes[n][0][0])
        self.local[n].start()

    def after_z(self, n):
        along, over = self.routes[n]
        self.local[n].wait()
        done(along[0])
        run(along[1])
        run(over[0])

    def after_first(self, n):
        along, over = self.routes[n]
        done(along[1])
        run(along[2])
        run(over[1])

    def after_second(self, n):
        along, over = self.routes[n]
        done(along[2])
        run(over[2])

    def end(self, n):
        for copies in self.routes[n][1]:
            done(copies)

    def early(self, spread, ready, conv, tiles):
        place = self.place
        place.greet()
        self.begin(0)
        conv_w, conv_b, scale, shift, _, up_b, _, down_b, gain = self.shards
        place_small(place, (conv_w, conv_b, scale, shift, up_b, down_b, gain), self.pack, self.group_count, self.taps)
        self.zbuf[place.z] = self.pack[...]
        run(self.small[0])
        self.begin(1)
        spread()
        done(self.small[0])
        run(self.small[1])
        self.after_z(0)
        done(self.small[1])
        total = self.zbuf[...]
        for p in range(1, place.side):
            total = total + self.first_in[p - 1]
        self.first_sum[...] = total
        run(self.small[2])
        self.after_z(1)
        self.begin(2)
        self.begin(3)
        done(self.small[2])
        total = self.first_sum[...]
        for p in range(1, place.side):
            total = total + self.second_in[p - 1]
        self.second_sum[...] = total
        run(self.small[3])
        self.after_first(0)
        done(self.small[3])
        self.finish_small()
        ready()
        conv(0, tiles // 4)
        self.after_first(1)
        conv(tiles // 4, tiles // 2)
        self.after_second(0)
        conv(tiles // 2, tiles)
        self.after_second(1)
        self.end(0)

    def finish_small(self):
        total = self.second_sum[...] + self.core_in[...]
        deep = self.place.deep
        per = self.upb_full.shape[2] // deep
        self.small_full[...] = jnp.zeros(self.small_full.shape, F32)
        for b in range(2):
            o = b * PACK
            for z in range(deep):
                self.small_full[b, 0:14, z * LANES : (z + 1) * LANES] = total[z, o : o + 14, :]
                for q in range(per // LANES):
                    at = z * per + q * LANES
                    self.upb_full[b, :, at : at + LANES] = total[z, o + 14 + q : o + 15 + q, :]

    def late(self, i, tiles, up_out, down_out):
        outs = (up_out, down_out)
        keep = lambda n: pltpu.make_async_copy(self.full[n % 2].at[n // 2], outs[n % 2].at[n // 2], self.out_sems.at[n])

        @pl.when(i == 1)
        def _():
            keep(0).start()
            self.after_z(2)
            self.after_z(3)

        @pl.when(i == tiles // 2 + 1)
        def _():
            self.after_first(2)
            self.after_first(3)

        @pl.when(i == tiles)
        def _():
            self.end(1)
            keep(1).start()

        @pl.when(i == 2 * tiles - tiles // 4)
        def _():
            self.after_second(2)
            self.after_second(3)

        @pl.when(i == 2 * tiles)
        def _():
            for n in (2, 3):
                self.end(n)
                keep(n).start()

        @pl.when(i == 3 * tiles - 1)
        def _():
            for n in range(4):
                keep(n).wait()


def gather_scratch(deep, side):
    buf = pltpu.VMEM((deep, 2 * PACK, LANES), F32)
    many = pltpu.VMEM((side - 1, deep, 2 * PACK, LANES), F32)
    n = deep - 1 + 2 * (side - 1) + 1
    return [pltpu.VMEM((2 * PACK, LANES), F32), buf, many, buf, many, buf, buf, DMA((4,)), DMA((4,)), DMA((n,)), DMA((n,))] + gather_sems(
        4, deep, side
    )


def conv_norm(masked, f0, frames, s8, normed, inv, shaped, taps, step=4):
    clips, width = s8.shape[1:]
    for j in range(0, frames, step):
        mixed = s8[CONV_BIAS][None]
        for k in range(taps):
            mixed = mixed + s8[TAPS + k][None] * masked[pl.ds(f0 + j + k, step)]
        center = mixed - jnp.mean(mixed, axis=-1, keepdims=True)
        inv_std = lax.rsqrt(jnp.mean(center * center, axis=-1, keepdims=True) + EPSILON)
        norm = center * inv_std
        normed[pl.ds(f0 + j, step)] = norm
        inv[pl.ds(f0 + j, step)] = jnp.broadcast_to(inv_std, (step, clips, LANES))
        rows = norm * s8[SCALE][None] + s8[SHIFT][None]
        at = pl.multiple_of((f0 + j) * clips, step * clips)
        shaped[pl.ds(at, step * clips), :] = rows.reshape(step * clips, width).astype(BF16)


def up_gelu(shaped, up_cols, u8, act, r0, slope, rows, hidden, cols=256, sub=16):
    left = shaped[pl.ds(r0, rows), :]
    for n in range(0, hidden, cols):
        before = mm(left, up_cols(n, n + cols), NN)
        for r in range(0, rows, sub):
            piece = before[r : r + sub].reshape(sub // 8, 8, cols) + u8[:, n : n + cols][None]
            a, s = gelu_pair(piece.reshape(sub, cols))
            act[pl.ds(r0 + r, sub), n : n + cols] = a.astype(BF16)
            slope[r : r + sub, n : n + cols] = s.astype(slope.dtype)


def forward_kernel(*refs, near, deep, side, ft, taps, group_count):
    lens, groups, frames = refs[:3]
    if near:
        shards, refs = refs[3:12], refs[12:]
        (out, act_out, slope, normed_out, inv_out, shaped_out, masked_out, up_out, down_out, small_full, upb_full) = refs[:11]
        refs = refs[11:]
    else:
        small_full, upb_full, up_full, down_full = refs[3:7]
        (out, act_out, slope, normed_out, inv_out, shaped_out, masked_out) = refs[7:14]
        refs = refs[14:]
    (stream, masked0, masked1, normed, inv, shaped, first_rows, act, s8, u8, len8, save_sem, act_sem, row_sem) = refs[:14]
    refs = refs[14:]
    if near:
        up_full, down_full = refs[:2]
        gather_refs = refs[2:]

    i = pl.program_id(0)
    clips, frame_count, width = frames.shape
    hidden = act.shape[1]
    tiles = frame_count // ft
    rows = ft * clips

    def up_cols(b):
        if near:
            return lambda lo, hi: up_full[b, :, :, :, :, :, lo:hi].reshape(width, hi - lo)
        return lambda lo, hi: up_full[b, :, lo:hi]

    def down_rows(b):
        return down_full[b].reshape(hidden, width)

    body = pl.ds(HALO, frame_count)
    save = lambda n, src, dst: pltpu.make_async_copy(src, dst, save_sem.at[n])
    saves0 = [
        save(0, masked0.at[body], masked_out.at[0]), save(1, normed, normed_out.at[0]),
        save(2, inv, inv_out.at[0]), save(3, shaped, shaped_out.at[0]),
    ]
    save_masked1 = save(4, masked1.at[body], masked_out.at[1])
    tail = lambda b, j: pltpu.make_async_copy(
        act.at[pl.ds(pl.multiple_of(j * rows, rows), rows)],
        act_out.at[b, pl.ds(pl.multiple_of(j * rows, rows), rows)], act_sem.at[j])

    def row_saves(j):
        f = pl.ds(j * ft, ft)
        r = pl.ds(pl.multiple_of(j * rows, rows), rows)
        return [
            pltpu.make_async_copy(normed.at[f], normed_out.at[1, f], row_sem.at[0, j]),
            pltpu.make_async_copy(inv.at[f], inv_out.at[1, f], row_sem.at[1, j]),
            pltpu.make_async_copy(shaped.at[r], shaped_out.at[1, r], row_sem.at[2, j]),
        ]

    def spread():
        def one(n, carry):
            t0 = pl.multiple_of(n * 16, 16)
            spread_clips(frames, t0, stream, 0, 16)
            v = rows_of(stream, 0, 16 * clips)
            at = pl.multiple_of(t0 * clips, 16 * clips)
            first_rows[pl.ds(at, 16 * clips), :] = v.astype(BF16)
            masked0[pl.ds(HALO + t0, 16)] = keep_frames(v.reshape(16, clips, width), t0, len8)
            return carry
        lax.fori_loop(0, frame_count // 16, one, 0)

    def conv0(lo, hi):
        def one(n, carry):
            conv_norm(masked0, n * ft, ft, s8.at[0], normed, inv, shaped, taps)
            return carry
        lax.fori_loop(lo, hi, one, 0)

    @pl.when(i == 0)
    def _():
        zeros = jnp.zeros((HALO, clips, width), F32)
        for m in (masked0, masked1):
            m[0:HALO] = zeros
            m[HALO + frame_count :] = zeros
        len8[...] = per_clip(lens, clips, width)

        def ready():
            for b in range(2):
                prepare(small_full.at[b], lens, groups, s8.at[b], len8, group_count)
                u8[b] = jnp.broadcast_to(upb_full[b, 0:1, :], u8.shape[1:])

        if near:
            Gather(shards, up_full, down_full, small_full, upb_full, gather_refs, deep, side, group_count, taps).early(
                spread, ready, conv0, tiles)
        else:
            spread()
            ready()
            conv0(0, tiles)
        for c in saves0:
            c.start()

    if near:
        Gather(shards, up_full, down_full, small_full, upb_full, gather_refs, deep, side, group_count, taps).late(
            i, tiles, up_out, down_out)

    @pl.when(i < tiles)
    def _():
        r0 = pl.multiple_of(i * rows, rows)
        up_gelu(shaped, up_cols(0), u8.at[0], act, r0, slope, rows, hidden)
        tail(0, i).start()

    @pl.when((i >= tiles) & (i < 2 * tiles))
    def _():
        j = i - tiles
        f0 = j * ft
        r0 = pl.multiple_of(j * rows, rows)
        branch = mm(act[pl.ds(r0, rows), :], down_rows(0), NN)
        for t in range(0, ft, 4):
            b = branch[t * clips : (t + 4) * clips].reshape(4, clips, width) + s8[0, DOWN_BIAS][None]
            total = masked0[pl.ds(HALO + f0 + t, 4)] + s8[0, GAIN][None] * b
            masked1[pl.ds(HALO + f0 + t, 4)] = keep_frames(total, f0 + t, len8)
        tail(0, j).wait()

    @pl.when(i == 2 * tiles)
    def _():
        for c in saves0:
            c.wait()
        save_masked1.start()

    @pl.when(i >= 2 * tiles)
    def _():
        j = i - 2 * tiles
        f0 = j * ft
        r0 = pl.multiple_of(j * rows, rows)
        conv_norm(masked1, f0, ft, s8.at[1], normed, inv, shaped, taps)
        for c in row_saves(j):
            c.start()
        up_gelu(shaped, up_cols(1), u8.at[1], act, r0, slope, rows, hidden)
        tail(1, j).start()
        branch = mm(act[pl.ds(r0, rows), :], down_rows(1), NN)
        for t in range(0, ft, 4):
            b = branch[t * clips : (t + 4) * clips].reshape(4, clips, width) + s8[1, DOWN_BIAS][None]
            total = masked1[pl.ds(HALO + f0 + t, 4)] + s8[1, GAIN][None] * b
            at = pl.multiple_of(r0 + t * clips, 4 * clips)
            first = first_rows[pl.ds(at, 4 * clips), :].astype(F32).reshape(4, clips, width)
            put_rows(stream, t * clips, keep_frames(total, f0 + t, len8, first).reshape(4 * clips, width))
        collect_clips(stream, out, ft)

    @pl.when(i == 3 * tiles - 1)
    def _():
        save_masked1.wait()
        for j in range(tiles):
            tail(1, j).wait()
            for c in row_saves(j):
                c.wait()


def forward(near, deep, side, lens, groups, frames, weights, hidden, ft, taps, group_count):
    clips, fc, d = frames.shape
    h = hidden
    n, r = fc // ft, ft * clips
    R = fc * clips
    slope_at = lambda i: jnp.where(i < n, i, jnp.where(i < 2 * n, n - 1, i - n))
    out_specs = [
        pl.BlockSpec((clips, ft, d), lambda i: (0, jnp.maximum(i - 2 * n, 0), 0)), hbm(),
        pl.BlockSpec((r, h), lambda i: (slope_at(i), 0)), hbm(), hbm(), hbm(), hbm(),
    ]
    out_shape = [
        shape((clips, fc, d), BF16), shape((2, R, h), BF16), shape((2 * R, h), BF16), shape((2, fc, clips, d)),
        shape((2, fc, clips, LANES)), shape((2, R, d), BF16), shape((2, fc, clips, d)),
    ]
    scratch = [
        pltpu.VMEM((d // LANES, max(r, 16 * clips), LANES), F32),
        pltpu.VMEM((fc + 2 * HALO, clips, d), F32), pltpu.VMEM((fc + 2 * HALO, clips, d), F32),
        pltpu.VMEM((fc, clips, d), F32), pltpu.VMEM((fc, clips, LANES), F32), pltpu.VMEM((R, d), BF16),
        pltpu.VMEM((R, d), BF16), pltpu.VMEM((R, h), BF16),
        pltpu.VMEM((2, 14, clips, d), F32), pltpu.VMEM((2, clips, h), F32), pltpu.VMEM((clips, d), jnp.int32),
        DMA((5,)), DMA((n,)), DMA((3, n)),
    ]
    params = dict(vmem_limit_bytes=VMEM_LIMIT)
    if near:
        urows, drows = weights[4].shape[1], weights[6].shape[1]
        dims = (2, deep, side, side, 2)
        full = [dims + (urows, h), dims + (drows, d)]
        in_specs = [smem(), smem(), whole(clips, fc, d)] + [vmem()] * 9
        out_specs += [hbm(), hbm(), vmem(), vmem()]
        out_shape += [shape(full[0], BF16), shape(full[1], BF16), shape((2, ROWS, d)), shape((2, 1, h))]
        scratch += [pltpu.VMEM(f, BF16) for f in full] + gather_scratch(deep, side)
        params.update(collective_id=0, has_side_effects=True)
    else:
        in_specs = [smem(), smem(), whole(clips, fc, d)] + [vmem()] * 4
    return pl.pallas_call(
        functools.partial(forward_kernel, near=near, deep=deep, side=side, ft=ft, taps=taps, group_count=group_count),
        name="forward",
        grid=(3 * n,),
        in_specs=in_specs,
        out_specs=out_specs,
        out_shape=out_shape,
        scratch_shapes=scratch,
        compiler_params=pltpu.CompilerParams(**params),
    )(lens, groups, frames, *weights)


class Scatter:
    def __init__(self, place, term, bufs, sems):
        self.place, self.term = place, term
        self.core_out, self.core_in, self.second_in, self.first_in, self.z_in = bufs
        self.sems = sems

    def entry(self, z, first, second):
        high, low = self.place.chip_of(first, second)
        return (z * self.place.side + high) * self.place.side + low

    def own(self, e, core):
        rows = self.core_in.shape[1]
        return self.term[pl.ds(pl.multiple_of((e * 2 + core) * rows, 8), rows), :]

    def fill(self, count, write):
        def one(n, carry):
            write(n)
            return carry
        lax.fori_loop(0, count, one, 0)


    def second_at(self, p):
        return (p - 1) * self.place.side * self.place.deep

    def first_at(self, p):
        return self.second_at(self.place.side) + (p - 1) * self.place.deep

    def z_at(self, p):
        return self.first_at(self.place.side) + p - 1

    def core_copies(self):
        return [send(self.core_out, self.core_in, self.sems[0].at[0], self.sems[1].at[0], self.place.core_peer())]

    def second_copies(self):
        return [
            send(self.core_out.at[pl.ds(self.second_at(p), self.place.side * self.place.deep)], self.second_in.at[p - 1], self.sems[2].at[p - 1], self.sems[3].at[p - 1], self.place.second_peer(p))
            for p in range(1, self.place.side)
        ]

    def first_copies(self):
        return [
            send(self.core_out.at[pl.ds(self.first_at(p), self.place.deep)], self.first_in.at[p - 1], self.sems[4].at[p - 1], self.sems[5].at[p - 1], self.place.first_peer(p))
            for p in range(1, self.place.side)
        ]

    def z_copies(self):
        return [
            send(self.core_out.at[self.z_at(p)], self.z_in.at[p - 1], self.sems[6].at[p - 1], self.sems[7].at[p - 1], self.place.z_peer(p))
            for p in range(1, self.place.deep)
        ]

    def core_start(self):
        def write(n):
            self.core_out[n] = self.own(n, 1 - self.place.core).astype(BF16)
        self.fill(self.core_out.shape[0], write)
        run(self.core_copies())

    def part1(self, z, first, second):
        e = self.entry(z, first, second)
        return self.own(e, self.place.core) + self.core_in[e].astype(F32)

    def part2(self, z, first):
        total = self.part1(z, first, self.place.second)
        for p in range(1, self.place.side):
            total = total + self.second_in[p - 1, first * self.place.deep + z].astype(F32)
        return total

    def part3(self, z):
        total = self.part2(z, self.place.first)
        for p in range(1, self.place.side):
            total = total + self.first_in[p - 1, z].astype(F32)
        return total

    def second_start(self):
        at = self.place
        done(self.core_copies())
        copies = self.second_copies()
        for p in range(1, at.side):
            to = lax.rem(at.second + p, at.side)
            def write(n):
                first, z = n // at.deep, lax.rem(n, at.deep)
                self.core_out[self.second_at(p) + n] = self.part1(z, first, to).astype(BF16)
            self.fill(at.side * at.deep, write)
            copies[p - 1].start()

    def first_start(self):
        at = self.place
        done(self.second_copies())
        copies = self.first_copies()
        for p in range(1, at.side):
            to = lax.rem(at.first + p, at.side)
            def write(z):
                self.core_out[self.first_at(p) + z] = self.part2(z, to).astype(BF16)
            self.fill(at.deep, write)
            copies[p - 1].start()

    def z_start(self):
        at = self.place
        done(self.first_copies())
        copies = self.z_copies()
        for p in range(1, at.deep):
            self.core_out[self.z_at(p)] = self.part3(lax.rem(at.z + p, at.deep)).astype(BF16)
            copies[p - 1].start()

    def finish(self, out):
        done(self.z_copies())
        total = self.part3(self.place.z)
        for p in range(1, self.place.deep):
            total = total + self.z_in[p - 1].astype(F32)
        out[...] = total


def scatter_bufs(deep, side, rows, cols):
    v = lambda *lead: pltpu.VMEM(lead + (rows, cols), BF16)
    e = deep * side * side
    return [v(e), v(e), v(side - 1, side * deep), v(side - 1, deep), v(deep - 1)]


def scatter_sems(count, deep, side):
    return [DMA((count, n)) for n in (1, 1, side - 1, side - 1, side - 1, side - 1, deep - 1, deep - 1)]


def pack_small(small, upb, b, terms, deep):
    per = upb.shape[1] // deep
    o = b * PACK
    for z in range(deep):
        terms[z, o : o + 14, :] = small[0:14, z * LANES : (z + 1) * LANES]
        for q in range(per // LANES):
            at = z * per + q * LANES
            terms[z, o + 14 + q : o + 15 + q, :] = upb[:, at : at + LANES]


def sum_small(place, terms, bufs, z_in, out, s, r):
    stages = [[place.core_peer()], [place.second_peer(p) for p in range(1, place.side)],
              [place.first_peer(p) for p in range(1, place.side)]]
    n = 0
    here = terms
    for stage, peers in enumerate(stages):
        into, total_ref = bufs[stage]
        copies = []
        for p, peer in enumerate(peers):
            copies.append(send(here, into.at[p], s.at[n], r.at[n], peer))
            n += 1
        run(copies)
        yield
        done(copies)
        total = here[...]
        for p in range(len(peers)):
            total = total + into[p]
        total_ref[...] = total
        here = total_ref
    copies = []
    for p in range(1, place.deep):
        to = lax.rem(place.z + p, place.deep)
        copies.append(send(here.at[to], z_in.at[p - 1], s.at[n], r.at[n], place.z_peer(p)))
        n += 1
    run(copies)
    yield
    done(copies)
    total = here[place.z]
    for p in range(1, place.deep):
        total = total + z_in[p - 1]
    out[...] = total


def small_bufs(deep, side):
    buf = pltpu.VMEM((deep, 2 * PACK, LANES), F32)
    many = lambda n: pltpu.VMEM((n, deep, 2 * PACK, LANES), F32)
    n = deep - 1 + 2 * (side - 1) + 1
    return [buf, many(1), buf, many(side - 1), buf, many(side - 1), buf, pltpu.VMEM((deep - 1, 2 * PACK, LANES), F32), DMA((n,)), DMA((n,))]


class Sums:
    def __init__(self, refs, dup, ddown, up_part, down_part, small_part, small_grad, upb_grad, deep, side):
        self.place = Place(deep, side)
        (self.terms, c_in, c_sum, s_in, s_sum, f_in, f_sum, self.z_in, self.small_s, self.small_r) = refs[:10]
        self.bufs = ((c_in, c_sum), (s_in, s_sum), (f_in, f_sum))
        refs = refs[10:]
        sems = refs[-8:]
        self.small_part, self.small_grad, self.upb_grad = small_part, small_grad, upb_grad
        self.jobs = {}
        self.outs = {}
        for n, (b, term, out) in enumerate(
            ((1, ddown, down_part), (1, dup, up_part), (0, ddown, down_part), (0, dup, up_part))
        ):
            job = Scatter(self.place, term.at[b], refs[5 * n : 5 * n + 5], [s.at[n] for s in sems])
            self.jobs.setdefault(b, []).append((job, out.at[b]))

    def each(self, b, what):
        for job, out in self.jobs[b]:
            if what == "finish":
                job.finish(out)
            else:
                getattr(job, what)()

    def before(self, i, span, parts, tiles):
        @pl.when(i == 0)
        def _():
            self.place.greet()

        plan = [
            (parts, 1, "core_start"), (parts + 3, 1, "second_start"), (span, 1, "first_start"),
            (span + 3, 1, "z_start"), (span + parts - 1, 1, "finish"),
            (span + parts, 0, "core_start"), (span + parts + 3, 0, "second_start"), (2 * span - 1, 0, "first_start"),
        ]
        for at, b, what in plan:
            @pl.when(i == at)
            def _():
                self.each(b, what)

    def after(self, i, span):
        @pl.when(i == 2 * span - 1)
        def _():
            self.terms[...] = jnp.zeros(self.terms.shape, F32)
            for b in range(2):
                pack_small(self.small_grad.at[b], self.upb_grad.at[b], b, self.terms, self.place.deep)
            steps = sum_small(self.place, self.terms, self.bufs, self.z_in, self.small_part, self.small_s, self.small_r)
            next(steps)
            next(steps)
            self.each(0, "z_start")
            for _ in steps:
                pass
            self.each(0, "finish")


def sums_scratch(deep, side, urows, drows, d, h):
    ub, db = scatter_bufs(deep, side, urows, h), scatter_bufs(deep, side, drows, d)
    return small_bufs(deep, side) + db + ub + db + ub + scatter_sems(4, deep, side)


def norm_back(gs, normed, inv, s8, gm, gm0, acc, frames, step=4):
    clips, width = s8.shape[1:]
    a_scale, a_shift, a_bias = acc[A_SCALE], acc[A_SHIFT], acc[A_BIAS]
    for j in range(0, frames, step):
        g = gs[j * clips : (j + step) * clips].reshape(step, clips, width)
        norm = normed[j : j + step]
        gn = g * norm
        a_scale = a_scale + fold(gn)
        a_shift = a_shift + fold(g)
        gg = g * s8[SCALE][None]
        mean = jnp.mean(gg, axis=-1, keepdims=True)
        mean_norm = jnp.mean(gn * s8[SCALE][None], axis=-1, keepdims=True)
        inv_std = jnp.concatenate([inv[j : j + step]] * (width // LANES), axis=-1)
        grad = inv_std * (gg - mean - norm * mean_norm)
        a_bias = a_bias + fold(grad)
        gm[pl.ds(gm0 + j, step)] = grad
    acc[A_SCALE], acc[A_SHIFT], acc[A_BIAS] = a_scale, a_shift, a_bias


def conv_back(gm, gm0, s8, masked, gs, t0, out, acc, frames, len8, taps, step=8):
    clips, width = len8.shape
    half = taps // 2
    for l in range(width // LANES):
        cols = slice(l * LANES, (l + 1) * LANES)
        sums = [acc[A_TAPS + k, :, cols] for k in range(taps)]
        for j in range(0, frames, step):
            here = masked[j : j + step, :, cols]
            total = None
            for k in range(taps):
                piece = gm[pl.ds(gm0 + j + half - k, step), :, cols]
                term = s8[TAPS + k, :, cols][None] * piece
                total = term if total is None else total + term
                sums[k] = sums[k] + fold(piece * here)
            t = lax.broadcasted_iota(jnp.int32, total.shape, 0) + (t0 + j)
            total = jnp.where(t < len8[:, cols][None], total, 0.0)
            total = gs[pl.ds(t0 + j, step), :, cols] + total
            gs[pl.ds(t0 + j, step), :, cols] = total
            out[l, j * clips : (j + step) * clips, :] = total.reshape(step * clips, LANES)
        for k in range(taps):
            acc[A_TAPS + k, :, cols] = sums[k]


def finish_small(acc, upb_acc, groups, s8, small_grad, upb_grad, group_count):
    clips, width = acc.shape[1:]
    member = per_clip(groups, clips, width)
    line = lambda v: jnp.sum(v, axis=0, keepdims=True)
    rows = [line(acc[A_TAPS + k]) for k in range(7)]
    rows.append(line(acc[A_BIAS]))
    for base in (A_SCALE, A_SHIFT):
        for g in range(group_count):
            rows.append(line(jnp.where(member == g, acc[base], 0.0)))
    rows.append(line(acc[A_DOWN]))
    rows.append(line((acc[A_GAIN] + s8[DOWN_BIAS] * acc[A_DOWN]) / s8[GAIN]))
    for r, row in enumerate(rows):
        small_grad[r : r + 1, :] = row
    for r in range(len(rows), small_grad.shape[0]):
        small_grad[r : r + 1, :] = jnp.zeros((1, width), F32)
    upb_grad[...] = line(upb_acc[...])


def backward_kernel(*refs, near, deep, side, ft, tiles, parts, taps, group_count):
    lens, groups, og, act, slope, normed, inv, shaped, masked, up, down, small = refs[:12]
    refs = refs[12:]
    if near:
        gs_out, up_part, down_part, small_part = refs[:4]
        dup, ddown, small_grad, upb_grad = refs[4:8]
        refs = refs[8:]
    else:
        gs_out, dup, ddown, small_grad, upb_grad = refs[:5]
        refs = refs[5:]
    gs, gb, gbef, gm, lanes, s8, len8, acc, upb_acc = refs[:9]
    refs = refs[9:]

    i = pl.program_id(0)
    frame_count, clips, width = gs.shape
    hidden = gbef.shape[1]
    cols = hidden // parts
    rows = ft * clips
    total_rows = frame_count * clips
    base = 2 * ft
    span = parts + tiles + 2
    step = lax.rem(i, span)
    b = 1 - i // span

    @pl.when(step == 0)
    def _():
        prepare(small.at[b], lens, groups, s8, len8, group_count)
        acc[...] = jnp.zeros(acc.shape, F32)

    @pl.when(i == 0)
    def _():
        gm[pl.ds(0, base)] = jnp.zeros((base, clips, width), F32)
        gm[pl.ds(base + frame_count, HALO)] = jnp.zeros((HALO, clips, width), F32)

        def one(n, carry):
            t0 = pl.multiple_of(n * 16, 16)
            spread_clips(og, t0, lanes, 0, 16)
            gs[pl.ds(t0, 16)] = rows_of(lanes, 0, 16 * clips).reshape(16, clips, width)
            return carry
        lax.fori_loop(0, frame_count // 16, one, 0)

    @pl.when(step == 0)
    def _():
        def one(n, a_down):
            t0 = n * 4
            gvb = s8[GAIN][None] * keep_frames(gs[pl.ds(t0, 4)], t0, len8)
            at = pl.multiple_of(t0 * clips, 4 * clips)
            gb[pl.ds(at, 4 * clips), :] = gvb.reshape(4 * clips, width).astype(BF16)
            return a_down + fold(gvb)
        acc[A_DOWN] = lax.fori_loop(0, frame_count // 4, one, jnp.zeros((clips, width), F32), unroll=4)

    if near:
        sums = Sums(refs, dup, ddown, up_part, down_part, small_part, small_grad, upb_grad, deep, side)
        sums.before(i, span, parts, tiles)

    @pl.when(step < parts)
    def _():
        c0 = pl.multiple_of(step * cols, cols)
        at = pl.ds(c0, cols)
        grads = gb[...]
        lower = down[0, at, :]
        term = mm(act[0], grads, TN)
        ddown[b, at, :] = term
        acc[A_GAIN] += fold((term * lower.astype(F32)).reshape(cols // 8, 8, width))
        ga = mm(grads, lower, NT)
        total = jnp.zeros((8, cols), F32)
        sub = 16
        for r in range(0, total_rows, sub):
            gr = ga[r : r + sub] * slope[0, r : r + sub, :].astype(F32)
            total = total + fold(gr.reshape(sub // 8, 8, cols))
            gbef[r : r + sub, at] = gr.astype(BF16)
        upb_acc[:, at] = total
        dup[b, :, at] = mm(shaped[0], gbef[:, at], TN)

    j = step - parts

    @pl.when((j >= 0) & (j < tiles))
    def _():
        r0 = pl.multiple_of(j * rows, rows)
        grad = mm(gbef[pl.ds(r0, rows), :], up[0], NT)
        norm_back(grad, normed.at[0], inv.at[0], s8, gm, base + j * ft, acc, ft)

    @pl.when(j >= 2)
    def _():
        conv_back(gm, base + (j - 2) * ft, s8, masked.at[0], gs, (j - 2) * ft, gs_out, acc, ft, len8, taps)

    @pl.when(step == span - 1)
    def _():
        finish_small(acc, upb_acc, groups, s8, small_grad.at[b], upb_grad.at[b], group_count)

    if near:
        sums.after(i, span)


def backward(near, deep, side, lens, groups, og, saved, ups, downs, small, ft, taps, group_count):
    act, slope, normed, inv, shaped, masked = saved
    clips, fc, d = og.shape
    h = ups.shape[2]
    R, r, n = fc * clips, ft * clips, fc // ft
    parts = 6
    cols = h // parts
    span = parts + n + 2
    block = lambda i: 1 - i // span
    part = lambda i: jnp.minimum(lax.rem(i, span), parts - 1)
    tile = lambda i: jnp.clip(lax.rem(i, span) - parts, 0, n - 1)
    late = lambda i: jnp.clip(lax.rem(i, span) - parts - 2, 0, n - 1)
    last = lambda i: jnp.clip(i - span - parts - 2, 0, n - 1)
    in_specs = [
        smem(), smem(), whole(clips, fc, d),
        pl.BlockSpec((1, R, cols), lambda i: (block(i), 0, part(i))),
        pl.BlockSpec((1, R, cols), lambda i: (block(i), 0, part(i))),
        pl.BlockSpec((1, ft, clips, d), lambda i: (block(i), tile(i), 0, 0)),
        pl.BlockSpec((1, ft, clips, LANES), lambda i: (block(i), tile(i), 0, 0)),
        pl.BlockSpec((1, R, d), lambda i: (block(i), 0, 0), pipeline_mode=pl.Buffered(1)),
        pl.BlockSpec((1, ft, clips, d), lambda i: (block(i), late(i), 0, 0)),
        pl.BlockSpec((1, d, h), lambda i: (block(i), 0, 0)),
        pl.BlockSpec((1, h, d), lambda i: (block(i), 0, 0)),
        whole(2, ROWS, d),
    ]
    out_specs = [pl.BlockSpec((d // LANES, r, LANES), lambda i: (0, last(i), 0))]
    out_shape = [shape((d // LANES, R, LANES))]
    sums = [(2, d, h), (2, h, d), (2, ROWS, d), (2, 1, h)]
    scratch = []
    params = dict(vmem_limit_bytes=VMEM_LIMIT)
    if near:
        e = deep * side * side * 2
        urows, drows = d // e, h // e
        out_specs += [vmem()] * 3
        out_shape += [shape((2, urows, h)), shape((2, drows, d)), shape((2 * PACK, LANES))]
        scratch += [pltpu.VMEM(v, F32) for v in sums]
        params.update(collective_id=1, has_side_effects=True)
    else:
        out_specs += [whole(*v) for v in sums]
        out_shape += [shape(v) for v in sums]
    scratch += [
        pltpu.VMEM((fc, clips, d), F32), pltpu.VMEM((R, d), BF16), pltpu.VMEM((R, h), BF16),
        pltpu.VMEM((fc + 2 * ft + HALO, clips, d), F32), pltpu.VMEM((d // LANES, 16 * clips, LANES), F32),
        pltpu.VMEM((14, clips, d), F32), pltpu.VMEM((clips, d), jnp.int32),
        pltpu.VMEM((12, clips, d), F32), pltpu.VMEM((clips, h), F32),
    ]
    if near:
        scratch += sums_scratch(deep, side, urows, drows, d, h)
    return pl.pallas_call(
        functools.partial(backward_kernel, near=near, deep=deep, side=side, ft=ft, tiles=n, parts=parts, taps=taps, group_count=group_count),
        name="backward",
        grid=(2 * span,),
        in_specs=in_specs,
        out_specs=out_specs,
        out_shape=out_shape,
        scratch_shapes=scratch,
        compiler_params=pltpu.CompilerParams(**params),
    )(lens, groups, og, act, slope, normed, inv, shaped, masked, ups, downs, small)


def unpack_kernel(gs, up_in, down_in, small, gin, conv_w, conv_b, scale, shift, up_w, up_b, down_w, down_b, gain):
    collect_clips(gs, gin, gin.shape[1])

    @pl.when(pl.program_id(0) == 0)
    def _():
        unpack_parts(up_in, down_in, small, conv_w, conv_b, scale, shift, up_w, up_b, down_w, down_b, gain)


def unpack_parts(up_in, down_in, small, conv_w, conv_b, scale, shift, up_w, up_b, down_w, down_b, gain):
    f = lax.axis_index("fsdp")
    width = conv_b.shape[1]
    wide = up_b.shape[1]
    span = wide * LANES // width
    turned = pltpu.roll(small[...], lax.rem(LANES - f * width, LANES), 1)
    for b in range(2):
        o = b * PACK
        for k in range(conv_w.shape[0]):
            conv_w[k, b : b + 1, :] = turned[o + k : o + k + 1, :width]
        conv_b[b : b + 1, :] = turned[o + CONV_BIAS : o + CONV_BIAS + 1, :width]
        scale[b] = turned[o + SCALE : o + SCALE + scale.shape[1], :width]
        shift[b] = turned[o + SHIFT : o + SHIFT + shift.shape[1], :width]
        down_b[b : b + 1, :] = turned[o + DOWN_BIAS : o + DOWN_BIAS + 1, :width]
        gain[b : b + 1, :] = turned[o + GAIN : o + GAIN + 1, :width]
        bias = jnp.concatenate([small[o + 14 + q : o + 15 + q, :] for q in range(span // LANES)], axis=1)
        bias = pltpu.roll(jnp.broadcast_to(bias, (8, span)), lax.rem(span - f * wide, span), 1)
        up_b[b : b + 1, :] = bias[0:1, :wide]
    up_w[...] = up_in[...]
    down_w[...] = down_in[...]


def unpack(gs, parts, clips, taps, group_count, width, wide):
    split, R, lanes = gs.shape
    fc = R // clips
    ft = 32
    if parts is None:
        return pl.pallas_call(
            lambda src, dst: collect_clips(src, dst, ft),
            name="unpack",
            grid=(fc // ft,),
            in_specs=[pl.BlockSpec((split, ft * clips, lanes), lambda i: (0, i, 0))],
            out_specs=pl.BlockSpec((clips, ft, split * lanes), lambda i: (0, i, 0)),
            out_shape=shape((clips, fc, split * lanes)),
        )(gs)
    up_in, down_in, small = parts
    outs = [(taps, 2, width), (2, width), (2, group_count, width), (2, group_count, width), up_in.shape, (2, wide),
            down_in.shape, (2, width), (2, width)]
    return pl.pallas_call(
        unpack_kernel,
        name="unpack",
        grid=(fc // ft,),
        in_specs=[pl.BlockSpec((split, ft * clips, lanes), lambda i: (0, i, 0))] + [whole(*v.shape) for v in parts],
        out_specs=[pl.BlockSpec((clips, ft, split * lanes), lambda i: (0, i, 0))] + [whole(*v) for v in outs],
        out_shape=[shape((clips, fc, split * lanes))] + [shape(v) for v in outs],
    )(gs, up_in, down_in, small)


def body(deep, fan, frames, group, lengths, conv_w, conv_b, scale, shift, up_w, up_b, down_w, down_b, gain, out_grad):
    side = math.isqrt(fan // 2)
    clips = frames.shape[0]
    taps, group_count, hidden = conv_w.shape[1], scale.shape[1], up_w.shape[2]
    width, wide = conv_b.shape[1], up_b.shape[1]
    axes = ("dp", "fsdp")
    near = width * fan == LANES and up_w.shape[1] % 16 == 0 and down_w.shape[1] % 16 == 0
    ft = 32
    if near:
        weights = (conv_w.transpose(1, 0, 2), conv_b, scale, shift, up_w, up_b, down_w, down_b, gain)
    else:
        whole_of = lambda v, axis: lax.all_gather(v, axes, axis=axis, tiled=True)
        ups, downs = whole_of(up_w, 1), whole_of(down_w, 1)
        lines = jnp.concatenate(
            [conv_w, conv_b[:, None], scale, shift, down_b[:, None], gain[:, None], jnp.zeros((2, 2, width), BF16)], axis=1
        )
        small = whole_of(lines, 2).astype(F32)
        upb = whole_of(up_b, 1).astype(F32)[:, None]
        weights = (small, upb, ups, downs)
    out, act, slope, normed, inv, shaped, masked, *full = forward(
        near, deep, side, lengths, group, frames, weights, hidden, ft, taps, group_count
    )
    if near:
        ups, downs, small, _ = full
        ups, downs = ups.reshape(2, -1, hidden), downs.reshape(2, hidden, -1)
    saved = (act, slope.reshape(act.shape), normed, inv, shaped, masked)
    gs, *parts = backward(near, deep, side, lengths, group, out_grad, saved, ups, downs, small, ft, taps, group_count)
    if near:
        gin, conv_grad, *grads = unpack(gs, parts, clips, taps, group_count, width, wide)
        return (out, gin, conv_grad.transpose(1, 0, 2), *grads)
    gin = unpack(gs, None, clips, taps, group_count, width, wide)
    dup, ddown, lines, ug = parts
    owner = lambda v, axis: lax.psum_scatter(v, axes, scatter_dimension=axis, tiled=True)
    lines = owner(lines, 2)
    return (
        out, gin, lines[:, :taps], lines[:, CONV_BIAS], lines[:, SCALE : SCALE + group_count],
        lines[:, SHIFT : SHIFT + group_count], owner(dup, 1), owner(ug[:, 0], 1), owner(ddown, 1),
        lines[:, DOWN_BIAS], lines[:, GAIN],
    )


def solution(mesh):
    split = ("dp", "fsdp")
    clip = P(split, None, None)
    first, middle, last = P(None, split), P(None, split, None), P(None, None, split)
    in_specs = (clip, P(split), P(split), last, first, last, last, middle, first, middle, first, first, clip)
    out_specs = (clip, clip, last, first, last, last, middle, first, middle, first, first)
    run = functools.partial(body, mesh.shape["dp"], mesh.shape["fsdp"])
    return jax.shard_map(run, mesh=mesh, in_specs=in_specs, out_specs=out_specs, check_vma=False)
```

time: 1740 us -> 190 us (0.11)
  waiting for transfers between devices: 1100 us -> 0 us
  blocking collectives: 311 us -> 0 us
  Pallas kernels: 0 us -> 188 us
  matrix products: 157 us -> 0 us
  other arithmetic: 111 us -> 0 us
  local copies, waits for them, and re-layouts: 50.3 us -> 1.33 us
    unnamed x20 -> x0, waiting for transfers between devices: 676 us -> none
    reduce_scatter x4 -> x0, waiting for transfers between devices: 420 us -> none  [the longest x2 211 us: body(): lax.psum_scatter(terms[4], ('dp', 'fsdp'), scatter_dimension=0, tiled=True)]
    all_gather x6 -> x0, blocking collectives: 231 us -> none  [the longest x2 79 us: body(): lax.all_gather(conv_weight[block_index], ('dp', 'fsdp'), axis=1, tiled=True)]
    pallas_call x0 -> x3, Pallas kernels: none -> 188 us  [the longest x1 100 us: backward(): pl.pallas_call(functools.partial(backward_kernel, near=near, deep=deep, s...]
    dot_general x16 -> x0, matrix products: 152 us -> none  [the longest x2 67.3 us: forward_block(): jnp.dot(shaped_low, up_matrix, preferred_element_type=jnp.float32)]
    reduce_sum x10 -> x0, other arithmetic: 80.3 us -> none  [the longest x2 44.2 us: backward_block(): jnp.sum(grad_mixed * padded[:, offset:offset + frame_count, :], axis=(0, 1))]
    unnamed x2 -> x0, blocking collectives: 79.5 us -> none
    slice x7 -> x0, local copies, waits for them, and re-layouts: 32.1 us -> none  [the longest x2 28.2 us: forward_block(): kernel_taps[offset] * padded[:, offset:offset + frame_count, :]]
  transfers between devices with their start and end apart: 14 -> 0, of which waited for: 10 -> 0; matrix products, arithmetic and copies ran while one was open for 13% -> 0% of each run, Pallas kernels for 0% -> 0%
where the time goes in v1:
time: 190 us
  Pallas kernels  188 us (99%)
    pallas_call x1, Pallas kernels, backward(): pl.pallas_call(functools.partial(backward_kernel, near=near, deep=deep, s...  100 us
    pallas_call x1, Pallas kernels, forward(): pl.pallas_call(functools.partial(forward_kernel, near=near, deep=deep, si...  79.9 us
    pallas_call x1, Pallas kernels, unpack(): pl.pallas_call(unpack_kernel, name='unpack', grid=(fc // ft,), in_specs=[...  7.33 us

profile of v1, /device:TPU:0, one launch (start us, length us, event | category | flops | bytes accessed | tf_op | source)
XLA Modules:
  0.0 189.6 jit_solution(5454880508092944525)
XLA Ops:
  0.6 79.9 %forward.1 = (bf16[8,256,512]{2,1,0:T(8,128)(2,1)}, bf16[2,2048,1536]{2,1,0:T(8,128)(2,1)}, bf16[4096,1536]{1,0:T(8,128)(2,1)}, f32[2,256,8,512]{3,2,1,0:T(8,128...) custom-call(s32[8]{0:T(128)} %refs_0_.3, ...), custom_call_target="tpu_custom_call" | custom-call | tf_op jit(solution)/shard_map/forward/pallas_call | solution.py:600
  80.5 100.4 %backward.1 = (f32[4,2048,128]{2,1,0:T(8,128)}, f32[2,16,1536]{2,1,0:T(8,128)}, f32[2,48,512]{2,1,0:T(8,128)}, f32[40,128]{1,0:T(8,128)}) custom-call(s32[8]{0:T(128)} %refs_0_.3, s32[8]{0:T(128)} %refs_1_.3, bf16[8,256,512]{2,1,0:T(8,128)(2,1)} %refs_2_.3, bf16[2,2048,1536]{2,1,0:T(8,128)(2,1)} %get-tuple-element.36.refs_3_, ...), custom_call_target="tpu_custom_call" | custom-call | tf_op jit(solution)/shard_map/backward/pallas_call | solution.py:1044
  180.9 0.0 copy-start
  180.9 7.3 %unpack.1 = (f32[8,256,512]{2,1,0:T(8,128)}, f32[7,2,16]{2,1,0:T(2,128)}, f32[2,16]{1,0:T(2,128)}, f32[2,2,16]{2,1,0:T(2,128)}, f32[2,2,16]{2,1,0:T(2,128)}, /*i...) custom-call(f32[4,2048,128]{2,1,0:T(8,128)} %get-tuple-element.45.gs, ...), custom_call_target="tpu_custom_call" | custom-call | tf_op jit(solution)/shard_map/unpack/pallas_call | solution.py:1102
  188.3 0.0 copy-done
  188.3 1.3 copy.25
Async XLA Ops:
  180.9 7.3 %copy-start = (bf16[8,256,512]{2,1,0:T(8,128)(2,1)S(1)}, bf16[8,256,512]{2,1,0:T(8,128)(2,1)}, u32[]{:S(2)}) copy-start(bf16[8,256,512]{2,1,0:T(8,128)(2,1)} %get-tuple-element.70) | copy-start | bytes 6291460

commit v2 on v1

--- a/solution.py
+++ b/solution.py
@@ -236,8 +236,8 @@
 class Gather:
     def __init__(self, shards, up_full, down_full, small_full, upb_full, refs, deep, side, group_count, taps):
         (self.pack, self.zbuf, self.first_in, self.first_sum, self.second_in, self.second_sum, self.core_in,
-         self.local_sems, self.out_sems, self.small_s, self.small_r) = refs[:11]
-        sems = refs[11:]
+         self.local_sems, self.small_s, self.small_r) = refs[:10]
+        sems = refs[10:]
         self.place = place = Place(deep, side)
         self.small_full, self.upb_full, self.shards = small_full, upb_full, shards
         self.group_count, self.taps = group_count, taps
@@ -344,13 +344,9 @@
                     at = z * per + q * LANES
                     self.upb_full[b, :, at : at + LANES] = total[z, o + 14 + q : o + 15 + q, :]
 
-    def late(self, i, tiles, up_out, down_out):
-        outs = (up_out, down_out)
-        keep = lambda n: pltpu.make_async_copy(self.full[n % 2].at[n // 2], outs[n % 2].at[n // 2], self.out_sems.at[n])
-
+    def late(self, i, tiles):
         @pl.when(i == 1)
         def _():
-            keep(0).start()
             self.after_z(2)
             self.after_z(3)
 
@@ -362,7 +358,6 @@
         @pl.when(i == tiles)
         def _():
             self.end(1)
-            keep(1).start()
 
         @pl.when(i == 2 * tiles - tiles // 4)
         def _():
@@ -373,24 +368,18 @@
         def _():
             for n in (2, 3):
                 self.end(n)
-                keep(n).start()
-
-        @pl.when(i == 3 * tiles - 1)
-        def _():
-            for n in range(4):
-                keep(n).wait()
 
 
 def gather_scratch(deep, side):
     buf = pltpu.VMEM((deep, 2 * PACK, LANES), F32)
     many = pltpu.VMEM((side - 1, deep, 2 * PACK, LANES), F32)
     n = deep - 1 + 2 * (side - 1) + 1
-    return [pltpu.VMEM((2 * PACK, LANES), F32), buf, many, buf, many, buf, buf, DMA((4,)), DMA((4,)), DMA((n,)), DMA((n,))] + gather_sems(
+    return [pltpu.VMEM((2 * PACK, LANES), F32), buf, many, buf, many, buf, buf, DMA((4,)), DMA((n,)), DMA((n,))] + gather_sems(
         4, deep, side
     )
 
 
-def conv_norm(masked, f0, frames, s8, normed, inv, shaped, taps, step=4):
+def conv_norm(masked, f0, frames, s8, normed, inv, shaped, taps, n0=0, step=4):
     clips, width = s8.shape[1:]
     for j in range(0, frames, step):
         mixed = s8[CONV_BIAS][None]
@@ -399,14 +388,14 @@
         center = mixed - jnp.mean(mixed, axis=-1, keepdims=True)
         inv_std = lax.rsqrt(jnp.mean(center * center, axis=-1, keepdims=True) + EPSILON)
         norm = center * inv_std
-        normed[pl.ds(f0 + j, step)] = norm
+        normed[pl.ds(n0 + f0 + j, step)] = norm
         inv[pl.ds(f0 + j, step)] = jnp.broadcast_to(inv_std, (step, clips, LANES))
         rows = norm * s8[SCALE][None] + s8[SHIFT][None]
         at = pl.multiple_of((f0 + j) * clips, step * clips)
         shaped[pl.ds(at, step * clips), :] = rows.reshape(step * clips, width).astype(BF16)
 
 
-def up_gelu(shaped, up_cols, u8, act, r0, slope, rows, hidden, cols=256, sub=16):
+def up_gelu(shaped, up_cols, u8, act, r0, slope, s0, rows, hidden, cols=256, sub=16):
     left = shaped[pl.ds(r0, rows), :]
     for n in range(0, hidden, cols):
         before = mm(left, up_cols(n, n + cols), NN)
@@ -414,25 +403,13 @@
             piece = before[r : r + sub].reshape(sub // 8, 8, cols) + u8[:, n : n + cols][None]
             a, s = gelu_pair(piece.reshape(sub, cols))
             act[pl.ds(r0 + r, sub), n : n + cols] = a.astype(BF16)
-            slope[r : r + sub, n : n + cols] = s.astype(slope.dtype)
-
-
-def forward_kernel(*refs, near, deep, side, ft, taps, group_count):
-    lens, groups, frames = refs[:3]
-    if near:
-        shards, refs = refs[3:12], refs[12:]
-        (out, act_out, slope, normed_out, inv_out, shaped_out, masked_out, up_out, down_out, small_full, upb_full) = refs[:11]
-        refs = refs[11:]
-    else:
-        small_full, upb_full, up_full, down_full = refs[3:7]
-        (out, act_out, slope, normed_out, inv_out, shaped_out, masked_out) = refs[7:14]
-        refs = refs[14:]
-    (stream, masked0, masked1, normed, inv, shaped, first_rows, act, s8, u8, len8, save_sem, act_sem, row_sem) = refs[:14]
-    refs = refs[14:]
-    if near:
-        up_full, down_full = refs[:2]
-        gather_refs = refs[2:]
-
+            slope[pl.ds(s0 + r, sub), n : n + cols] = s.astype(slope.dtype)
+
+
+def forward_kernel(
+    lens, groups, frames, small_full, upb_full, up_full, down_full, out, act_out, slope, normed_out, inv_out, shaped_out, masked_out,
+    stream, masked0, masked1, normed, inv, shaped, first_rows, act, s8, u8, len8, save_sem, act_sem, row_sem, *, ft, taps, group_count,
+):
     i = pl.program_id(0)
     clips, frame_count, width = frames.shape
     hidden = act.shape[1]
@@ -440,12 +417,7 @@
     rows = ft * clips
 
     def up_cols(b):
-        if near:
-            return lambda lo, hi: up_full[b, :, :, :, :, :, lo:hi].reshape(width, hi - lo)
         return lambda lo, hi: up_full[b, :, lo:hi]
-
-    def down_rows(b):
-        return down_full[b].reshape(hidden, width)
 
     body = pl.ds(HALO, frame_count)
     save = lambda n, src, dst: pltpu.make_async_copy(src, dst, save_sem.at[n])
@@ -467,8 +439,15 @@
             pltpu.make_async_copy(shaped.at[r], shaped_out.at[1, r], row_sem.at[2, j]),
         ]
 
-    def spread():
-        def one(n, carry):
+    @pl.when(i == 0)
+    def _():
+        zeros = jnp.zeros((HALO, clips, width), F32)
+        for m in (masked0, masked1):
+            m[0:HALO] = zeros
+            m[HALO + frame_count :] = zeros
+        len8[...] = per_clip(lens, clips, width)
+
+        def spread(n, carry):
             t0 = pl.multiple_of(n * 16, 16)
             spread_clips(frames, t0, stream, 0, 16)
             v = rows_of(stream, 0, 16 * clips)
@@ -476,45 +455,22 @@
             first_rows[pl.ds(at, 16 * clips), :] = v.astype(BF16)
             masked0[pl.ds(HALO + t0, 16)] = keep_frames(v.reshape(16, clips, width), t0, len8)
             return carry
-        lax.fori_loop(0, frame_count // 16, one, 0)
-
-    def conv0(lo, hi):
-        def one(n, carry):
+        lax.fori_loop(0, frame_count // 16, spread, 0)
+        for b in range(2):
+            prepare(small_full.at[b], lens, groups, s8.at[b], len8, group_count)
+            u8[b] = jnp.broadcast_to(upb_full[b, 0:1, :], u8.shape[1:])
+
+        def conv0(n, carry):
             conv_norm(masked0, n * ft, ft, s8.at[0], normed, inv, shaped, taps)
             return carry
-        lax.fori_loop(lo, hi, one, 0)
-
-    @pl.when(i == 0)
-    def _():
-        zeros = jnp.zeros((HALO, clips, width), F32)
-        for m in (masked0, masked1):
-            m[0:HALO] = zeros
-            m[HALO + frame_count :] = zeros
-        len8[...] = per_clip(lens, clips, width)
-
-        def ready():
-            for b in range(2):
-                prepare(small_full.at[b], lens, groups, s8.at[b], len8, group_count)
-                u8[b] = jnp.broadcast_to(upb_full[b, 0:1, :], u8.shape[1:])
-
-        if near:
-            Gather(shards, up_full, down_full, small_full, upb_full, gather_refs, deep, side, group_count, taps).early(
-                spread, ready, conv0, tiles)
-        else:
-            spread()
-            ready()
-            conv0(0, tiles)
+        lax.fori_loop(0, tiles, conv0, 0)
         for c in saves0:
             c.start()
 
-    if near:
-        Gather(shards, up_full, down_full, small_full, upb_full, gather_refs, deep, side, group_count, taps).late(
-            i, tiles, up_out, down_out)
-
     @pl.when(i < tiles)
     def _():
         r0 = pl.multiple_of(i * rows, rows)
-        up_gelu(shaped, up_cols(0), u8.at[0], act, r0, slope, rows, hidden)
+        up_gelu(shaped, up_cols(0), u8.at[0], act, r0, slope, 0, rows, hidden)
         tail(0, i).start()
 
     @pl.when((i >= tiles) & (i < 2 * tiles))
@@ -522,7 +478,7 @@
         j = i - tiles
         f0 = j * ft
         r0 = pl.multiple_of(j * rows, rows)
-        branch = mm(act[pl.ds(r0, rows), :], down_rows(0), NN)
+        branch = mm(act[pl.ds(r0, rows), :], down_full[0], NN)
         for t in range(0, ft, 4):
             b = branch[t * clips : (t + 4) * clips].reshape(4, clips, width) + s8[0, DOWN_BIAS][None]
             total = masked0[pl.ds(HALO + f0 + t, 4)] + s8[0, GAIN][None] * b
@@ -543,16 +499,10 @@
         conv_norm(masked1, f0, ft, s8.at[1], normed, inv, shaped, taps)
         for c in row_saves(j):
             c.start()
-        up_gelu(shaped, up_cols(1), u8.at[1], act, r0, slope, rows, hidden)
+        up_gelu(shaped, up_cols(1), u8.at[1], act, r0, slope, 0, rows, hidden)
         tail(1, j).start()
-        branch = mm(act[pl.ds(r0, rows), :], down_rows(1), NN)
-        for t in range(0, ft, 4):
-            b = branch[t * clips : (t + 4) * clips].reshape(4, clips, width) + s8[1, DOWN_BIAS][None]
-            total = masked1[pl.ds(HALO + f0 + t, 4)] + s8[1, GAIN][None] * b
-            at = pl.multiple_of(r0 + t * clips, 4 * clips)
-            first = first_rows[pl.ds(at, 4 * clips), :].astype(F32).reshape(4, clips, width)
-            put_rows(stream, t * clips, keep_frames(total, f0 + t, len8, first).reshape(4 * clips, width))
-        collect_clips(stream, out, ft)
+        branch = mm(act[pl.ds(r0, rows), :], down_full[1], NN)
+        last_block(branch, masked1, f0, r0, ft, s8.at[1], len8, first_rows, stream, out)
 
     @pl.when(i == 3 * tiles - 1)
     def _():
@@ -563,117 +513,94 @@
                 c.wait()
 
 
-def forward(near, deep, side, lens, groups, frames, weights, hidden, ft, taps, group_count):
+def last_block(branch, masked1, f0, r0, ft, s8, len8, first_rows, stream, out):
+    clips, width = len8.shape
+    for t in range(0, ft, 4):
+        b = branch[t * clips : (t + 4) * clips].reshape(4, clips, width) + s8[DOWN_BIAS][None]
+        total = masked1[pl.ds(HALO + f0 + t, 4)] + s8[GAIN][None] * b
+        at = pl.multiple_of(r0 + t * clips, 4 * clips)
+        first = first_rows[pl.ds(at, 4 * clips), :].astype(F32).reshape(4, clips, width)
+        put_rows(stream, t * clips, keep_frames(total, f0 + t, len8, first).reshape(4 * clips, width))
+    collect_clips(stream, out, ft)
+
+
+def forward(lens, groups, frames, weights, hidden, ft, taps, group_count):
     clips, fc, d = frames.shape
     h = hidden
     n, r = fc // ft, ft * clips
     R = fc * clips
     slope_at = lambda i: jnp.where(i < n, i, jnp.where(i < 2 * n, n - 1, i - n))
-    out_specs = [
-        pl.BlockSpec((clips, ft, d), lambda i: (0, jnp.maximum(i - 2 * n, 0), 0)), hbm(),
-        pl.BlockSpec((r, h), lambda i: (slope_at(i), 0)), hbm(), hbm(), hbm(), hbm(),
-    ]
-    out_shape = [
-        shape((clips, fc, d), BF16), shape((2, R, h), BF16), shape((2 * R, h), BF16), shape((2, fc, clips, d)),
-        shape((2, fc, clips, LANES)), shape((2, R, d), BF16), shape((2, fc, clips, d)),
-    ]
-    scratch = [
-        pltpu.VMEM((d // LANES, max(r, 16 * clips), LANES), F32),
-        pltpu.VMEM((fc + 2 * HALO, clips, d), F32), pltpu.VMEM((fc + 2 * HALO, clips, d), F32),
-        pltpu.VMEM((fc, clips, d), F32), pltpu.VMEM((fc, clips, LANES), F32), pltpu.VMEM((R, d), BF16),
-        pltpu.VMEM((R, d), BF16), pltpu.VMEM((R, h), BF16),
-        pltpu.VMEM((2, 14, clips, d), F32), pltpu.VMEM((2, clips, h), F32), pltpu.VMEM((clips, d), jnp.int32),
-        DMA((5,)), DMA((n,)), DMA((3, n)),
-    ]
-    params = dict(vmem_limit_bytes=VMEM_LIMIT)
-    if near:
-        urows, drows = weights[4].shape[1], weights[6].shape[1]
-        dims = (2, deep, side, side, 2)
-        full = [dims + (urows, h), dims + (drows, d)]
-        in_specs = [smem(), smem(), whole(clips, fc, d)] + [vmem()] * 9
-        out_specs += [hbm(), hbm(), vmem(), vmem()]
-        out_shape += [shape(full[0], BF16), shape(full[1], BF16), shape((2, ROWS, d)), shape((2, 1, h))]
-        scratch += [pltpu.VMEM(f, BF16) for f in full] + gather_scratch(deep, side)
-        params.update(collective_id=0, has_side_effects=True)
-    else:
-        in_specs = [smem(), smem(), whole(clips, fc, d)] + [vmem()] * 4
     return pl.pallas_call(
-        functools.partial(forward_kernel, near=near, deep=deep, side=side, ft=ft, taps=taps, group_count=group_count),
+        functools.partial(forward_kernel, ft=ft, taps=taps, group_count=group_count),
         name="forward",
         grid=(3 * n,),
-        in_specs=in_specs,
-        out_specs=out_specs,
-        out_shape=out_shape,
-        scratch_shapes=scratch,
-        compiler_params=pltpu.CompilerParams(**params),
+        in_specs=[smem(), smem(), whole(clips, fc, d)] + [vmem()] * 4,
+        out_specs=[
+            pl.BlockSpec((clips, ft, d), lambda i: (0, jnp.maximum(i - 2 * n, 0), 0)), hbm(),
+            pl.BlockSpec((r, h), lambda i: (slope_at(i), 0)), hbm(), hbm(), hbm(), hbm(),
+        ],
+        out_shape=[
+            shape((clips, fc, d), BF16), shape((2, R, h), BF16), shape((2 * R, h), BF16), shape((2, fc, clips, d)),
+            shape((2, fc, clips, LANES)), shape((2, R, d), BF16), shape((2, fc, clips, d)),
+        ],
+        scratch_shapes=[
+            pltpu.VMEM((d // LANES, max(r, 16 * clips), LANES), F32),
+            pltpu.VMEM((fc + 2 * HALO, clips, d), F32), pltpu.VMEM((fc + 2 * HALO, clips, d), F32),
+            pltpu.VMEM((fc, clips, d), F32), pltpu.VMEM((fc, clips, LANES), F32), pltpu.VMEM((R, d), BF16),
+            pltpu.VMEM((R, d), BF16), pltpu.VMEM((R, h), BF16),
+            pltpu.VMEM((2, 14, clips, d), F32), pltpu.VMEM((2, clips, h), F32), pltpu.VMEM((clips, d), jnp.int32),
+            DMA((5,)), DMA((n,)), DMA((3, n)),
+        ],
+        compiler_params=pltpu.CompilerParams(vmem_limit_bytes=VMEM_LIMIT),
     )(lens, groups, frames, *weights)
 
 
 class Scatter:
     def __init__(self, place, term, bufs, sems):
         self.place, self.term = place, term
-        self.core_out, self.core_in, self.second_in, self.first_in, self.z_in = bufs
+        self.core_in, self.second_in, self.first_in, self.z_in = bufs
         self.sems = sems
 
-    def entry(self, z, first, second):
+    def line(self, first, second):
         high, low = self.place.chip_of(first, second)
-        return (z * self.place.side + high) * self.place.side + low
-
-    def own(self, e, core):
-        rows = self.core_in.shape[1]
-        return self.term[pl.ds(pl.multiple_of((e * 2 + core) * rows, 8), rows), :]
-
-    def fill(self, count, write):
-        def one(n, carry):
-            write(n)
-            return carry
-        lax.fori_loop(0, count, one, 0)
-
-
-    def second_at(self, p):
-        return (p - 1) * self.place.side * self.place.deep
-
-    def first_at(self, p):
-        return self.second_at(self.place.side) + (p - 1) * self.place.deep
-
-    def z_at(self, p):
-        return self.first_at(self.place.side) + p - 1
+        return self.term.at[:, high, low, self.place.core]
+
+    def spot(self, z, first, second):
+        high, low = self.place.chip_of(first, second)
+        return (z, high, low)
 
     def core_copies(self):
-        return [send(self.core_out, self.core_in, self.sems[0].at[0], self.sems[1].at[0], self.place.core_peer())]
-
-    def second_copies(self):
+        at = self.place
+        return [send(self.term.at[:, :, :, 1 - at.core], self.core_in, self.sems[0].at[0], self.sems[1].at[0], at.core_peer())]
+
+    def second_copies(self, p):
+        at = self.place
+        to = lax.rem(at.second + p, at.side)
+        n = (p - 1) * at.side
         return [
-            send(self.core_out.at[pl.ds(self.second_at(p), self.place.side * self.place.deep)], self.second_in.at[p - 1], self.sems[2].at[p - 1], self.sems[3].at[p - 1], self.place.second_peer(p))
-            for p in range(1, self.place.side)
+            send(self.line(f, to), self.second_in.at[p - 1, f], self.sems[2].at[n + f], self.sems[3].at[n + f], at.second_peer(p))
+            for f in range(at.side)
         ]
 
-    def first_copies(self):
-        return [
-            send(self.core_out.at[pl.ds(self.first_at(p), self.place.deep)], self.first_in.at[p - 1], self.sems[4].at[p - 1], self.sems[5].at[p - 1], self.place.first_peer(p))
-            for p in range(1, self.place.side)
-        ]
-
-    def z_copies(self):
-        return [
-            send(self.core_out.at[self.z_at(p)], self.z_in.at[p - 1], self.sems[6].at[p - 1], self.sems[7].at[p - 1], self.place.z_peer(p))
-            for p in range(1, self.place.deep)
-        ]
-
-    def core_start(self):
-        def write(n):
-            self.core_out[n] = self.own(n, 1 - self.place.core).astype(BF16)
-        self.fill(self.core_out.shape[0], write)
-        run(self.core_copies())
+    def first_copy(self, p):
+        at = self.place
+        to = lax.rem(at.first + p, at.side)
+        return send(self.line(to, at.second), self.first_in.at[p - 1], self.sems[4].at[p - 1], self.sems[5].at[p - 1], at.first_peer(p))
+
+    def z_copy(self, p):
+        at = self.place
+        to = lax.rem(at.z + p, at.deep)
+        high, low = at.chip_of(at.first, at.second)
+        return send(self.term.at[to, high, low, at.core], self.z_in.at[p - 1], self.sems[6].at[p - 1], self.sems[7].at[p - 1], at.z_peer(p))
 
     def part1(self, z, first, second):
-        e = self.entry(z, first, second)
-        return self.own(e, self.place.core) + self.core_in[e].astype(F32)
+        z, high, low = self.spot(z, first, second)
+        return self.term[z, high, low, self.place.core].astype(F32) + self.core_in[z, high, low].astype(F32)
 
     def part2(self, z, first):
         total = self.part1(z, first, self.place.second)
         for p in range(1, self.place.side):
-            total = total + self.second_in[p - 1, first * self.place.deep + z].astype(F32)
+            total = total + self.second_in[p - 1, first, z].astype(F32)
         return total
 
     def part3(self, z):
@@ -682,53 +609,62 @@
             total = total + self.first_in[p - 1, z].astype(F32)
         return total
 
+    def put(self, z, first, second, total):
+        z, high, low = self.spot(z, first, second)
+        self.term[z, high, low, self.place.core] = total.astype(BF16)
+
+    def core_start(self):
+        run(self.core_copies())
+
     def second_start(self):
         at = self.place
         done(self.core_copies())
-        copies = self.second_copies()
         for p in range(1, at.side):
             to = lax.rem(at.second + p, at.side)
-            def write(n):
-                first, z = n // at.deep, lax.rem(n, at.deep)
-                self.core_out[self.second_at(p) + n] = self.part1(z, first, to).astype(BF16)
-            self.fill(at.side * at.deep, write)
-            copies[p - 1].start()
+            copies = self.second_copies(p)
+            for first in range(at.side):
+                def one(z, carry):
+                    self.put(z, first, to, self.part1(z, first, to))
+                    return carry
+                lax.fori_loop(0, at.deep, one, 0)
+                copies[first].start()
 
     def first_start(self):
         at = self.place
-        done(self.second_copies())
-        copies = self.first_copies()
+        for p in range(1, at.side):
+            done(self.second_copies(p))
         for p in range(1, at.side):
             to = lax.rem(at.first + p, at.side)
-            def write(z):
-                self.core_out[self.first_at(p) + z] = self.part2(z, to).astype(BF16)
-            self.fill(at.deep, write)
-            copies[p - 1].start()
+            def one(z, carry):
+                self.put(z, to, at.second, self.part2(z, to))
+                return carry
+            lax.fori_loop(0, at.deep, one, 0)
+            self.first_copy(p).start()
 
     def z_start(self):
         at = self.place
-        done(self.first_copies())
-        copies = self.z_copies()
+        done([self.first_copy(p) for p in range(1, at.side)])
         for p in range(1, at.deep):
-            self.core_out[self.z_at(p)] = self.part3(lax.rem(at.z + p, at.deep)).astype(BF16)
-            copies[p - 1].start()
+            to = lax.rem(at.z + p, at.deep)
+            self.put(to, at.first, at.second, self.part3(to))
+            self.z_copy(p).start()
 
     def finish(self, out):
-        done(self.z_copies())
-        total = self.part3(self.place.z)
-        for p in range(1, self.place.deep):
+        at = self.place
+        done([self.z_copy(p) for p in range(1, at.deep)])
+        total = self.part3(at.z)
+        for p in range(1, at.deep):
             total = total + self.z_in[p - 1].astype(F32)
         out[...] = total
 
 
 def scatter_bufs(deep, side, rows, cols):
     v = lambda *lead: pltpu.VMEM(lead + (rows, cols), BF16)
-    e = deep * side * side
-    return [v(e), v(e), v(side - 1, side * deep), v(side - 1, deep), v(deep - 1)]
+    return [v(deep, side, side), v(side - 1, side, deep), v(side - 1, deep), v(deep - 1)]
 
 
 def scatter_sems(count, deep, side):
-    return [DMA((count, n)) for n in (1, 1, side - 1, side - 1, side - 1, side - 1, deep - 1, deep - 1)]
+    return [DMA((count, n)) for n in (1, 1, side * (side - 1), side * (side - 1), side - 1, side - 1, deep - 1, deep - 1)]
 
 
 def pack_small(small, upb, b, terms, deep):
@@ -794,7 +730,7 @@
         for n, (b, term, out) in enumerate(
             ((1, ddown, down_part), (1, dup, up_part), (0, ddown, down_part), (0, dup, up_part))
         ):
-            job = Scatter(self.place, term.at[b], refs[5 * n : 5 * n + 5], [s.at[n] for s in sems])
+            job = Scatter(self.place, term.at[b], refs[4 * n : 4 * n + 4], [s.at[n] for s in sems])
             self.jobs.setdefault(b, []).append((job, out.at[b]))
 
     def each(self, b, what):
@@ -805,10 +741,6 @@
                 getattr(job, what)()
 
     def before(self, i, span, parts, tiles):
-        @pl.when(i == 0)
-        def _():
-            self.place.greet()
-
         plan = [
             (parts, 1, "core_start"), (parts + 3, 1, "second_start"), (span, 1, "first_start"),
             (span + 3, 1, "z_start"), (span + parts - 1, 1, "finish"),
@@ -839,33 +771,33 @@
     return small_bufs(deep, side) + db + ub + db + ub + scatter_sems(4, deep, side)
 
 
-def norm_back(gs, normed, inv, s8, gm, gm0, acc, frames, step=4):
+def norm_back(gs, normed, n0, inv, i0, s8, gm, gm0, acc, frames, step=4):
     clips, width = s8.shape[1:]
     a_scale, a_shift, a_bias = acc[A_SCALE], acc[A_SHIFT], acc[A_BIAS]
     for j in range(0, frames, step):
         g = gs[j * clips : (j + step) * clips].reshape(step, clips, width)
-        norm = normed[j : j + step]
+        norm = normed[pl.ds(n0 + j, step)]
         gn = g * norm
         a_scale = a_scale + fold(gn)
         a_shift = a_shift + fold(g)
         gg = g * s8[SCALE][None]
         mean = jnp.mean(gg, axis=-1, keepdims=True)
         mean_norm = jnp.mean(gn * s8[SCALE][None], axis=-1, keepdims=True)
-        inv_std = jnp.concatenate([inv[j : j + step]] * (width // LANES), axis=-1)
+        inv_std = jnp.concatenate([inv[pl.ds(i0 + j, step)]] * (width // LANES), axis=-1)
         grad = inv_std * (gg - mean - norm * mean_norm)
         a_bias = a_bias + fold(grad)
         gm[pl.ds(gm0 + j, step)] = grad
     acc[A_SCALE], acc[A_SHIFT], acc[A_BIAS] = a_scale, a_shift, a_bias
 
 
-def conv_back(gm, gm0, s8, masked, gs, t0, out, acc, frames, len8, taps, step=8):
+def conv_back(gm, gm0, s8, masked, m0, gs, g0, t0, out, acc, frames, len8, taps, step=8):
     clips, width = len8.shape
     half = taps // 2
     for l in range(width // LANES):
         cols = slice(l * LANES, (l + 1) * LANES)
         sums = [acc[A_TAPS + k, :, cols] for k in range(taps)]
         for j in range(0, frames, step):
-            here = masked[j : j + step, :, cols]
+            here = masked[pl.ds(m0 + j, step), :, cols]
             total = None
             for k in range(taps):
                 piece = gm[pl.ds(gm0 + j + half - k, step), :, cols]
@@ -874,8 +806,8 @@
                 sums[k] = sums[k] + fold(piece * here)
             t = lax.broadcasted_iota(jnp.int32, total.shape, 0) + (t0 + j)
             total = jnp.where(t < len8[:, cols][None], total, 0.0)
-            total = gs[pl.ds(t0 + j, step), :, cols] + total
-            gs[pl.ds(t0 + j, step), :, cols] = total
+            total = gs[pl.ds(g0 + j, step), :, cols] + total
+            gs[pl.ds(g0 + j, step), :, cols] = total
             out[l, j * clips : (j + step) * clips, :] = total.reshape(step * clips, LANES)
         for k in range(taps):
             acc[A_TAPS + k, :, cols] = sums[k]
@@ -899,19 +831,10 @@
     upb_grad[...] = line(upb_acc[...])
 
 
-def backward_kernel(*refs, near, deep, side, ft, tiles, parts, taps, group_count):
-    lens, groups, og, act, slope, normed, inv, shaped, masked, up, down, small = refs[:12]
-    refs = refs[12:]
-    if near:
-        gs_out, up_part, down_part, small_part = refs[:4]
-        dup, ddown, small_grad, upb_grad = refs[4:8]
-        refs = refs[8:]
-    else:
-        gs_out, dup, ddown, small_grad, upb_grad = refs[:5]
-        refs = refs[5:]
-    gs, gb, gbef, gm, lanes, s8, len8, acc, upb_acc = refs[:9]
-    refs = refs[9:]
-
+def backward_kernel(
+    lens, groups, og, act, slope, normed, inv, shaped, masked, up, down, small, gs_out, dup, ddown, small_grad, upb_grad,
+    gs, gb, gbef, gm, lanes, s8, len8, acc, upb_acc, *, ft, tiles, parts, taps, group_count,
+):
     i = pl.program_id(0)
     frame_count, clips, width = gs.shape
     hidden = gbef.shape[1]
@@ -932,45 +855,21 @@
     def _():
         gm[pl.ds(0, base)] = jnp.zeros((base, clips, width), F32)
         gm[pl.ds(base + frame_count, HALO)] = jnp.zeros((HALO, clips, width), F32)
-
-        def one(n, carry):
-            t0 = pl.multiple_of(n * 16, 16)
-            spread_clips(og, t0, lanes, 0, 16)
-            gs[pl.ds(t0, 16)] = rows_of(lanes, 0, 16 * clips).reshape(16, clips, width)
-            return carry
-        lax.fori_loop(0, frame_count // 16, one, 0)
+        spread_grad(og, lanes, gs, 0)
 
     @pl.when(step == 0)
     def _():
-        def one(n, a_down):
-            t0 = n * 4
-            gvb = s8[GAIN][None] * keep_frames(gs[pl.ds(t0, 4)], t0, len8)
-            at = pl.multiple_of(t0 * clips, 4 * clips)
-            gb[pl.ds(at, 4 * clips), :] = gvb.reshape(4 * clips, width).astype(BF16)
-            return a_down + fold(gvb)
-        acc[A_DOWN] = lax.fori_loop(0, frame_count // 4, one, jnp.zeros((clips, width), F32), unroll=4)
-
-    if near:
-        sums = Sums(refs, dup, ddown, up_part, down_part, small_part, small_grad, upb_grad, deep, side)
-        sums.before(i, span, parts, tiles)
+        acc[A_DOWN] = branch_grad(gs, 0, s8, len8, gb)
 
     @pl.when(step < parts)
     def _():
         c0 = pl.multiple_of(step * cols, cols)
         at = pl.ds(c0, cols)
-        grads = gb[...]
         lower = down[0, at, :]
-        term = mm(act[0], grads, TN)
+        term = mm(act[0], gb[...], TN)
         ddown[b, at, :] = term
         acc[A_GAIN] += fold((term * lower.astype(F32)).reshape(cols // 8, 8, width))
-        ga = mm(grads, lower, NT)
-        total = jnp.zeros((8, cols), F32)
-        sub = 16
-        for r in range(0, total_rows, sub):
-            gr = ga[r : r + sub] * slope[0, r : r + sub, :].astype(F32)
-            total = total + fold(gr.reshape(sub // 8, 8, cols))
-            gbef[r : r + sub, at] = gr.astype(BF16)
-        upb_acc[:, at] = total
+        before_grad(gb, lower, slope.at[0], slice(None), gbef, at, upb_acc, total_rows)
         dup[b, :, at] = mm(shaped[0], gbef[:, at], TN)
 
     j = step - parts
@@ -979,21 +878,54 @@
     def _():
         r0 = pl.multiple_of(j * rows, rows)
         grad = mm(gbef[pl.ds(r0, rows), :], up[0], NT)
-        norm_back(grad, normed.at[0], inv.at[0], s8, gm, base + j * ft, acc, ft)
+        norm_back(grad, normed.at[0], 0, inv.at[0], 0, s8, gm, base + j * ft, acc, ft)
 
     @pl.when(j >= 2)
     def _():
-        conv_back(gm, base + (j - 2) * ft, s8, masked.at[0], gs, (j - 2) * ft, gs_out, acc, ft, len8, taps)
+        f0 = (j - 2) * ft
+        conv_back(gm, base + f0, s8, masked.at[0], 0, gs, f0, f0, gs_out, acc, ft, len8, taps)
 
     @pl.when(step == span - 1)
     def _():
         finish_small(acc, upb_acc, groups, s8, small_grad.at[b], upb_grad.at[b], group_count)
 
-    if near:
-        sums.after(i, span)
-
-
-def backward(near, deep, side, lens, groups, og, saved, ups, downs, small, ft, taps, group_count):
+
+def spread_grad(og, lanes, gs, g0):
+    clips, frame_count, width = og.shape
+
+    def one(n, carry):
+        t0 = pl.multiple_of(n * 16, 16)
+        spread_clips(og, t0, lanes, 0, 16)
+        gs[pl.ds(g0 + t0, 16)] = rows_of(lanes, 0, 16 * clips).reshape(16, clips, width)
+        return carry
+    lax.fori_loop(0, frame_count // 16, one, 0)
+
+
+def branch_grad(gs, g0, s8, len8, gb):
+    clips, width = len8.shape
+    frame_count = gb.shape[0] // clips
+
+    def one(n, a_down):
+        t0 = n * 4
+        gvb = s8[GAIN][None] * keep_frames(gs[pl.ds(g0 + t0, 4)], t0, len8)
+        at = pl.multiple_of(t0 * clips, 4 * clips)
+        gb[pl.ds(at, 4 * clips), :] = gvb.reshape(4 * clips, width).astype(BF16)
+        return a_down + fold(gvb)
+    return lax.fori_loop(0, frame_count // 4, one, jnp.zeros((clips, width), F32), unroll=4)
+
+
+def before_grad(gb, lower, slope, slope_cols, gbef, at, upb_acc, rows, sub=16):
+    cols = lower.shape[0]
+    ga = mm(gb[...], lower, NT)
+    total = jnp.zeros((8, cols), F32)
+    for r in range(0, rows, sub):
+        gr = ga[r : r + sub] * slope[r : r + sub, slope_cols].astype(F32)
+        total = total + fold(gr.reshape(sub // 8, 8, cols))
+        gbef[r : r + sub, at] = gr.astype(BF16)
+    upb_acc[:, at] = total
+
+
+def backward(lens, groups, og, saved, ups, downs, small, ft, taps, group_count):
     act, slope, normed, inv, shaped, masked = saved
     clips, fc, d = og.shape
     h = ups.shape[2]
@@ -1006,51 +938,260 @@
     tile = lambda i: jnp.clip(lax.rem(i, span) - parts, 0, n - 1)
     late = lambda i: jnp.clip(lax.rem(i, span) - parts - 2, 0, n - 1)
     last = lambda i: jnp.clip(i - span - parts - 2, 0, n - 1)
-    in_specs = [
-        smem(), smem(), whole(clips, fc, d),
-        pl.BlockSpec((1, R, cols), lambda i: (block(i), 0, part(i))),
-        pl.BlockSpec((1, R, cols), lambda i: (block(i), 0, part(i))),
-        pl.BlockSpec((1, ft, clips, d), lambda i: (block(i), tile(i), 0, 0)),
-        pl.BlockSpec((1, ft, clips, LANES), lambda i: (block(i), tile(i), 0, 0)),
-        pl.BlockSpec((1, R, d), lambda i: (block(i), 0, 0), pipeline_mode=pl.Buffered(1)),
-        pl.BlockSpec((1, ft, clips, d), lambda i: (block(i), late(i), 0, 0)),
-        pl.BlockSpec((1, d, h), lambda i: (block(i), 0, 0)),
-        pl.BlockSpec((1, h, d), lambda i: (block(i), 0, 0)),
-        whole(2, ROWS, d),
-    ]
-    out_specs = [pl.BlockSpec((d // LANES, r, LANES), lambda i: (0, last(i), 0))]
-    out_shape = [shape((d // LANES, R, LANES))]
     sums = [(2, d, h), (2, h, d), (2, ROWS, d), (2, 1, h)]
-    scratch = []
-    params = dict(vmem_limit_bytes=VMEM_LIMIT)
-    if near:
-        e = deep * side * side * 2
-        urows, drows = d // e, h // e
-        out_specs += [vmem()] * 3
-        out_shape += [shape((2, urows, h)), shape((2, drows, d)), shape((2 * PACK, LANES))]
-        scratch += [pltpu.VMEM(v, F32) for v in sums]
-        params.update(collective_id=1, has_side_effects=True)
-    else:
-        out_specs += [whole(*v) for v in sums]
-        out_shape += [shape(v) for v in sums]
-    scratch += [
-        pltpu.VMEM((fc, clips, d), F32), pltpu.VMEM((R, d), BF16), pltpu.VMEM((R, h), BF16),
-        pltpu.VMEM((fc + 2 * ft + HALO, clips, d), F32), pltpu.VMEM((d // LANES, 16 * clips, LANES), F32),
-        pltpu.VMEM((14, clips, d), F32), pltpu.VMEM((clips, d), jnp.int32),
-        pltpu.VMEM((12, clips, d), F32), pltpu.VMEM((clips, h), F32),
-    ]
-    if near:
-        scratch += sums_scratch(deep, side, urows, drows, d, h)
     return pl.pallas_call(
-        functools.partial(backward_kernel, near=near, deep=deep, side=side, ft=ft, tiles=n, parts=parts, taps=taps, group_count=group_count),
+        functools.partial(backward_kernel, ft=ft, tiles=n, parts=parts, taps=taps, group_count=group_count),
         name="backward",
         grid=(2 * span,),
-        in_specs=in_specs,
-        out_specs=out_specs,
-        out_shape=out_shape,
-        scratch_shapes=scratch,
-        compiler_params=pltpu.CompilerParams(**params),
+        in_specs=[
+            smem(), smem(), whole(clips, fc, d),
+            pl.BlockSpec((1, R, cols), lambda i: (block(i), 0, part(i))),
+            pl.BlockSpec((1, R, cols), lambda i: (block(i), 0, part(i))),
+            pl.BlockSpec((1, ft, clips, d), lambda i: (block(i), tile(i), 0, 0)),
+            pl.BlockSpec((1, ft, clips, LANES), lambda i: (block(i), tile(i), 0, 0)),
+            pl.BlockSpec((1, R, d), lambda i: (block(i), 0, 0), pipeline_mode=pl.Buffered(1)),
+            pl.BlockSpec((1, ft, clips, d), lambda i: (block(i), late(i), 0, 0)),
+            pl.BlockSpec((1, d, h), lambda i: (block(i), 0, 0)),
+            pl.BlockSpec((1, h, d), lambda i: (block(i), 0, 0)),
+            whole(2, ROWS, d),
+        ],
+        out_specs=[pl.BlockSpec((d // LANES, r, LANES), lambda i: (0, last(i), 0))] + [whole(*v) for v in sums],
+        out_shape=[shape((d // LANES, R, LANES))] + [shape(v) for v in sums],
+        scratch_shapes=[
+            pltpu.VMEM((fc, clips, d), F32), pltpu.VMEM((R, d), BF16), pltpu.VMEM((R, h), BF16),
+            pltpu.VMEM((fc + 2 * ft + HALO, clips, d), F32), pltpu.VMEM((d // LANES, 16 * clips, LANES), F32),
+            pltpu.VMEM((14, clips, d), F32), pltpu.VMEM((clips, d), jnp.int32),
+            pltpu.VMEM((12, clips, d), F32), pltpu.VMEM((clips, h), F32),
+        ],
+        compiler_params=pltpu.CompilerParams(vmem_limit_bytes=VMEM_LIMIT),
     )(lens, groups, og, act, slope, normed, inv, shaped, masked, ups, downs, small)
+
+
+def step_kernel(*refs, deep, side, ft, parts, taps, group_count):
+    lens, groups, frames, og = refs[:4]
+    shards = refs[4:13]
+    out, gs_out, up_part, down_part, small_part, act_far, slope_far = refs[13:20]
+    (io, stream, masked0, masked1, normed, inv, shaped, first_rows, act, slope, gb, s8, u8, len8, acc, upb_acc) = refs[20:36]
+    small_full, upb_full, small_grad, upb_grad, up_full, down_full, up_term, down_term = refs[36:44]
+    io_sem, act_sem, slope_sem, act_back_sem, slope_back_sem = refs[44:49]
+    gather_refs, sum_refs = refs[49:67], refs[67:]
+
+    i = pl.program_id(0)
+    clips, frame_count, width = io.shape
+    hidden = act.shape[1]
+    tiles = frame_count // ft
+    rows = ft * clips
+    cols = hidden // parts
+    span = parts + tiles + 1
+    body = pl.ds(HALO, frame_count)
+
+    load = lambda n, src: pltpu.make_async_copy(src, io, io_sem.at[n])
+    tile_rows = lambda j: pl.ds(pl.multiple_of(j * rows, rows), rows)
+    part_at = lambda p: pl.ds(pl.multiple_of(p * cols, cols), cols)
+
+    def spills(j):
+        r = tile_rows(j)
+        return [
+            pltpu.make_async_copy(act.at[r], act_far.at[r], act_sem.at[j]),
+            pltpu.make_async_copy(slope.at[r], slope_far.at[r], slope_sem.at[j]),
+        ]
+
+    def act_back(p):
+        return pltpu.make_async_copy(act_far.at[:, part_at(p)], act.at[:, part_at(p)], act_back_sem.at[p])
+
+    def slope_back(j):
+        return pltpu.make_async_copy(slope_far.at[tile_rows(j)], slope.at[tile_rows(j)], slope_back_sem.at[j])
+
+    def up_cols(b):
+        return lambda lo, hi: up_full[b, :, :, :, :, :, lo:hi].reshape(width, hi - lo)
+
+    def spread():
+        load(0, frames).wait()
+
+        def one(n, carry):
+            t0 = pl.multiple_of(n * 16, 16)
+            spread_clips(io, t0, stream, 0, 16)
+            v = rows_of(stream, 0, 16 * clips)
+            at = pl.multiple_of(t0 * clips, 16 * clips)
+            first_rows[pl.ds(at, 16 * clips), :] = v.astype(BF16)
+            masked0[pl.ds(HALO + t0, 16)] = keep_frames(v.reshape(16, clips, width), t0, len8)
+            return carry
+        lax.fori_loop(0, frame_count // 16, one, 0)
+        load(1, og).start()
+
+    def conv0(lo, hi):
+        def one(n, carry):
+            conv_norm(masked0, n * ft, ft, s8.at[0], normed.at[0], inv.at[0], shaped, taps, HALO)
+            return carry
+        lax.fori_loop(lo, hi, one, 0)
+
+    def ready():
+        for b in range(2):
+            prepare(small_full.at[b], lens, groups, s8.at[b], len8, group_count)
+            u8[b] = jnp.broadcast_to(upb_full[b, 0:1, :], u8.shape[1:])
+
+    @pl.when(i == 0)
+    def _():
+        load(0, frames).start()
+        zeros = jnp.zeros((HALO, clips, width), F32)
+        for m in (masked0, masked1, normed.at[0], normed.at[1]):
+            m[0:HALO] = zeros
+            m[HALO + frame_count : HALO + frame_count + HALO] = zeros
+        len8[...] = per_clip(lens, clips, width)
+        Gather(shards, up_full, down_full, small_full, upb_full, gather_refs, deep, side, group_count, taps).early(
+            spread, ready, conv0, tiles)
+
+    Gather(shards, up_full, down_full, small_full, upb_full, gather_refs, deep, side, group_count, taps).late(i, tiles)
+
+    @pl.when(i < tiles)
+    def _():
+        r0 = pl.multiple_of(i * rows, rows)
+        up_gelu(shaped, up_cols(0), u8.at[0], act, r0, slope, r0, rows, hidden)
+        run(spills(i))
+
+    @pl.when((i >= tiles) & (i < 2 * tiles))
+    def _():
+        j = i - tiles
+        f0 = j * ft
+        r0 = pl.multiple_of(j * rows, rows)
+        branch = mm(act[pl.ds(r0, rows), :], down_full[0].reshape(hidden, width), NN)
+        for t in range(0, ft, 4):
+            b = branch[t * clips : (t + 4) * clips].reshape(4, clips, width) + s8[0, DOWN_BIAS][None]
+            total = masked0[pl.ds(HALO + f0 + t, 4)] + s8[0, GAIN][None] * b
+            masked1[pl.ds(HALO + f0 + t, 4)] = keep_frames(total, f0 + t, len8)
+
+    @pl.when((i >= 2 * tiles) & (i < 3 * tiles))
+    def _():
+        j = i - 2 * tiles
+        f0 = j * ft
+        r0 = pl.multiple_of(j * rows, rows)
+        done(spills(j))
+        conv_norm(masked1, f0, ft, s8.at[1], normed.at[1], inv.at[1], shaped, taps, HALO)
+        up_gelu(shaped, up_cols(1), u8.at[1], act, r0, slope, r0, rows, hidden)
+        branch = mm(act[pl.ds(r0, rows), :], down_full[1].reshape(hidden, width), NN)
+        last_block(branch, masked1, f0, r0, ft, s8.at[1], len8, first_rows, stream, out)
+
+    k = i - 3 * tiles
+    step = lax.rem(jnp.maximum(k, 0), span)
+    b = jnp.where(k < span, 1, 0)
+
+    @pl.when(k == 0)
+    def _():
+        load(1, og).wait()
+        spread_grad(io, stream, masked0, HALO)
+
+    @pl.when(k == span)
+    def _():
+        def one(n, carry):
+            t0 = n * 4
+            at = pl.multiple_of(t0 * clips, 4 * clips)
+            v = normed[0, pl.ds(HALO + t0, 4)] * s8[0, SCALE][None] + s8[0, SHIFT][None]
+            shaped[pl.ds(at, 4 * clips), :] = v.reshape(4 * clips, width).astype(BF16)
+            first = first_rows[pl.ds(at, 4 * clips), :].astype(F32).reshape(4, clips, width)
+            masked1[pl.ds(HALO + t0, 4)] = keep_frames(first, t0, len8)
+            return carry
+        lax.fori_loop(0, frame_count // 4, one, 0, unroll=4)
+        for j in range(tiles):
+            slope_back(j).wait()
+
+    @pl.when((k >= 0) & (step == 0))
+    def _():
+        acc[...] = jnp.zeros(acc.shape, F32)
+        acc[A_DOWN] = branch_grad(masked0, HALO, s8.at[b], len8, gb)
+
+    sums = Sums(sum_refs, up_term, down_term, up_part, down_part, small_part, small_grad, upb_grad, deep, side)
+    sums.before(k, span, parts, tiles)
+
+    @pl.when((k >= span) & (step < parts))
+    def _():
+        act_back(step).wait()
+
+    @pl.when((k >= 0) & (step < parts))
+    def _():
+        at = part_at(step)
+        drows, urows = down_full.shape[5], up_full.shape[5]
+        per = drows // 16
+        spots = []
+        for m in range(cols // 16):
+            row = step * (cols // 16) + m
+            e = row // per
+            z, chip = e // (2 * side * side), e // 2
+            sub = pl.ds(pl.multiple_of((row - e * per) * 16, 16), 16)
+            spots.append((b, z, lax.rem(chip // side, side), lax.rem(chip, side), lax.rem(e, 2), sub))
+        lower = jnp.concatenate([down_full[spot] for spot in spots], axis=0)
+        term = mm(act[:, at], gb[...], TN)
+        for m, spot in enumerate(spots):
+            down_term[spot] = term[m * 16 : (m + 1) * 16].astype(BF16)
+        acc[A_GAIN] += fold((term * lower.astype(F32)).reshape(cols // 8, 8, width))
+        before_grad(gb, lower, slope, at, slope, at, upb_acc, frame_count * clips)
+        term = mm(shaped[...], slope[:, at], TN).astype(BF16)
+        up_term[b, :, :, :, :, :, at] = term.reshape(deep, side, side, 2, urows, cols)
+
+    @pl.when((k >= 0) & (k < parts))
+    def _():
+        act_back(step).start()
+
+    j = step - parts
+
+    @pl.when((j >= 0) & (j < tiles))
+    def _():
+        r0 = pl.multiple_of(j * rows, rows)
+        grad = mm(slope[pl.ds(r0, rows), :], up_full[b].reshape(width, hidden), NT)
+        norm_back(grad, normed.at[b], HALO + j * ft, inv.at[b], j * ft, s8.at[b], normed.at[b], HALO + j * ft, acc, ft)
+
+    @pl.when((k < span) & (j >= 0) & (j < tiles))
+    def _():
+        slope_back(j).start()
+
+    @pl.when(j >= 1)
+    def _():
+        f0 = (j - 1) * ft
+        conv_back(
+            normed.at[b], HALO + f0, s8.at[b], masked1, HALO + f0, masked0, HALO + f0, f0, gs_out, acc, ft, len8, taps)
+
+    @pl.when((k >= 0) & (step == span - 1))
+    def _():
+        finish_small(acc, upb_acc, groups, s8.at[b], small_grad.at[b], upb_grad.at[b], group_count)
+
+    sums.after(k, span)
+
+
+def whole_step(deep, side, lens, groups, frames, og, weights, ft, taps, group_count):
+    clips, fc, d = frames.shape
+    h = weights[4].shape[2]
+    urows, drows = weights[4].shape[1], weights[6].shape[1]
+    R, r, n = fc * clips, ft * clips, fc // ft
+    parts = 6
+    span = parts + n + 1
+    last = lambda i: jnp.clip(i - 3 * n - span - parts - 1, 0, n - 1)
+    dims = (2, deep, side, side, 2)
+    rows = lambda dtype, *lead: pltpu.VMEM(lead + (d,), dtype)
+    halo = fc + 2 * HALO
+    return pl.pallas_call(
+        functools.partial(step_kernel, deep=deep, side=side, ft=ft, parts=parts, taps=taps, group_count=group_count),
+        name="step",
+        grid=(3 * n + 2 * span,),
+        in_specs=[smem(), smem(), hbm(), hbm()] + [vmem()] * 9,
+        out_specs=[
+            pl.BlockSpec((clips, ft, d), lambda i: (0, jnp.clip(i - 2 * n, 0, n - 1), 0)),
+            pl.BlockSpec((d // LANES, r, LANES), lambda i: (0, last(i), 0)), vmem(), vmem(), vmem(), hbm(), hbm(),
+        ],
+        out_shape=[
+            shape((clips, fc, d), BF16), shape((d // LANES, R, LANES)), shape((2, urows, h)), shape((2, drows, d)),
+            shape((2 * PACK, LANES)), shape((R, h), BF16), shape((R, h), BF16),
+        ],
+        scratch_shapes=[
+            rows(BF16, clips, fc), pltpu.VMEM((d // LANES, max(r, 16 * clips), LANES), F32),
+            rows(F32, halo, clips), rows(F32, halo, clips), rows(F32, 2, halo, clips), pltpu.VMEM((2, fc, clips, LANES), F32),
+            rows(BF16, R), rows(BF16, R), pltpu.VMEM((R, h), BF16), pltpu.VMEM((R, h), BF16), rows(BF16, R),
+            rows(F32, 2, 14, clips), pltpu.VMEM((2, clips, h), F32), rows(jnp.int32, clips), rows(F32, 12, clips),
+            pltpu.VMEM((clips, h), F32),
+            rows(F32, 2, ROWS), pltpu.VMEM((2, 1, h), F32), rows(F32, 2, ROWS), pltpu.VMEM((2, 1, h), F32),
+            pltpu.VMEM(dims + (urows, h), BF16), rows(BF16, *dims, drows), pltpu.VMEM(dims + (urows, h), BF16), rows(BF16, *dims, drows),
+            DMA((2,)), DMA((n,)), DMA((n,)), DMA((parts,)), DMA((n,)),
+        ] + gather_scratch(deep, side) + sums_scratch(deep, side, urows, drows, d, h),
+        compiler_params=pltpu.CompilerParams(vmem_limit_bytes=VMEM_LIMIT, collective_id=0, has_side_effects=True),
+    )(lens, groups, frames, og, *weights)
 
 
 def unpack_kernel(gs, up_in, down_in, small, gin, conv_w, conv_b, scale, shift, up_w, up_b, down_w, down_b, gain):
@@ -1128,17 +1269,13 @@
         small = whole_of(lines, 2).astype(F32)
         upb = whole_of(up_b, 1).astype(F32)[:, None]
         weights = (small, upb, ups, downs)
-    out, act, slope, normed, inv, shaped, masked, *full = forward(
-        near, deep, side, lengths, group, frames, weights, hidden, ft, taps, group_count
-    )
     if near:
-        ups, downs, small, _ = full
-        ups, downs = ups.reshape(2, -1, hidden), downs.reshape(2, hidden, -1)
-    saved = (act, slope.reshape(act.shape), normed, inv, shaped, masked)
-    gs, *parts = backward(near, deep, side, lengths, group, out_grad, saved, ups, downs, small, ft, taps, group_count)
-    if near:
+        out, gs, *parts, _, _ = whole_step(deep, side, lengths, group, frames, out_grad, weights, ft, taps, group_count)
         gin, conv_grad, *grads = unpack(gs, parts, clips, taps, group_count, width, wide)
         return (out, gin, conv_grad.transpose(1, 0, 2), *grads)
+    out, act, slope, *rest = forward(lengths, group, frames, weights, hidden, ft, taps, group_count)
+    saved = (act, slope.reshape(act.shape), *rest)
+    gs, *parts = backward(lengths, group, out_grad, saved, ups, downs, small, ft, taps, group_count)
     gin = unpack(gs, None, clips, taps, group_count, width, wide)
     dup, ddown, lines, ug = parts
     owner = lambda v, axis: lax.psum_scatter(v, axes, scatter_dimension=axis, tiled=True)

time: 190 us -> 181 us (0.953)
  Pallas kernels: 188 us -> 178 us
    pallas_call x2 -> x1, Pallas kernels: 180 us -> 171 us  [whole_step(): pl.pallas_call(functools.partial(step_kernel, deep=deep, side=side, ft=ft...]
where the time goes in v2:
time: 181 us; the launch traced here: 180 us
  Pallas kernels  178 us (98%)
    pallas_call x1, Pallas kernels, whole_step(): pl.pallas_call(functools.partial(step_kernel, deep=deep, side=side, ft=ft...  171 us
    pallas_call x1, Pallas kernels, unpack(): pl.pallas_call(unpack_kernel, name='unpack', grid=(fc // ft,), in_specs=[...  7.33 us

profile of v2, /device:TPU:0, one launch (start us, length us, event | category | flops | bytes accessed | tf_op | source)
XLA Modules:
  0.0 180.5 jit_solution(5034141625705769858)
XLA Ops:
  0.6 171.1 %step.1 = (bf16[8,256,512]{2,1,0:T(8,128)(2,1)}, f32[4,2048,128]{2,1,0:T(8,128)}, f32[2,16,1536]{2,1,0:T(8,128)}, f32[2,48,512]{2,1,0:T(8,128)}, f32[40,128]{1,0...) custom-call(s32[8]{0:T(128)} %refs_0_.1, s32[8]{0:T(128)} %refs_1_.1, bf16[8,256,512]{2,1,0:T(8,128)(2,1)} %refs_2_.1, ...), custom_call_target="tpu_custom_call" | custom-call | tf_op jit(solution)/shard_map/step/pallas_call | solution.py:1170
  171.8 0.0 copy-start
  171.8 7.3 %unpack.1 = (f32[8,256,512]{2,1,0:T(8,128)}, f32[7,2,16]{2,1,0:T(2,128)}, f32[2,16]{1,0:T(2,128)}, f32[2,2,16]{2,1,0:T(2,128)}, f32[2,2,16]{2,1,0:T(2,128)}, /*i...) custom-call(f32[4,2048,128]{2,1,0:T(8,128)} %get-tuple-element.27.gs, ...), custom_call_target="tpu_custom_call" | custom-call | tf_op jit(solution)/shard_map/unpack/pallas_call | solution.py:1243
  179.1 0.0 copy-done
  179.1 1.3 copy.25
Async XLA Ops:
  171.8 7.3 %copy-start = (bf16[8,256,512]{2,1,0:T(8,128)(2,1)S(1)}, bf16[8,256,512]{2,1,0:T(8,128)(2,1)}, u32[]{:S(2)}) copy-start(bf16[8,256,512]{2,1,0:T(8,128)(2,1)} %get-tuple-element.52) | copy-start | bytes 6291460

commit v3 on v2

--- a/solution.py
+++ b/solution.py
@@ -300,6 +300,8 @@
         self.zbuf[place.z] = self.pack[...]
         run(self.small[0])
         self.begin(1)
+        self.begin(2)
+        self.begin(3)
         spread()
         done(self.small[0])
         run(self.small[1])
@@ -311,8 +313,6 @@
         self.first_sum[...] = total
         run(self.small[2])
         self.after_z(1)
-        self.begin(2)
-        self.begin(3)
         done(self.small[2])
         total = self.first_sum[...]
         for p in range(1, place.side):
@@ -323,12 +323,14 @@
         done(self.small[3])
         self.finish_small()
         ready()
-        conv(0, tiles // 4)
         self.after_first(1)
-        conv(tiles // 4, tiles // 2)
+        conv(0, tiles // 2)
         self.after_second(0)
-        conv(tiles // 2, tiles)
+        self.after_z(2)
+        self.after_z(3)
+        conv(tiles // 2, 3 * tiles // 4)
         self.after_second(1)
+        conv(3 * tiles // 4, tiles)
         self.end(0)
 
     def finish_small(self):
@@ -345,23 +347,24 @@
                     self.upb_full[b, :, at : at + LANES] = total[z, o + 14 + q : o + 15 + q, :]
 
     def late(self, i, tiles):
-        @pl.when(i == 1)
-        def _():
-            self.after_z(2)
-            self.after_z(3)
-
-        @pl.when(i == tiles // 2 + 1)
+        @pl.when(i == tiles // 4)
         def _():
             self.after_first(2)
+
+        @pl.when(i == tiles // 2)
+        def _():
             self.after_first(3)
 
         @pl.when(i == tiles)
         def _():
             self.end(1)
 
-        @pl.when(i == 2 * tiles - tiles // 4)
+        @pl.when(i == tiles + tiles // 2)
         def _():
             self.after_second(2)
+
+        @pl.when(i == 2 * tiles - 1)
+        def _():
             self.after_second(3)
 
         @pl.when(i == 2 * tiles)
@@ -677,13 +680,23 @@
             terms[z, o + 14 + q : o + 15 + q, :] = upb[:, at : at + LANES]
 
 
-def sum_small(place, terms, bufs, z_in, out, s, r):
+def sum_small(place, terms, z_in, bufs, out, s, r):
+    n = 0
+    copies = []
+    for p in range(1, place.deep):
+        to = lax.rem(place.z + p, place.deep)
+        copies.append(send(terms.at[to], z_in.at[p - 1], s.at[n], r.at[n], place.z_peer(p)))
+        n += 1
+    run(copies)
+    yield
+    done(copies)
+    total = terms[place.z]
+    for p in range(1, place.deep):
+        total = total + z_in[p - 1]
     stages = [[place.core_peer()], [place.second_peer(p) for p in range(1, place.side)],
               [place.first_peer(p) for p in range(1, place.side)]]
-    n = 0
-    here = terms
-    for stage, peers in enumerate(stages):
-        into, total_ref = bufs[stage]
+    for (here, into), peers in zip(bufs, stages):
+        here[...] = total
         copies = []
         for p, peer in enumerate(peers):
             copies.append(send(here, into.at[p], s.at[n], r.at[n], peer))
@@ -691,65 +704,61 @@
         run(copies)
         yield
         done(copies)
-        total = here[...]
         for p in range(len(peers)):
             total = total + into[p]
-        total_ref[...] = total
-        here = total_ref
-    copies = []
-    for p in range(1, place.deep):
-        to = lax.rem(place.z + p, place.deep)
-        copies.append(send(here.at[to], z_in.at[p - 1], s.at[n], r.at[n], place.z_peer(p)))
-        n += 1
-    run(copies)
-    yield
-    done(copies)
-    total = here[place.z]
-    for p in range(1, place.deep):
-        total = total + z_in[p - 1]
     out[...] = total
 
 
 def small_bufs(deep, side):
-    buf = pltpu.VMEM((deep, 2 * PACK, LANES), F32)
-    many = lambda n: pltpu.VMEM((n, deep, 2 * PACK, LANES), F32)
+    many = lambda *n: pltpu.VMEM(n + (2 * PACK, LANES), F32)
     n = deep - 1 + 2 * (side - 1) + 1
-    return [buf, many(1), buf, many(side - 1), buf, many(side - 1), buf, pltpu.VMEM((deep - 1, 2 * PACK, LANES), F32), DMA((n,)), DMA((n,))]
+    return [many(deep), many(deep - 1), many(), many(1), many(), many(side - 1), many(), many(side - 1), DMA((n,)), DMA((n,))]
 
 
 class Sums:
-    def __init__(self, refs, dup, ddown, up_part, down_part, small_part, small_grad, upb_grad, deep, side):
+    def __init__(self, refs, up_term, down_term, up_part, down_part, small_part, small_grad, upb_grad, deep, side):
         self.place = Place(deep, side)
-        (self.terms, c_in, c_sum, s_in, s_sum, f_in, f_sum, self.z_in, self.small_s, self.small_r) = refs[:10]
-        self.bufs = ((c_in, c_sum), (s_in, s_sum), (f_in, f_sum))
+        self.terms, self.z_in = refs[:2]
+        self.bufs = [refs[2:4], refs[4:6], refs[6:8]]
+        self.small_s, self.small_r = refs[8:10]
         refs = refs[10:]
         sems = refs[-8:]
         self.small_part, self.small_grad, self.upb_grad = small_part, small_grad, upb_grad
-        self.jobs = {}
-        self.outs = {}
-        for n, (b, term, out) in enumerate(
-            ((1, ddown, down_part), (1, dup, up_part), (0, ddown, down_part), (0, dup, up_part))
-        ):
-            job = Scatter(self.place, term.at[b], refs[4 * n : 4 * n + 4], [s.at[n] for s in sems])
-            self.jobs.setdefault(b, []).append((job, out.at[b]))
-
-    def each(self, b, what):
-        for job, out in self.jobs[b]:
-            if what == "finish":
-                job.finish(out)
-            else:
-                getattr(job, what)()
-
-    def before(self, i, span, parts, tiles):
-        plan = [
-            (parts, 1, "core_start"), (parts + 3, 1, "second_start"), (span, 1, "first_start"),
-            (span + 3, 1, "z_start"), (span + parts - 1, 1, "finish"),
-            (span + parts, 0, "core_start"), (span + parts + 3, 0, "second_start"), (2 * span - 1, 0, "first_start"),
+        half = up_part.shape[2] // 2
+        self.jobs = []
+        for b in (1, 0):
+            views = [(down_term.at[b], down_part.at[b])]
+            for lo in (0, half):
+                views.append((up_term.at[b, :, :, :, :, :, pl.ds(lo, half)], up_part.at[b, :, pl.ds(lo, half)]))
+            for term, out in views:
+                n = len(self.jobs)
+                self.jobs.append((Scatter(self.place, term, refs[4 * n : 4 * n + 4], [s.at[n] for s in sems]), out))
+
+    def do(self, n, what):
+        job, out = self.jobs[n]
+        if what == "finish":
+            job.finish(out)
+        else:
+            getattr(job, what)()
+
+    def before(self, i, span, parts):
+        times = [
+            {"core_start": parts, "second_start": parts + 2, "first_start": 2 * parts, "z_start": 2 * parts + 3, "finish": span - 1},
+            {"core_start": parts + 3, "second_start": parts + 5, "first_start": 2 * parts + 2, "z_start": 2 * parts + 5, "finish": span - 1},
+            {"core_start": 2 * parts, "second_start": 2 * parts + 2, "first_start": 2 * parts + 5, "z_start": span - 1, "finish": span + 2},
         ]
-        for at, b, what in plan:
+        plan = []
+        for order, what in enumerate(("core_start", "second_start", "first_start", "z_start", "finish")):
+            for n in range(6):
+                at = times[n % 3][what] + (n // 3) * span
+                if at < 2 * span:
+                    plan.append((at, order, n, what))
+        for at in sorted({p[0] for p in plan}):
             @pl.when(i == at)
             def _():
-                self.each(b, what)
+                for now, _, n, what in plan:
+                    if now == at:
+                        self.do(n, what)
 
     def after(self, i, span):
         @pl.when(i == 2 * span - 1)
@@ -757,18 +766,16 @@
             self.terms[...] = jnp.zeros(self.terms.shape, F32)
             for b in range(2):
                 pack_small(self.small_grad.at[b], self.upb_grad.at[b], b, self.terms, self.place.deep)
-            steps = sum_small(self.place, self.terms, self.bufs, self.z_in, self.small_part, self.small_s, self.small_r)
+            steps = sum_small(self.place, self.terms, self.z_in, self.bufs, self.small_part, self.small_s, self.small_r)
             next(steps)
-            next(steps)
-            self.each(0, "z_start")
+            self.do(5, "finish")
             for _ in steps:
                 pass
-            self.each(0, "finish")
 
 
 def sums_scratch(deep, side, urows, drows, d, h):
-    ub, db = scatter_bufs(deep, side, urows, h), scatter_bufs(deep, side, drows, d)
-    return small_bufs(deep, side) + db + ub + db + ub + scatter_sems(4, deep, side)
+    ub, db = scatter_bufs(deep, side, urows, h // 2), scatter_bufs(deep, side, drows, d)
+    return small_bufs(deep, side) + 2 * (db + ub + ub) + scatter_sems(6, deep, side)
 
 
 def norm_back(gs, normed, n0, inv, i0, s8, gm, gm0, acc, frames, step=4):
@@ -982,8 +989,7 @@
     tiles = frame_count // ft
     rows = ft * clips
     cols = hidden // parts
-    span = parts + tiles + 1
-    body = pl.ds(HALO, frame_count)
+    span = 2 * parts + tiles + 1
 
     load = lambda n, src: pltpu.make_async_copy(src, io, io_sem.at[n])
     tile_rows = lambda j: pl.ds(pl.multiple_of(j * rows, rows), rows)
@@ -1100,38 +1106,44 @@
         acc[A_DOWN] = branch_grad(masked0, HALO, s8.at[b], len8, gb)
 
     sums = Sums(sum_refs, up_term, down_term, up_part, down_part, small_part, small_grad, upb_grad, deep, side)
-    sums.before(k, span, parts, tiles)
+    sums.before(k, span, parts)
 
     @pl.when((k >= span) & (step < parts))
     def _():
         act_back(step).wait()
 
-    @pl.when((k >= 0) & (step < parts))
-    def _():
-        at = part_at(step)
-        drows, urows = down_full.shape[5], up_full.shape[5]
-        per = drows // 16
-        spots = []
+    def spots(p):
+        per = down_full.shape[5] // 16
         for m in range(cols // 16):
-            row = step * (cols // 16) + m
+            row = p * (cols // 16) + m
             e = row // per
             z, chip = e // (2 * side * side), e // 2
             sub = pl.ds(pl.multiple_of((row - e * per) * 16, 16), 16)
-            spots.append((b, z, lax.rem(chip // side, side), lax.rem(chip, side), lax.rem(e, 2), sub))
-        lower = jnp.concatenate([down_full[spot] for spot in spots], axis=0)
-        term = mm(act[:, at], gb[...], TN)
-        for m, spot in enumerate(spots):
-            down_term[spot] = term[m * 16 : (m + 1) * 16].astype(BF16)
-        acc[A_GAIN] += fold((term * lower.astype(F32)).reshape(cols // 8, 8, width))
+            yield (b, z, lax.rem(chip // side, side), lax.rem(chip, side), lax.rem(e, 2), sub)
+
+    @pl.when((k >= 0) & (step < parts))
+    def _():
+        term = mm(act[:, part_at(step)], gb[...], TN)
+        total = jnp.zeros((clips, width), F32)
+        for m, spot in enumerate(spots(step)):
+            piece = term[m * 16 : (m + 1) * 16]
+            down_term[spot] = piece.astype(BF16)
+            total = total + fold((piece * down_full[spot].astype(F32)).reshape(2, 8, width))
+        acc[A_GAIN] += total
+
+    @pl.when((k >= 0) & (k < parts))
+    def _():
+        act_back(step).start()
+
+    @pl.when((k >= 0) & (step >= parts) & (step < 2 * parts))
+    def _():
+        at = part_at(step - parts)
+        lower = jnp.concatenate([down_full[spot] for spot in spots(step - parts)], axis=0)
         before_grad(gb, lower, slope, at, slope, at, upb_acc, frame_count * clips)
         term = mm(shaped[...], slope[:, at], TN).astype(BF16)
-        up_term[b, :, :, :, :, :, at] = term.reshape(deep, side, side, 2, urows, cols)
-
-    @pl.when((k >= 0) & (k < parts))
-    def _():
-        act_back(step).start()
-
-    j = step - parts
+        up_term[b, :, :, :, :, :, at] = term.reshape(deep, side, side, 2, up_full.shape[5], cols)
+
+    j = step - 2 * parts
 
     @pl.when((j >= 0) & (j < tiles))
     def _():
@@ -1162,8 +1174,8 @@
     urows, drows = weights[4].shape[1], weights[6].shape[1]
     R, r, n = fc * clips, ft * clips, fc // ft
     parts = 6
-    span = parts + n + 1
-    last = lambda i: jnp.clip(i - 3 * n - span - parts - 1, 0, n - 1)
+    span = 2 * parts + n + 1
+    last = lambda i: jnp.clip(i - 3 * n - span - 2 * parts - 1, 0, n - 1)
     dims = (2, deep, side, side, 2)
     rows = lambda dtype, *lead: pltpu.VMEM(lead + (d,), dtype)
     halo = fc + 2 * HALO

time: 181 us -> 191 us (1.055)
  Pallas kernels: 178 us -> 189 us
    pallas_call x1, Pallas kernels: 171 us -> 181 us  [whole_step(): pl.pallas_call(functools.partial(step_kernel, deep=deep, side=side, ft=ft...]
where the time goes in v3:
time: 191 us
  Pallas kernels  189 us (99%)
    pallas_call x1, Pallas kernels, whole_step(): pl.pallas_call(functools.partial(step_kernel, deep=deep, side=side, ft=ft...  181 us
    pallas_call x1, Pallas kernels, unpack(): pl.pallas_call(unpack_kernel, name='unpack', grid=(fc // ft,), in_specs=[...  7.33 us

profile of v3, /device:TPU:0, one launch (start us, length us, event | category | flops | bytes accessed | tf_op | source)
XLA Modules:
  0.0 190.6 jit_solution(11591901954078689987)
XLA Ops:
  0.6 181.3 %step.1 = (bf16[8,256,512]{2,1,0:T(8,128)(2,1)}, f32[4,2048,128]{2,1,0:T(8,128)}, f32[2,16,1536]{2,1,0:T(8,128)}, f32[2,48,512]{2,1,0:T(8,128)}, f32[40,128]{1,0...) custom-call(s32[8]{0:T(128)} %refs_0_.1, s32[8]{0:T(128)} %refs_1_.1, bf16[8,256,512]{2,1,0:T(8,128)(2,1)} %refs_2_.1, ...), custom_call_target="tpu_custom_call" | custom-call | tf_op jit(solution)/shard_map/step/pallas_call | solution.py:1182
  181.9 0.0 copy-start
  182.0 7.3 %unpack.1 = (f32[8,256,512]{2,1,0:T(8,128)}, f32[7,2,16]{2,1,0:T(2,128)}, f32[2,16]{1,0:T(2,128)}, f32[2,2,16]{2,1,0:T(2,128)}, f32[2,2,16]{2,1,0:T(2,128)}, /*i...) custom-call(f32[4,2048,128]{2,1,0:T(8,128)} %get-tuple-element.27.gs, ...), custom_call_target="tpu_custom_call" | custom-call | tf_op jit(solution)/shard_map/unpack/pallas_call | solution.py:1255
  189.3 0.0 copy-done
  189.3 1.3 copy.25
Async XLA Ops:
  181.9 7.3 %copy-start = (bf16[8,256,512]{2,1,0:T(8,128)(2,1)S(1)}, bf16[8,256,512]{2,1,0:T(8,128)(2,1)}, u32[]{:S(2)}) copy-start(bf16[8,256,512]{2,1,0:T(8,128)(2,1)} %get-tuple-element.52) | copy-start | bytes 6291460

commit v4 on v3

--- a/solution.py
+++ b/solution.py
@@ -300,8 +300,6 @@
         self.zbuf[place.z] = self.pack[...]
         run(self.small[0])
         self.begin(1)
-        self.begin(2)
-        self.begin(3)
         spread()
         done(self.small[0])
         run(self.small[1])
@@ -312,7 +310,6 @@
             total = total + self.first_in[p - 1]
         self.first_sum[...] = total
         run(self.small[2])
-        self.after_z(1)
         done(self.small[2])
         total = self.first_sum[...]
         for p in range(1, place.side):
@@ -320,16 +317,15 @@
         self.second_sum[...] = total
         run(self.small[3])
         self.after_first(0)
+        self.after_z(1)
+        self.begin(2)
+        self.begin(3)
         done(self.small[3])
         self.finish_small()
         ready()
+        conv(0, 3 * tiles // 4)
+        self.after_second(0)
         self.after_first(1)
-        conv(0, tiles // 2)
-        self.after_second(0)
-        self.after_z(2)
-        self.after_z(3)
-        conv(tiles // 2, 3 * tiles // 4)
-        self.after_second(1)
         conv(3 * tiles // 4, tiles)
         self.end(0)
 
@@ -349,26 +345,26 @@
     def late(self, i, tiles):
         @pl.when(i == tiles // 4)
         def _():
-            self.after_first(2)
-
-        @pl.when(i == tiles // 2)
+            self.after_z(2)
+            self.after_z(3)
+
+        @pl.when(i == 3 * tiles // 4)
         def _():
-            self.after_first(3)
+            self.after_second(1)
 
         @pl.when(i == tiles)
         def _():
             self.end(1)
 
-        @pl.when(i == tiles + tiles // 2)
+        @pl.when(i == tiles + tiles // 4)
         def _():
-            self.after_second(2)
-
-        @pl.when(i == 2 * tiles - 1)
-        def _():
-            self.after_second(3)
+            self.after_first(2)
+            self.after_first(3)
 
         @pl.when(i == 2 * tiles)
         def _():
+            for n in (2, 3):
+                self.after_second(n)
             for n in (2, 3):
                 self.end(n)
 
@@ -716,7 +712,7 @@
 
 
 class Sums:
-    def __init__(self, refs, up_term, down_term, up_part, down_part, small_part, small_grad, upb_grad, deep, side):
+    def __init__(self, refs, up_term, down_term, up_part, down_part, small_part, small_grad, upb_grad, deep, side, parts):
         self.place = Place(deep, side)
         self.terms, self.z_in = refs[:2]
         self.bufs = [refs[2:4], refs[4:6], refs[6:8]]
@@ -724,12 +720,15 @@
         refs = refs[10:]
         sems = refs[-8:]
         self.small_part, self.small_grad, self.upb_grad = small_part, small_grad, upb_grad
-        half = up_part.shape[2] // 2
+        self.parts = parts
+        cols = up_part.shape[2] // parts
         self.jobs = []
         for b in (1, 0):
-            views = [(down_term.at[b], down_part.at[b])]
-            for lo in (0, half):
-                views.append((up_term.at[b, :, :, :, :, :, pl.ds(lo, half)], up_part.at[b, :, pl.ds(lo, half)]))
+            views = []
+            for p in range(parts):
+                c = pl.ds(p * cols, cols)
+                views.append((up_term.at[b, :, :, :, :, :, c], up_part.at[b, :, c]))
+            views.append((down_term.at[b], down_part.at[b]))
             for term, out in views:
                 n = len(self.jobs)
                 self.jobs.append((Scatter(self.place, term, refs[4 * n : 4 * n + 4], [s.at[n] for s in sems]), out))
@@ -741,23 +740,27 @@
         else:
             getattr(job, what)()
 
-    def before(self, i, span, parts):
-        times = [
-            {"core_start": parts, "second_start": parts + 2, "first_start": 2 * parts, "z_start": 2 * parts + 3, "finish": span - 1},
-            {"core_start": parts + 3, "second_start": parts + 5, "first_start": 2 * parts + 2, "z_start": 2 * parts + 5, "finish": span - 1},
-            {"core_start": 2 * parts, "second_start": 2 * parts + 2, "first_start": 2 * parts + 5, "z_start": span - 1, "finish": span + 2},
-        ]
+    def at(self, i, half, span):
+        parts, per = self.parts, self.parts + 1
+        whats = ("core_start", "second_start", "first_start", "z_start", "finish")
+        when = []
+        for p in range(parts - 1):
+            t = 2 * (p + 1)
+            when.append((t, t + 1, t + 3, t + 5, 2 * parts + 6))
+        t = 2 * parts
+        when.append((t, t + 2, t + 5, t + 8, t + 12))
+        when.append((t, t + 3, t + 9, t + 12, t + 16))
         plan = []
-        for order, what in enumerate(("core_start", "second_start", "first_start", "z_start", "finish")):
-            for n in range(6):
-                at = times[n % 3][what] + (n // 3) * span
-                if at < 2 * span:
-                    plan.append((at, order, n, what))
-        for at in sorted({p[0] for p in plan}):
-            @pl.when(i == at)
+        for order, what in enumerate(whats):
+            for n in range(2 * per):
+                slot = when[n % per][order] + 2 * span * (n // per)
+                if slot < 4 * span and slot % 2 == half:
+                    plan.append((slot // 2, n, what))
+        for now in sorted({p[0] for p in plan}):
+            @pl.when(i == now)
             def _():
-                for now, _, n, what in plan:
-                    if now == at:
+                for step, n, what in plan:
+                    if step == now:
                         self.do(n, what)
 
     def after(self, i, span):
@@ -767,15 +770,21 @@
             for b in range(2):
                 pack_small(self.small_grad.at[b], self.upb_grad.at[b], b, self.terms, self.place.deep)
             steps = sum_small(self.place, self.terms, self.z_in, self.bufs, self.small_part, self.small_s, self.small_r)
+            last = 2 * (self.parts + 1) - 1
             next(steps)
-            self.do(5, "finish")
+            next(steps)
+            self.do(last, "z_start")
+            self.do(last - 1, "finish")
+            next(steps)
+            next(steps)
+            self.do(last, "finish")
             for _ in steps:
                 pass
 
 
-def sums_scratch(deep, side, urows, drows, d, h):
-    ub, db = scatter_bufs(deep, side, urows, h // 2), scatter_bufs(deep, side, drows, d)
-    return small_bufs(deep, side) + 2 * (db + ub + ub) + scatter_sems(6, deep, side)
+def sums_scratch(deep, side, urows, drows, d, h, parts):
+    ub, db = scatter_bufs(deep, side, urows, h // parts), scatter_bufs(deep, side, drows, d)
+    return small_bufs(deep, side) + 2 * (parts * ub + db) + scatter_sems(2 * (parts + 1), deep, side)
 
 
 def norm_back(gs, normed, n0, inv, i0, s8, gm, gm0, acc, frames, step=4):
@@ -815,7 +824,8 @@
             total = jnp.where(t < len8[:, cols][None], total, 0.0)
             total = gs[pl.ds(g0 + j, step), :, cols] + total
             gs[pl.ds(g0 + j, step), :, cols] = total
-            out[l, j * clips : (j + step) * clips, :] = total.reshape(step * clips, LANES)
+            if out is not None:
+                out[l, j * clips : (j + step) * clips, :] = total.reshape(step * clips, LANES)
         for k in range(taps):
             acc[A_TAPS + k, :, cols] = sums[k]
 
@@ -921,14 +931,15 @@
     return lax.fori_loop(0, frame_count // 4, one, jnp.zeros((clips, width), F32), unroll=4)
 
 
-def before_grad(gb, lower, slope, slope_cols, gbef, at, upb_acc, rows, sub=16):
+def before_grad(gb, lower, slope, slope_cols, gbef, at, upb_acc, rows, chunk=1024, sub=16):
     cols = lower.shape[0]
-    ga = mm(gb[...], lower, NT)
     total = jnp.zeros((8, cols), F32)
-    for r in range(0, rows, sub):
-        gr = ga[r : r + sub] * slope[r : r + sub, slope_cols].astype(F32)
-        total = total + fold(gr.reshape(sub // 8, 8, cols))
-        gbef[r : r + sub, at] = gr.astype(BF16)
+    for c in range(0, rows, chunk):
+        ga = mm(gb[c : c + chunk, :], lower, NT)
+        for r in range(0, chunk, sub):
+            gr = ga[r : r + sub] * slope[c + r : c + r + sub, slope_cols].astype(F32)
+            total = total + fold(gr.reshape(sub // 8, 8, cols))
+            gbef[c + r : c + r + sub, at] = gr.astype(BF16)
     upb_acc[:, at] = total
 
 
@@ -980,8 +991,8 @@
     out, gs_out, up_part, down_part, small_part, act_far, slope_far = refs[13:20]
     (io, stream, masked0, masked1, normed, inv, shaped, first_rows, act, slope, gb, s8, u8, len8, acc, upb_acc) = refs[20:36]
     small_full, upb_full, small_grad, upb_grad, up_full, down_full, up_term, down_term = refs[36:44]
-    io_sem, act_sem, slope_sem, act_back_sem, slope_back_sem = refs[44:49]
-    gather_refs, sum_refs = refs[49:67], refs[67:]
+    io_sem, act_sem, slope_sem, act_back_sem, slope_back_sem, gs_sem = refs[44:50]
+    gather_refs, sum_refs = refs[50:68], refs[68:]
 
     i = pl.program_id(0)
     clips, frame_count, width = io.shape
@@ -989,7 +1000,8 @@
     tiles = frame_count // ft
     rows = ft * clips
     cols = hidden // parts
-    span = 2 * parts + tiles + 1
+    span = parts + tiles + 1
+    body = pl.ds(HALO, frame_count)
 
     load = lambda n, src: pltpu.make_async_copy(src, io, io_sem.at[n])
     tile_rows = lambda j: pl.ds(pl.multiple_of(j * rows, rows), rows)
@@ -1105,45 +1117,39 @@
         acc[...] = jnp.zeros(acc.shape, F32)
         acc[A_DOWN] = branch_grad(masked0, HALO, s8.at[b], len8, gb)
 
-    sums = Sums(sum_refs, up_term, down_term, up_part, down_part, small_part, small_grad, upb_grad, deep, side)
-    sums.before(k, span, parts)
+    sums = Sums(sum_refs, up_term, down_term, up_part, down_part, small_part, small_grad, upb_grad, deep, side, parts)
+    sums.at(k, 0, span)
 
     @pl.when((k >= span) & (step < parts))
     def _():
         act_back(step).wait()
 
-    def spots(p):
-        per = down_full.shape[5] // 16
+    @pl.when((k >= 0) & (step < parts))
+    def _():
+        at = part_at(step)
+        drows, urows = down_full.shape[5], up_full.shape[5]
+        per = drows // 16
+        spots = []
         for m in range(cols // 16):
-            row = p * (cols // 16) + m
+            row = step * (cols // 16) + m
             e = row // per
             z, chip = e // (2 * side * side), e // 2
             sub = pl.ds(pl.multiple_of((row - e * per) * 16, 16), 16)
-            yield (b, z, lax.rem(chip // side, side), lax.rem(chip, side), lax.rem(e, 2), sub)
-
-    @pl.when((k >= 0) & (step < parts))
-    def _():
-        term = mm(act[:, part_at(step)], gb[...], TN)
-        total = jnp.zeros((clips, width), F32)
-        for m, spot in enumerate(spots(step)):
-            piece = term[m * 16 : (m + 1) * 16]
-            down_term[spot] = piece.astype(BF16)
-            total = total + fold((piece * down_full[spot].astype(F32)).reshape(2, 8, width))
-        acc[A_GAIN] += total
-
-    @pl.when((k >= 0) & (k < parts))
-    def _():
-        act_back(step).start()
-
-    @pl.when((k >= 0) & (step >= parts) & (step < 2 * parts))
-    def _():
-        at = part_at(step - parts)
-        lower = jnp.concatenate([down_full[spot] for spot in spots(step - parts)], axis=0)
+            spots.append((b, z, lax.rem(chip // side, side), lax.rem(chip, side), lax.rem(e, 2), sub))
+        lower = jnp.concatenate([down_full[spot] for spot in spots], axis=0)
+        term = mm(act[:, at], gb[...], TN)
+        for m, spot in enumerate(spots):
+            down_term[spot] = term[m * 16 : (m + 1) * 16].astype(BF16)
+        acc[A_GAIN] += fold((term * lower.astype(F32)).reshape(cols // 8, 8, width))
         before_grad(gb, lower, slope, at, slope, at, upb_acc, frame_count * clips)
         term = mm(shaped[...], slope[:, at], TN).astype(BF16)
-        up_term[b, :, :, :, :, :, at] = term.reshape(deep, side, side, 2, up_full.shape[5], cols)
-
-    j = step - 2 * parts
+        up_term[b, :, :, :, :, :, at] = term.reshape(deep, side, side, 2, urows, cols)
+
+    @pl.when((k >= 0) & (k < parts))
+    def _():
+        act_back(step).start()
+
+    j = step - parts
 
     @pl.when((j >= 0) & (j < tiles))
     def _():
@@ -1155,17 +1161,29 @@
     def _():
         slope_back(j).start()
 
+    sums.at(k, 1, span)
+    gs_copy = lambda f0, n: pltpu.make_async_copy(masked0.at[pl.ds(HALO + f0, ft)], gs_out.at[pl.ds(f0, ft)], gs_sem.at[n])
+
     @pl.when(j >= 1)
     def _():
         f0 = (j - 1) * ft
         conv_back(
-            normed.at[b], HALO + f0, s8.at[b], masked1, HALO + f0, masked0, HALO + f0, f0, gs_out, acc, ft, len8, taps)
+            normed.at[b], HALO + f0, s8.at[b], masked1, HALO + f0, masked0, HALO + f0, f0, None, acc, ft, len8, taps)
+
+    @pl.when((k >= span) & (j >= 1))
+    def _():
+        gs_copy((j - 1) * ft, j - 1).start()
 
     @pl.when((k >= 0) & (step == span - 1))
     def _():
         finish_small(acc, upb_acc, groups, s8.at[b], small_grad.at[b], upb_grad.at[b], group_count)
 
     sums.after(k, span)
+
+    @pl.when(k == 2 * span - 1)
+    def _():
+        for n in range(tiles):
+            gs_copy(n * ft, n).wait()
 
 
 def whole_step(deep, side, lens, groups, frames, og, weights, ft, taps, group_count):
@@ -1173,9 +1191,8 @@
     h = weights[4].shape[2]
     urows, drows = weights[4].shape[1], weights[6].shape[1]
     R, r, n = fc * clips, ft * clips, fc // ft
-    parts = 6
-    span = 2 * parts + n + 1
-    last = lambda i: jnp.clip(i - 3 * n - span - 2 * parts - 1, 0, n - 1)
+    parts = 3
+    span = parts + n + 1
     dims = (2, deep, side, side, 2)
     rows = lambda dtype, *lead: pltpu.VMEM(lead + (d,), dtype)
     halo = fc + 2 * HALO
@@ -1186,10 +1203,10 @@
         in_specs=[smem(), smem(), hbm(), hbm()] + [vmem()] * 9,
         out_specs=[
             pl.BlockSpec((clips, ft, d), lambda i: (0, jnp.clip(i - 2 * n, 0, n - 1), 0)),
-            pl.BlockSpec((d // LANES, r, LANES), lambda i: (0, last(i), 0)), vmem(), vmem(), vmem(), hbm(), hbm(),
+            hbm(), vmem(), vmem(), vmem(), hbm(), hbm(),
         ],
         out_shape=[
-            shape((clips, fc, d), BF16), shape((d // LANES, R, LANES)), shape((2, urows, h)), shape((2, drows, d)),
+            shape((clips, fc, d), BF16), shape((fc, clips, d)), shape((2, urows, h)), shape((2, drows, d)),
             shape((2 * PACK, LANES)), shape((R, h), BF16), shape((R, h), BF16),
         ],
         scratch_shapes=[
@@ -1200,16 +1217,19 @@
             pltpu.VMEM((clips, h), F32),
             rows(F32, 2, ROWS), pltpu.VMEM((2, 1, h), F32), rows(F32, 2, ROWS), pltpu.VMEM((2, 1, h), F32),
             pltpu.VMEM(dims + (urows, h), BF16), rows(BF16, *dims, drows), pltpu.VMEM(dims + (urows, h), BF16), rows(BF16, *dims, drows),
-            DMA((2,)), DMA((n,)), DMA((n,)), DMA((parts,)), DMA((n,)),
-        ] + gather_scratch(deep, side) + sums_scratch(deep, side, urows, drows, d, h),
+            DMA((2,)), DMA((n,)), DMA((n,)), DMA((parts,)), DMA((n,)), DMA((n,)),
+        ] + gather_scratch(deep, side) + sums_scratch(deep, side, urows, drows, d, h, parts),
         compiler_params=pltpu.CompilerParams(vmem_limit_bytes=VMEM_LIMIT, collective_id=0, has_side_effects=True),
     )(lens, groups, frames, og, *weights)
 
 
 def unpack_kernel(gs, up_in, down_in, small, gin, conv_w, conv_b, scale, shift, up_w, up_b, down_w, down_b, gain):
-    collect_clips(gs, gin, gin.shape[1])
-
-    @pl.when(pl.program_id(0) == 0)
+    clips, frames, _ = gin.shape
+    for c in range(clips):
+        for t in range(0, frames, 16):
+            gin[c, t : t + 16, :] = gs[pl.ds(t * clips + c, 16, stride=clips), :]
+
+    @pl.when((pl.program_id(0) == 0) & (pl.program_id(1) == 0))
     def _():
         unpack_parts(up_in, down_in, small, conv_w, conv_b, scale, shift, up_w, up_b, down_w, down_b, gain)
 
@@ -1236,30 +1256,35 @@
     down_w[...] = down_in[...]
 
 
-def unpack(gs, parts, clips, taps, group_count, width, wide):
+def unpack_far(gs, clips):
     split, R, lanes = gs.shape
     fc = R // clips
     ft = 32
-    if parts is None:
-        return pl.pallas_call(
-            lambda src, dst: collect_clips(src, dst, ft),
-            name="unpack",
-            grid=(fc // ft,),
-            in_specs=[pl.BlockSpec((split, ft * clips, lanes), lambda i: (0, i, 0))],
-            out_specs=pl.BlockSpec((clips, ft, split * lanes), lambda i: (0, i, 0)),
-            out_shape=shape((clips, fc, split * lanes)),
-        )(gs)
+    return pl.pallas_call(
+        lambda src, dst: collect_clips(src, dst, ft),
+        name="unpack",
+        grid=(fc // ft,),
+        in_specs=[pl.BlockSpec((split, ft * clips, lanes), lambda i: (0, i, 0))],
+        out_specs=pl.BlockSpec((clips, ft, split * lanes), lambda i: (0, i, 0)),
+        out_shape=shape((clips, fc, split * lanes)),
+    )(gs)
+
+
+def unpack(gs, parts, taps, group_count, width, wide):
+    fc, clips, d = gs.shape
+    ft = 128
+    fixed = lambda *dims: pl.BlockSpec(dims, lambda i, l: (0,) * len(dims), pipeline_mode=pl.Buffered(1))
     up_in, down_in, small = parts
     outs = [(taps, 2, width), (2, width), (2, group_count, width), (2, group_count, width), up_in.shape, (2, wide),
             down_in.shape, (2, width), (2, width)]
     return pl.pallas_call(
         unpack_kernel,
         name="unpack",
-        grid=(fc // ft,),
-        in_specs=[pl.BlockSpec((split, ft * clips, lanes), lambda i: (0, i, 0))] + [whole(*v.shape) for v in parts],
-        out_specs=[pl.BlockSpec((clips, ft, split * lanes), lambda i: (0, i, 0))] + [whole(*v) for v in outs],
-        out_shape=[shape((clips, fc, split * lanes))] + [shape(v) for v in outs],
-    )(gs, up_in, down_in, small)
+        grid=(fc // ft, d // LANES),
+        in_specs=[pl.BlockSpec((ft * clips, LANES), lambda i, l: (i, l))] + [fixed(*v.shape) for v in parts],
+        out_specs=[pl.BlockSpec((clips, ft, LANES), lambda i, l: (0, i, l))] + [fixed(*v) for v in outs],
+        out_shape=[shape((clips, fc, d))] + [shape(v) for v in outs],
+    )(gs.reshape(fc * clips, d), up_in, down_in, small)
 
 
 def body(deep, fan, frames, group, lengths, conv_w, conv_b, scale, shift, up_w, up_b, down_w, down_b, gain, out_grad):
@@ -1282,13 +1307,13 @@
         upb = whole_of(up_b, 1).astype(F32)[:, None]
         weights = (small, upb, ups, downs)
     if near:
-        out, gs, *parts, _, _ = whole_step(deep, side, lengths, group, frames, out_grad, weights, ft, taps, group_count)
-        gin, conv_grad, *grads = unpack(gs, parts, clips, taps, group_count, width, wide)
+        out, gs, *parts, _, _ = whole_step(deep, side, lengths, group, frames, out_grad, weights, 64, taps, group_count)
+        gin, conv_grad, *grads = unpack(gs, parts, taps, group_count, width, wide)
         return (out, gin, conv_grad.transpose(1, 0, 2), *grads)
     out, act, slope, *rest = forward(lengths, group, frames, weights, hidden, ft, taps, group_count)
     saved = (act, slope.reshape(act.shape), *rest)
     gs, *parts = backward(lengths, group, out_grad, saved, ups, downs, small, ft, taps, group_count)
-    gin = unpack(gs, None, clips, taps, group_count, width, wide)
+    gin = unpack_far(gs, clips)
     dup, ddown, lines, ug = parts
     owner = lambda v, axis: lax.psum_scatter(v, axes, scatter_dimension=axis, tiled=True)
     lines = owner(lines, 2)

time: 191 us -> 164 us (0.86)
  Pallas kernels: 189 us -> 162 us
    pallas_call x1, Pallas kernels: 181 us -> 154 us  [whole_step(): pl.pallas_call(functools.partial(step_kernel, deep=deep, side=side, ft=ft...]
where the time goes in v4:
time: 164 us
  Pallas kernels  162 us (99%)
    pallas_call x1, Pallas kernels, whole_step(): pl.pallas_call(functools.partial(step_kernel, deep=deep, side=side, ft=ft...  154 us
    pallas_call x1, Pallas kernels, unpack(): pl.pallas_call(unpack_kernel, name='unpack', grid=(fc // ft, d // LANES),...  7.34 us

profile of v4, /device:TPU:0, one launch (start us, length us, event | category | flops | bytes accessed | tf_op | source)
XLA Modules:
  0.0 163.8 jit_solution(3675081884996597918)
XLA Ops:
  0.6 154.5 %step.1 = (bf16[8,256,512]{2,1,0:T(8,128)(2,1)}, f32[256,8,512]{2,1,0:T(8,128)}, f32[2,16,1536]{2,1,0:T(8,128)}, f32[2,48,512]{2,1,0:T(8,128)}, f32[40,128]{1,0:...) custom-call(s32[8]{0:T(128)} %refs_0_.1, s32[8]{0:T(128)} %refs_1_.1, bf16[8,256,512]{2,1,0:T(8,128)(2,1)} %refs_2_.1, ...), custom_call_target="tpu_custom_call" | custom-call | tf_op jit(solution)/shard_map/step/pallas_call | solution.py:1199
  155.1 0.0 copy-start
  155.1 7.3 %unpack.1 = (f32[8,256,512]{2,1,0:T(8,128)}, f32[7,2,16]{2,1,0:T(2,128)}, f32[2,16]{1,0:T(2,128)}, f32[2,2,16]{2,1,0:T(2,128)}, f32[2,2,16]{2,1,0:T(2,128)}, /*i...) custom-call(f32[2048,512]{1,0:T(8,128)} %bitcast.3, ...), custom_call_target="tpu_custom_call" | custom-call | tf_op jit(solution)/shard_map/unpack/pallas_call | solution.py:1280
  162.5 0.0 copy-done
  162.5 1.3 copy.25
Async XLA Ops:
  155.1 7.4 %copy-start = (bf16[8,256,512]{2,1,0:T(8,128)(2,1)S(1)}, bf16[8,256,512]{2,1,0:T(8,128)(2,1)}, u32[]{:S(2)}) copy-start(bf16[8,256,512]{2,1,0:T(8,128)(2,1)} %get-tuple-element.52) | copy-start | bytes 6291460

commit v5 on v4

--- a/solution.py
+++ b/solution.py
@@ -61,31 +61,8 @@
     return jnp.where(t < len8[...][None], v, other)
 
 
-def spread_clips(block, t0, dst, d0, frames):
-    clips = block.shape[0]
-    for c in range(clips):
-        for t in range(0, frames, 16):
-            v = block[c, pl.ds(t0 + t, 16), :].astype(F32)
-            for l in range(dst.shape[0]):
-                dst[l, pl.ds((d0 + t) * clips + c, 16, stride=clips), :] = v[:, l * LANES : (l + 1) * LANES]
-
-
-def collect_clips(src, block, frames):
-    clips = block.shape[0]
-    for c in range(clips):
-        for t in range(0, frames, 16):
-            for l in range(src.shape[0]):
-                v = src[l, pl.ds(t * clips + c, 16, stride=clips), :]
-                block[c, t : t + 16, l * LANES : (l + 1) * LANES] = v.astype(block.dtype)
-
-
-def rows_of(src, start, n):
-    return jnp.concatenate([src[l, pl.ds(start, n), :] for l in range(src.shape[0])], axis=-1)
-
-
-def put_rows(dst, start, v):
-    for l in range(dst.shape[0]):
-        dst[l, pl.ds(start, v.shape[0]), :] = v[:, l * LANES : (l + 1) * LANES]
+def swap_frames(block, t0, frames):
+    return jnp.swapaxes(block[:, pl.ds(t0, frames), :].astype(F32), 0, 1)
 
 
 def fold(v):
@@ -323,9 +300,11 @@
         done(self.small[3])
         self.finish_small()
         ready()
-        conv(0, 3 * tiles // 4)
+        conv(0, tiles // 2)
         self.after_second(0)
         self.after_first(1)
+        conv(tiles // 2, 3 * tiles // 4)
+        self.after_z(2)
         conv(3 * tiles // 4, tiles)
         self.end(0)
 
@@ -345,26 +324,28 @@
     def late(self, i, tiles):
         @pl.when(i == tiles // 4)
         def _():
-            self.after_z(2)
             self.after_z(3)
+            self.after_second(1)
+
+        @pl.when(i == tiles // 2)
+        def _():
+            self.after_first(2)
 
         @pl.when(i == 3 * tiles // 4)
         def _():
-            self.after_second(1)
+            self.after_first(3)
 
         @pl.when(i == tiles)
         def _():
             self.end(1)
 
-        @pl.when(i == tiles + tiles // 4)
+        @pl.when(i == 2 * tiles - 1)
         def _():
-            self.after_first(2)
-            self.after_first(3)
+            self.after_second(2)
 
         @pl.when(i == 2 * tiles)
         def _():
-            for n in (2, 3):
-                self.after_second(n)
+            self.after_second(3)
             for n in (2, 3):
                 self.end(n)
 
@@ -407,7 +388,7 @@
 
 def forward_kernel(
     lens, groups, frames, small_full, upb_full, up_full, down_full, out, act_out, slope, normed_out, inv_out, shaped_out, masked_out,
-    stream, masked0, masked1, normed, inv, shaped, first_rows, act, s8, u8, len8, save_sem, act_sem, row_sem, *, ft, taps, group_count,
+    masked0, masked1, normed, inv, shaped, first_rows, act, s8, u8, len8, save_sem, act_sem, row_sem, *, ft, taps, group_count,
 ):
     i = pl.program_id(0)
     clips, frame_count, width = frames.shape
@@ -448,11 +429,10 @@
 
         def spread(n, carry):
             t0 = pl.multiple_of(n * 16, 16)
-            spread_clips(frames, t0, stream, 0, 16)
-            v = rows_of(stream, 0, 16 * clips)
+            v = swap_frames(frames, t0, 16)
             at = pl.multiple_of(t0 * clips, 16 * clips)
-            first_rows[pl.ds(at, 16 * clips), :] = v.astype(BF16)
-            masked0[pl.ds(HALO + t0, 16)] = keep_frames(v.reshape(16, clips, width), t0, len8)
+            first_rows[pl.ds(at, 16 * clips), :] = v.reshape(16 * clips, width).astype(BF16)
+            masked0[pl.ds(HALO + t0, 16)] = keep_frames(v, t0, len8)
             return carry
         lax.fori_loop(0, frame_count // 16, spread, 0)
         for b in range(2):
@@ -501,7 +481,7 @@
         up_gelu(shaped, up_cols(1), u8.at[1], act, r0, slope, 0, rows, hidden)
         tail(1, j).start()
         branch = mm(act[pl.ds(r0, rows), :], down_full[1], NN)
-        last_block(branch, masked1, f0, r0, ft, s8.at[1], len8, first_rows, stream, out)
+        last_block(branch, masked1, f0, r0, ft, s8.at[1], len8, first_rows, out)
 
     @pl.when(i == 3 * tiles - 1)
     def _():
@@ -512,15 +492,14 @@
                 c.wait()
 
 
-def last_block(branch, masked1, f0, r0, ft, s8, len8, first_rows, stream, out):
+def last_block(branch, masked1, f0, r0, ft, s8, len8, first_rows, out, step=16):
     clips, width = len8.shape
-    for t in range(0, ft, 4):
-        b = branch[t * clips : (t + 4) * clips].reshape(4, clips, width) + s8[DOWN_BIAS][None]
-        total = masked1[pl.ds(HALO + f0 + t, 4)] + s8[GAIN][None] * b
-        at = pl.multiple_of(r0 + t * clips, 4 * clips)
-        first = first_rows[pl.ds(at, 4 * clips), :].astype(F32).reshape(4, clips, width)
-        put_rows(stream, t * clips, keep_frames(total, f0 + t, len8, first).reshape(4 * clips, width))
-    collect_clips(stream, out, ft)
+    for t in range(0, ft, step):
+        b = branch[t * clips : (t + step) * clips].reshape(step, clips, width) + s8[DOWN_BIAS][None]
+        total = masked1[pl.ds(HALO + f0 + t, step)] + s8[GAIN][None] * b
+        at = pl.multiple_of(r0 + t * clips, step * clips)
+        first = first_rows[pl.ds(at, step * clips), :].astype(F32).reshape(step, clips, width)
+        out[:, t : t + step, :] = jnp.swapaxes(keep_frames(total, f0 + t, len8, first), 0, 1).astype(BF16)
 
 
 def forward(lens, groups, frames, weights, hidden, ft, taps, group_count):
@@ -543,7 +522,6 @@
             shape((2, fc, clips, LANES)), shape((2, R, d), BF16), shape((2, fc, clips, d)),
         ],
         scratch_shapes=[
-            pltpu.VMEM((d // LANES, max(r, 16 * clips), LANES), F32),
             pltpu.VMEM((fc + 2 * HALO, clips, d), F32), pltpu.VMEM((fc + 2 * HALO, clips, d), F32),
             pltpu.VMEM((fc, clips, d), F32), pltpu.VMEM((fc, clips, LANES), F32), pltpu.VMEM((R, d), BF16),
             pltpu.VMEM((R, d), BF16), pltpu.VMEM((R, h), BF16),
@@ -744,12 +722,12 @@
         parts, per = self.parts, self.parts + 1
         whats = ("core_start", "second_start", "first_start", "z_start", "finish")
         when = []
+        top = 2 * parts
         for p in range(parts - 1):
             t = 2 * (p + 1)
-            when.append((t, t + 1, t + 3, t + 5, 2 * parts + 6))
-        t = 2 * parts
-        when.append((t, t + 2, t + 5, t + 8, t + 12))
-        when.append((t, t + 3, t + 9, t + 12, t + 16))
+            when.append((t, t + 1, t + 3 if p < parts - 2 else top + 3, top + 3 if p < parts - 2 else top + 6, top + 9))
+        when.append((top, top + 3, top + 6, top + 9, top + 12))
+        when.append((top, top + 3, top + 10, top + 13, top + 16))
         plan = []
         for order, what in enumerate(whats):
             for n in range(2 * per):
@@ -772,10 +750,11 @@
             steps = sum_small(self.place, self.terms, self.z_in, self.bufs, self.small_part, self.small_s, self.small_r)
             last = 2 * (self.parts + 1) - 1
             next(steps)
+            self.do(last, "first_start")
+            next(steps)
+            self.do(last - 1, "finish")
             next(steps)
             self.do(last, "z_start")
-            self.do(last - 1, "finish")
-            next(steps)
             next(steps)
             self.do(last, "finish")
             for _ in steps:
@@ -825,7 +804,7 @@
             total = gs[pl.ds(g0 + j, step), :, cols] + total
             gs[pl.ds(g0 + j, step), :, cols] = total
             if out is not None:
-                out[l, j * clips : (j + step) * clips, :] = total.reshape(step * clips, LANES)
+                out[j : j + step, :, cols] = total
         for k in range(taps):
             acc[A_TAPS + k, :, cols] = sums[k]
 
@@ -850,7 +829,7 @@
 
 def backward_kernel(
     lens, groups, og, act, slope, normed, inv, shaped, masked, up, down, small, gs_out, dup, ddown, small_grad, upb_grad,
-    gs, gb, gbef, gm, lanes, s8, len8, acc, upb_acc, *, ft, tiles, parts, taps, group_count,
+    gs, gb, gbef, gm, s8, len8, acc, upb_acc, *, ft, tiles, parts, taps, group_count,
 ):
     i = pl.program_id(0)
     frame_count, clips, width = gs.shape
@@ -872,7 +851,7 @@
     def _():
         gm[pl.ds(0, base)] = jnp.zeros((base, clips, width), F32)
         gm[pl.ds(base + frame_count, HALO)] = jnp.zeros((HALO, clips, width), F32)
-        spread_grad(og, lanes, gs, 0)
+        spread_grad(og, gs, 0)
 
     @pl.when(step == 0)
     def _():
@@ -907,15 +886,12 @@
         finish_small(acc, upb_acc, groups, s8, small_grad.at[b], upb_grad.at[b], group_count)
 
 
-def spread_grad(og, lanes, gs, g0):
-    clips, frame_count, width = og.shape
-
+def spread_grad(og, gs, g0):
     def one(n, carry):
         t0 = pl.multiple_of(n * 16, 16)
-        spread_clips(og, t0, lanes, 0, 16)
-        gs[pl.ds(g0 + t0, 16)] = rows_of(lanes, 0, 16 * clips).reshape(16, clips, width)
+        gs[pl.ds(g0 + t0, 16)] = swap_frames(og, t0, 16)
         return carry
-    lax.fori_loop(0, frame_count // 16, one, 0)
+    lax.fori_loop(0, og.shape[1] // 16, one, 0)
 
 
 def branch_grad(gs, g0, s8, len8, gb):
@@ -973,11 +949,11 @@
             pl.BlockSpec((1, h, d), lambda i: (block(i), 0, 0)),
             whole(2, ROWS, d),
         ],
-        out_specs=[pl.BlockSpec((d // LANES, r, LANES), lambda i: (0, last(i), 0))] + [whole(*v) for v in sums],
-        out_shape=[shape((d // LANES, R, LANES))] + [shape(v) for v in sums],
+        out_specs=[pl.BlockSpec((ft, clips, d), lambda i: (last(i), 0, 0))] + [whole(*v) for v in sums],
+        out_shape=[shape((fc, clips, d))] + [shape(v) for v in sums],
         scratch_shapes=[
             pltpu.VMEM((fc, clips, d), F32), pltpu.VMEM((R, d), BF16), pltpu.VMEM((R, h), BF16),
-            pltpu.VMEM((fc + 2 * ft + HALO, clips, d), F32), pltpu.VMEM((d // LANES, 16 * clips, LANES), F32),
+            pltpu.VMEM((fc + 2 * ft + HALO, clips, d), F32),
             pltpu.VMEM((14, clips, d), F32), pltpu.VMEM((clips, d), jnp.int32),
             pltpu.VMEM((12, clips, d), F32), pltpu.VMEM((clips, h), F32),
         ],
@@ -989,10 +965,10 @@
     lens, groups, frames, og = refs[:4]
     shards = refs[4:13]
     out, gs_out, up_part, down_part, small_part, act_far, slope_far = refs[13:20]
-    (io, stream, masked0, masked1, normed, inv, shaped, first_rows, act, slope, gb, s8, u8, len8, acc, upb_acc) = refs[20:36]
-    small_full, upb_full, small_grad, upb_grad, up_full, down_full, up_term, down_term = refs[36:44]
-    io_sem, act_sem, slope_sem, act_back_sem, slope_back_sem, gs_sem = refs[44:50]
-    gather_refs, sum_refs = refs[50:68], refs[68:]
+    (io, masked0, masked1, normed, inv, shaped, first_rows, act, slope, gb, s8, u8, len8, acc, upb_acc) = refs[20:35]
+    small_full, upb_full, small_grad, upb_grad, up_full, down_full, up_term, down_term = refs[35:43]
+    io_sem, act_sem, slope_sem, act_back_sem, slope_back_sem, gs_sem = refs[43:49]
+    gather_refs, sum_refs = refs[49:67], refs[67:]
 
     i = pl.program_id(0)
     clips, frame_count, width = io.shape
@@ -1028,11 +1004,10 @@
 
         def one(n, carry):
             t0 = pl.multiple_of(n * 16, 16)
-            spread_clips(io, t0, stream, 0, 16)
-            v = rows_of(stream, 0, 16 * clips)
+            v = swap_frames(io, t0, 16)
             at = pl.multiple_of(t0 * clips, 16 * clips)
-            first_rows[pl.ds(at, 16 * clips), :] = v.astype(BF16)
-            masked0[pl.ds(HALO + t0, 16)] = keep_frames(v.reshape(16, clips, width), t0, len8)
+            first_rows[pl.ds(at, 16 * clips), :] = v.reshape(16 * clips, width).astype(BF16)
+            masked0[pl.ds(HALO + t0, 16)] = keep_frames(v, t0, len8)
             return carry
         lax.fori_loop(0, frame_count // 16, one, 0)
         load(1, og).start()
@@ -1087,7 +1062,7 @@
         conv_norm(masked1, f0, ft, s8.at[1], normed.at[1], inv.at[1], shaped, taps, HALO)
         up_gelu(shaped, up_cols(1), u8.at[1], act, r0, slope, r0, rows, hidden)
         branch = mm(act[pl.ds(r0, rows), :], down_full[1].reshape(hidden, width), NN)
-        last_block(branch, masked1, f0, r0, ft, s8.at[1], len8, first_rows, stream, out)
+        last_block(branch, masked1, f0, r0, ft, s8.at[1], len8, first_rows, out)
 
     k = i - 3 * tiles
     step = lax.rem(jnp.maximum(k, 0), span)
@@ -1096,7 +1071,7 @@
     @pl.when(k == 0)
     def _():
         load(1, og).wait()
-        spread_grad(io, stream, masked0, HALO)
+        spread_grad(io, masked0, HALO)
 
     @pl.when(k == span)
     def _():
@@ -1210,7 +1185,7 @@
             shape((2 * PACK, LANES)), shape((R, h), BF16), shape((R, h), BF16),
         ],
         scratch_shapes=[
-            rows(BF16, clips, fc), pltpu.VMEM((d // LANES, max(r, 16 * clips), LANES), F32),
+            rows(BF16, clips, fc),
             rows(F32, halo, clips), rows(F32, halo, clips), rows(F32, 2, halo, clips), pltpu.VMEM((2, fc, clips, LANES), F32),
             rows(BF16, R), rows(BF16, R), pltpu.VMEM((R, h), BF16), pltpu.VMEM((R, h), BF16), rows(BF16, R),
             rows(F32, 2, 14, clips), pltpu.VMEM((2, clips, h), F32), rows(jnp.int32, clips), rows(F32, 12, clips),
@@ -1223,13 +1198,15 @@
     )(lens, groups, frames, og, *weights)
 
 
+def swap_rows(src, dst):
+    for t in range(0, src.shape[0], 8):
+        dst[:, t : t + 8, :] = jnp.swapaxes(src[t : t + 8], 0, 1)
+
+
 def unpack_kernel(gs, up_in, down_in, small, gin, conv_w, conv_b, scale, shift, up_w, up_b, down_w, down_b, gain):
-    clips, frames, _ = gin.shape
-    for c in range(clips):
-        for t in range(0, frames, 16):
-            gin[c, t : t + 16, :] = gs[pl.ds(t * clips + c, 16, stride=clips), :]
-
-    @pl.when((pl.program_id(0) == 0) & (pl.program_id(1) == 0))
+    swap_rows(gs, gin)
+
+    @pl.when(pl.program_id(0) == 0)
     def _():
         unpack_parts(up_in, down_in, small, conv_w, conv_b, scale, shift, up_w, up_b, down_w, down_b, gain)
 
@@ -1256,35 +1233,33 @@
     down_w[...] = down_in[...]
 
 
-def unpack_far(gs, clips):
-    split, R, lanes = gs.shape
-    fc = R // clips
-    ft = 32
+def unpack_far(gs):
+    fc, clips, d = gs.shape
+    ft = 64
     return pl.pallas_call(
-        lambda src, dst: collect_clips(src, dst, ft),
+        swap_rows,
         name="unpack",
         grid=(fc // ft,),
-        in_specs=[pl.BlockSpec((split, ft * clips, lanes), lambda i: (0, i, 0))],
-        out_specs=pl.BlockSpec((clips, ft, split * lanes), lambda i: (0, i, 0)),
-        out_shape=shape((clips, fc, split * lanes)),
+        in_specs=[pl.BlockSpec((ft, clips, d), lambda i: (i, 0, 0))],
+        out_specs=pl.BlockSpec((clips, ft, d), lambda i: (0, i, 0)),
+        out_shape=shape((clips, fc, d)),
     )(gs)
 
 
 def unpack(gs, parts, taps, group_count, width, wide):
     fc, clips, d = gs.shape
-    ft = 128
-    fixed = lambda *dims: pl.BlockSpec(dims, lambda i, l: (0,) * len(dims), pipeline_mode=pl.Buffered(1))
+    ft = 64
     up_in, down_in, small = parts
     outs = [(taps, 2, width), (2, width), (2, group_count, width), (2, group_count, width), up_in.shape, (2, wide),
             down_in.shape, (2, width), (2, width)]
     return pl.pallas_call(
         unpack_kernel,
         name="unpack",
-        grid=(fc // ft, d // LANES),
-        in_specs=[pl.BlockSpec((ft * clips, LANES), lambda i, l: (i, l))] + [fixed(*v.shape) for v in parts],
-        out_specs=[pl.BlockSpec((clips, ft, LANES), lambda i, l: (0, i, l))] + [fixed(*v) for v in outs],
+        grid=(fc // ft,),
+        in_specs=[pl.BlockSpec((ft, clips, d), lambda i: (i, 0, 0))] + [whole(*v.shape) for v in parts],
+        out_specs=[pl.BlockSpec((clips, ft, d), lambda i: (0, i, 0))] + [whole(*v) for v in outs],
         out_shape=[shape((clips, fc, d))] + [shape(v) for v in outs],
-    )(gs.reshape(fc * clips, d), up_in, down_in, small)
+    )(gs, up_in, down_in, small)
 
 
 def body(deep, fan, frames, group, lengths, conv_w, conv_b, scale, shift, up_w, up_b, down_w, down_b, gain, out_grad):
@@ -1313,7 +1288,7 @@
     out, act, slope, *rest = forward(lengths, group, frames, weights, hidden, ft, taps, group_count)
     saved = (act, slope.reshape(act.shape), *rest)
     gs, *parts = backward(lengths, group, out_grad, saved, ups, downs, small, ft, taps, group_count)
-    gin = unpack_far(gs, clips)
+    gin = unpack_far(gs)
     dup, ddown, lines, ug = parts
     owner = lambda v, axis: lax.psum_scatter(v, axes, scatter_dimension=axis, tiled=True)
     lines = owner(lines, 2)

time: 164 us -> 154 us (0.939)
  Pallas kernels: 162 us -> 152 us
    pallas_call x1, Pallas kernels: 154 us -> 147 us  [whole_step(): pl.pallas_call(functools.partial(step_kernel, deep=deep, side=side, ft=ft...]
    pallas_call x1, Pallas kernels: 7.34 us -> 5.41 us  [unpack(): pl.pallas_call(unpack_kernel, name='unpack', grid=(fc // ft,), in_specs=[...]
where the time goes in v5:
time: 154 us
  Pallas kernels  152 us (99%)
    pallas_call x1, Pallas kernels, whole_step(): pl.pallas_call(functools.partial(step_kernel, deep=deep, side=side, ft=ft...  147 us
    pallas_call x1, Pallas kernels, unpack(): pl.pallas_call(unpack_kernel, name='unpack', grid=(fc // ft,), in_specs=[...  5.41 us

profile of v5, /device:TPU:0, one launch (start us, length us, event | category | flops | bytes accessed | tf_op | source)
XLA Modules:
  0.0 154.1 jit_solution(1328417341605652493)
XLA Ops:
  0.6 146.6 %step.1 = (bf16[8,256,512]{2,1,0:T(8,128)(2,1)}, f32[256,8,512]{2,1,0:T(8,128)}, f32[2,16,1536]{2,1,0:T(8,128)}, f32[2,48,512]{2,1,0:T(8,128)}, f32[40,128]{1,0:...) custom-call(s32[8]{0:T(128)} %refs_0_.1, s32[8]{0:T(128)} %refs_1_.1, bf16[8,256,512]{2,1,0:T(8,128)(2,1)} %refs_2_.1, ...), custom_call_target="tpu_custom_call" | custom-call | tf_op jit(solution)/shard_map/step/pallas_call | solution.py:1174
  147.3 0.0 copy-start
  147.3 5.4 %unpack.1 = (f32[8,256,512]{2,1,0:T(8,128)}, f32[7,2,16]{2,1,0:T(2,128)}, f32[2,16]{1,0:T(2,128)}, f32[2,2,16]{2,1,0:T(2,128)}, f32[2,2,16]{2,1,0:T(2,128)}, /*i...) custom-call(f32[256,8,512]{2,1,0:T(8,128)} %get-tuple-element.27.gs, ...), custom_call_target="tpu_custom_call" | custom-call | tf_op jit(solution)/shard_map/unpack/pallas_call | solution.py:1255
  152.7 0.0 copy-done
  152.7 1.3 copy.25
Async XLA Ops:
  147.3 5.4 %copy-start = (bf16[8,256,512]{2,1,0:T(8,128)(2,1)S(1)}, bf16[8,256,512]{2,1,0:T(8,128)(2,1)}, u32[]{:S(2)}) copy-start(bf16[8,256,512]{2,1,0:T(8,128)(2,1)} %get-tuple-element.52) | copy-start | bytes 6291460

commit v6 on v5

--- a/solution.py
+++ b/solution.py
@@ -90,7 +90,7 @@
 
 
 MESH = pl.DeviceIdType.MESH
-PACK = 20
+PACK = 24
 
 
 class Place:
@@ -270,46 +270,46 @@
 
     def early(self, spread, ready, conv, tiles):
         place = self.place
-        place.greet()
-        self.begin(0)
         conv_w, conv_b, scale, shift, _, up_b, _, down_b, gain = self.shards
         place_small(place, (conv_w, conv_b, scale, shift, up_b, down_b, gain), self.pack, self.group_count, self.taps)
-        self.zbuf[place.z] = self.pack[...]
+        self.zbuf[place.z] = self.pack[...].astype(BF16)
+        place.greet()
         run(self.small[0])
+        self.begin(0)
         self.begin(1)
         spread()
         done(self.small[0])
         run(self.small[1])
         self.after_z(0)
         done(self.small[1])
-        total = self.zbuf[...]
+        total = self.zbuf[...].astype(F32)
         for p in range(1, place.side):
-            total = total + self.first_in[p - 1]
-        self.first_sum[...] = total
+            total = total + self.first_in[p - 1].astype(F32)
+        self.first_sum[...] = total.astype(BF16)
         run(self.small[2])
         done(self.small[2])
-        total = self.first_sum[...]
+        total = self.first_sum[...].astype(F32)
         for p in range(1, place.side):
-            total = total + self.second_in[p - 1]
-        self.second_sum[...] = total
+            total = total + self.second_in[p - 1].astype(F32)
+        self.second_sum[...] = total.astype(BF16)
         run(self.small[3])
         self.after_first(0)
-        self.after_z(1)
         self.begin(2)
         self.begin(3)
         done(self.small[3])
         self.finish_small()
         ready()
-        conv(0, tiles // 2)
+        conv(0, tiles // 4)
+        self.after_z(1)
+        conv(tiles // 4, 3 * tiles // 4)
         self.after_second(0)
         self.after_first(1)
-        conv(tiles // 2, 3 * tiles // 4)
         self.after_z(2)
         conv(3 * tiles // 4, tiles)
         self.end(0)
 
     def finish_small(self):
-        total = self.second_sum[...] + self.core_in[...]
+        total = self.second_sum[...].astype(F32) + self.core_in[...].astype(F32)
         deep = self.place.deep
         per = self.upb_full.shape[2] // deep
         self.small_full[...] = jnp.zeros(self.small_full.shape, F32)
@@ -325,19 +325,19 @@
         @pl.when(i == tiles // 4)
         def _():
             self.after_z(3)
-            self.after_second(1)
-
-        @pl.when(i == tiles // 2)
-        def _():
-            self.after_first(2)
 
         @pl.when(i == 3 * tiles // 4)
         def _():
-            self.after_first(3)
+            self.after_second(1)
+            self.after_first(2)
 
         @pl.when(i == tiles)
         def _():
             self.end(1)
+
+        @pl.when(i == tiles + tiles // 4)
+        def _():
+            self.after_first(3)
 
         @pl.when(i == 2 * tiles - 1)
         def _():
@@ -351,8 +351,8 @@
 
 
 def gather_scratch(deep, side):
-    buf = pltpu.VMEM((deep, 2 * PACK, LANES), F32)
-    many = pltpu.VMEM((side - 1, deep, 2 * PACK, LANES), F32)
+    buf = pltpu.VMEM((deep, 2 * PACK, LANES), BF16)
+    many = pltpu.VMEM((side - 1, deep, 2 * PACK, LANES), BF16)
     n = deep - 1 + 2 * (side - 1) + 1
     return [pltpu.VMEM((2 * PACK, LANES), F32), buf, many, buf, many, buf, buf, DMA((4,)), DMA((n,)), DMA((n,))] + gather_sems(
         4, deep, side

time: 154 us -> 151 us (0.981)
  Pallas kernels: 152 us -> 149 us
    pallas_call x1, Pallas kernels: 147 us -> 143 us  [whole_step(): pl.pallas_call(functools.partial(step_kernel, deep=deep, side=side, ft=ft...]
where the time goes in v6:
time: 151 us
  Pallas kernels  149 us (99%)
    pallas_call x1, Pallas kernels, whole_step(): pl.pallas_call(functools.partial(step_kernel, deep=deep, side=side, ft=ft...  143 us
    pallas_call x1, Pallas kernels, unpack(): pl.pallas_call(unpack_kernel, name='unpack', grid=(fc // ft,), in_specs=[...  5.42 us

profile of v6, /device:TPU:0, one launch (start us, length us, event | category | flops | bytes accessed | tf_op | source)
XLA Modules:
  0.0 150.7 jit_solution(13880378251814446775)
XLA Ops:
  0.6 143.3 %step.1 = (bf16[8,256,512]{2,1,0:T(8,128)(2,1)}, f32[256,8,512]{2,1,0:T(8,128)}, f32[2,16,1536]{2,1,0:T(8,128)}, f32[2,48,512]{2,1,0:T(8,128)}, f32[48,128]{1,0:...) custom-call(s32[8]{0:T(128)} %refs_0_.1, s32[8]{0:T(128)} %refs_1_.1, bf16[8,256,512]{2,1,0:T(8,128)(2,1)} %refs_2_.1, ...), custom_call_target="tpu_custom_call" | custom-call | tf_op jit(solution)/shard_map/step/pallas_call | solution.py:1174
  143.9 0.0 copy-start
  143.9 5.4 %unpack.1 = (f32[8,256,512]{2,1,0:T(8,128)}, f32[7,2,16]{2,1,0:T(2,128)}, f32[2,16]{1,0:T(2,128)}, f32[2,2,16]{2,1,0:T(2,128)}, f32[2,2,16]{2,1,0:T(2,128)}, /*i...) custom-call(f32[256,8,512]{2,1,0:T(8,128)} %get-tuple-element.27.gs, ...), custom_call_target="tpu_custom_call" | custom-call | tf_op jit(solution)/shard_map/unpack/pallas_call | solution.py:1255
  149.3 0.0 copy-done
  149.3 1.3 copy.25
Async XLA Ops:
  143.9 5.4 %copy-start = (bf16[8,256,512]{2,1,0:T(8,128)(2,1)S(1)}, bf16[8,256,512]{2,1,0:T(8,128)(2,1)}, u32[]{:S(2)}) copy-start(bf16[8,256,512]{2,1,0:T(8,128)(2,1)} %get-tuple-element.52) | copy-start | bytes 6291460

commit v7 on v6

--- a/solution.py
+++ b/solution.py
@@ -124,14 +124,17 @@
     def second_peer(self, p):
         return {"fsdp": self.fsdp_of(self.first, lax.rem(self.second + p, self.side))}
 
+    def plane_peers(self):
+        ends = [(p, q) for p in range(self.side) for q in range(self.side) if p or q]
+        return [{"fsdp": self.fsdp_of(lax.rem(self.first + p, self.side), lax.rem(self.second + q, self.side))} for p, q in ends]
+
     def core_peer(self):
         return {"fsdp": self.f + 1 - 2 * self.core}
 
     def greet(self):
         barrier = pltpu.get_barrier_semaphore()
         peers = [self.z_peer(p) for p in range(1, self.deep)]
-        peers += [self.first_peer(p) for p in range(1, self.side)]
-        peers += [self.second_peer(p) for p in range(1, self.side)]
+        peers += self.plane_peers()
         peers.append(self.core_peer())
         for peer in peers:
             pl.semaphore_signal(barrier, inc=1, device_id=peer, device_id_type=MESH)
@@ -667,8 +670,7 @@
     total = terms[place.z]
     for p in range(1, place.deep):
         total = total + z_in[p - 1]
-    stages = [[place.core_peer()], [place.second_peer(p) for p in range(1, place.side)],
-              [place.first_peer(p) for p in range(1, place.side)]]
+    stages = [[place.core_peer()], place.plane_peers()]
     for (here, into), peers in zip(bufs, stages):
         here[...] = total
         copies = []
@@ -685,17 +687,18 @@
 
 def small_bufs(deep, side):
     many = lambda *n: pltpu.VMEM(n + (2 * PACK, LANES), F32)
-    n = deep - 1 + 2 * (side - 1) + 1
-    return [many(deep), many(deep - 1), many(), many(1), many(), many(side - 1), many(), many(side - 1), DMA((n,)), DMA((n,))]
+    others = side * side - 1
+    n = deep + others
+    return [many(deep), many(deep - 1), many(), many(1), many(), many(others), DMA((n,)), DMA((n,))]
 
 
 class Sums:
     def __init__(self, refs, up_term, down_term, up_part, down_part, small_part, small_grad, upb_grad, deep, side, parts):
         self.place = Place(deep, side)
         self.terms, self.z_in = refs[:2]
-        self.bufs = [refs[2:4], refs[4:6], refs[6:8]]
-        self.small_s, self.small_r = refs[8:10]
-        refs = refs[10:]
+        self.bufs = [refs[2:4], refs[4:6]]
+        self.small_s, self.small_r = refs[6:8]
+        refs = refs[8:]
         sems = refs[-8:]
         self.small_part, self.small_grad, self.upb_grad = small_part, small_grad, upb_grad
         self.parts = parts
@@ -755,7 +758,6 @@
             self.do(last - 1, "finish")
             next(steps)
             self.do(last, "z_start")
-            next(steps)
             self.do(last, "finish")
             for _ in steps:
                 pass

time: 151 us -> 151 us (level)
  no operation moved by 1% of the time
where the time goes in v7:
time: 151 us
  Pallas kernels  149 us (99%)
    pallas_call x1, Pallas kernels, whole_step(): pl.pallas_call(functools.partial(step_kernel, deep=deep, side=side, ft=ft...  143 us
    pallas_call x1, Pallas kernels, unpack(): pl.pallas_call(unpack_kernel, name='unpack', grid=(fc // ft,), in_specs=[...  5.42 us

profile of v7, /device:TPU:0, one launch (start us, length us, event | category | flops | bytes accessed | tf_op | source)
XLA Modules:
  0.0 150.8 jit_solution(10890841175938523109)
XLA Ops:
  0.6 143.4 %step.1 = (bf16[8,256,512]{2,1,0:T(8,128)(2,1)}, f32[256,8,512]{2,1,0:T(8,128)}, f32[2,16,1536]{2,1,0:T(8,128)}, f32[2,48,512]{2,1,0:T(8,128)}, f32[48,128]{1,0:...) custom-call(s32[8]{0:T(128)} %refs_0_.1, s32[8]{0:T(128)} %refs_1_.1, bf16[8,256,512]{2,1,0:T(8,128)(2,1)} %refs_2_.1, ...), custom_call_target="tpu_custom_call" | custom-call | tf_op jit(solution)/shard_map/step/pallas_call | solution.py:1176
  144.1 0.0 copy-start
  144.1 5.4 %unpack.1 = (f32[8,256,512]{2,1,0:T(8,128)}, f32[7,2,16]{2,1,0:T(2,128)}, f32[2,16]{1,0:T(2,128)}, f32[2,2,16]{2,1,0:T(2,128)}, f32[2,2,16]{2,1,0:T(2,128)}, /*i...) custom-call(f32[256,8,512]{2,1,0:T(8,128)} %get-tuple-element.27.gs, ...), custom_call_target="tpu_custom_call" | custom-call | tf_op jit(solution)/shard_map/unpack/pallas_call | solution.py:1257
  149.5 0.0 copy-done
  149.5 1.3 copy.25
Async XLA Ops:
  144.1 5.4 %copy-start = (bf16[8,256,512]{2,1,0:T(8,128)(2,1)S(1)}, bf16[8,256,512]{2,1,0:T(8,128)(2,1)}, u32[]{:S(2)}) copy-start(bf16[8,256,512]{2,1,0:T(8,128)(2,1)} %get-tuple-element.52) | copy-start | bytes 6291460
